TPU v7x, 32 devices: a whole 2x2x4 slice. The times are simulated.
32 devices in a mesh: groups: 2 (over y), rows: 4 (over z), cols: 4 (over x, core).
Axes of the slice: x: 2, y: 2, z: 4, core: 2. Of those that a mesh axis runs over, the one named last changes fastest.
Arguments:
- query_grid: bfloat16 [128, 96, 768], P(('groups', 'rows'), 'cols'), parts along dimension 0, may hold values from -9 to 9
- key_grid: bfloat16 [128, 96, 768], P(('groups', 'rows'), 'cols'), parts along dimension 0, may hold values from -9 to 9
- value_grid: bfloat16 [128, 96, 768], P(('groups', 'rows'), 'cols'), parts along dimension 0, may hold values from -6 to 6
- out_grad: bfloat16 [128, 96, 768], P(('groups', 'rows'), 'cols'), parts along dimension 0, may hold values from -6 to 6
- tissue: int32 [16, 12], P(('groups', 'rows'), 'cols'), parts along dimension 0, may hold values from 0 to 1, as said below
Outputs:
- attended: bfloat16 [128, 96, 768], P(('groups', 'rows'), 'cols'), parts along dimension 0
- grad_query: bfloat16 [128, 96, 768], P(('groups', 'rows'), 'cols'), parts along dimension 0
- grad_key: bfloat16 [128, 96, 768], P(('groups', 'rows'), 'cols'), parts along dimension 0
- grad_value: bfloat16 [128, 96, 768], P(('groups', 'rows'), 'cols'), parts along dimension 0
There are 2 independent parts, one for each index of `groups`. A program takes and returns all parts, laid end to end along the dimension named above; each array names one. Nothing has to cross between parts.
Inputs may be any that keep to these rules, and one draw needn't show every extreme that they name: 1 marks a tile of tissue.
All inputs are finite; a program needn't handle non-finite values.
Results may differ from a plain program's by a relative error of at most 0.019.
Values may be sent and summed in bfloat16 or wider, within the bound.
No kernel may reach another device: no remote copies, remote signals or barrier semaphores. Data moves between devices by JAX's collectives and lax.ppermute only.
A program may use at most 128 MiB of HBM per device.

v0:
```python
import jax
import jax.numpy as jnp
from jax import lax
from jax.sharding import PartitionSpec as P

D = 768
HEADS = 12
HEAD = 64
TILE = 8


NEG = -1e30


def with_halo(shard, sides, width):
    for axis, dim in sides:
        count, length = (lax.axis_size(axis), shard.shape[dim])
        up = [(i, (i + 1) % count) for i in range(count - 1)]
        down = [(j, i) for i, j in up]
        last = lax.slice_in_dim(shard, length - width, length, axis=dim)
        leading = lax.slice_in_dim(shard, 0, width, axis=dim)
        before = lax.ppermute(last, axis, up)
        after = lax.ppermute(leading, axis, down)
        shard = jnp.concatenate([before, shard, after], axis=dim)
    return shard


def from_behind(shard, axis, by):
    count = lax.axis_size(axis)
    pairs = [(i, i + by) for i in range(count) if 0 <= i + by < count]
    return lax.ppermute(shard, axis, pairs)


def trailing(first, array):
    return tuple(range(first, array.ndim))


def row_tiles(stripe, number):
    inner_shape = stripe.shape[2:]
    shaped = stripe.reshape((TILE, number, TILE) + inner_shape)
    return shaped.transpose((1, 0, 2) + trailing(3, shaped)).reshape(
        (number, TILE * TILE) + inner_shape
    )


def tiles_rows(tiles, number):
    inner_shape = tiles.shape[2:]
    shaped = tiles.reshape((number, TILE, TILE) + inner_shape)
    return shaped.transpose((1, 0, 2) + trailing(3, shaped)).reshape(
        (TILE, number * TILE) + inner_shape
    )


def neighbour_tiles(stripe, number):
    inner_shape = stripe.shape[2:]
    shaped = stripe.reshape((3, TILE, number + 2, TILE) + inner_shape)
    pieces = jnp.stack([shaped[:, :, column : column + number] for column in range(3)], axis=0)
    reordered = pieces.transpose((3, 1, 0, 2, 4) + trailing(5, pieces))
    return reordered.reshape((number, 9 * TILE * TILE) + inner_shape)


def stripe_sum(key_parts, number):
    inner_shape = key_parts.shape[2:]
    shaped = key_parts.reshape((number, 3, 3, TILE, TILE) + inner_shape)
    total_sum = 0.0
    for column in range(3):
        column_piece = shaped[:, :, column]
        reordered = column_piece.transpose((1, 2, 0, 3) + trailing(4, column_piece))
        widths = [(0, 0), (0, 0), (column, 2 - column)] + [(0, 0)] * (reordered.ndim - 3)
        total_sum = total_sum + jnp.pad(reordered, widths)
    return total_sum.reshape((3 * TILE, (number + 2) * TILE) + inner_shape)


def neighbour_marks(stripe, number):
    pieces = jnp.stack([stripe[:, column : column + number] for column in range(3)], axis=0)
    reordered = pieces.transpose(2, 1, 0).reshape(number, 9, 1)
    return jnp.broadcast_to(reordered, (number, 9, TILE * TILE)).reshape(number, 9 * TILE * TILE)


def pair_allowed(own_marks, near_marks):
    own_tile = jnp.arange(9 * TILE * TILE, dtype=jnp.int32) // (TILE * TILE) == 4
    return jnp.logical_or(own_marks[:, None] * near_marks > 0, own_tile[None, :])


def split_heads(tiles):
    return tiles.reshape(tiles.shape[:2] + (HEADS, HEAD))


def query_pass(query_tiles, grad_tiles, key_tiles, value_tiles, query_marks, key_marks):
    score_scale = HEAD ** (-0.5)
    number = query_tiles.shape[0]
    query_heads = split_heads(query_tiles)
    key_heads = split_heads(key_tiles)
    value_heads = split_heads(value_tiles)
    grad_heads = split_heads(grad_tiles)
    allowed = pair_allowed(query_marks, key_marks)[:, None, None, :]
    scores = (
        jnp.einsum("tqhd,tkhd->thqk", query_heads, key_heads, preferred_element_type=jnp.float32)
        * score_scale
    )
    masked = jnp.where(allowed, scores, NEG)
    row_max = jnp.max(masked, axis=-1, keepdims=True)
    row_sum = jnp.sum(jnp.where(allowed, jnp.exp(masked - row_max), 0.0), axis=-1, keepdims=True)
    log_total = row_max + jnp.log(row_sum)
    attn_probs = jnp.where(allowed, jnp.exp(masked - log_total), 0.0)
    probs_low = attn_probs.astype(jnp.bfloat16)
    query_mark = query_marks.astype(jnp.float32)[:, None, None, None]
    attended = (
        jnp.einsum("thqk,tkhd->tqhd", probs_low, value_heads, preferred_element_type=jnp.float32)
        * query_mark
    )
    attended_low = attended.astype(jnp.bfloat16)
    row_dot = jnp.sum(grad_heads.astype(jnp.float32) * attended_low.astype(jnp.float32), axis=-1)
    row_dot = row_dot.transpose(0, 2, 1)[..., None]
    grad_probs = jnp.einsum(
        "tqhd,tkhd->thqk", grad_heads, value_heads, preferred_element_type=jnp.float32
    )
    grad_scores = (attn_probs * (grad_probs - row_dot) * score_scale).astype(jnp.bfloat16)
    grad_query = jnp.einsum(
        "thqk,tkhd->tqhd", grad_scores, key_heads, preferred_element_type=jnp.float32
    )
    return (
        attended_low.reshape(number, TILE * TILE, D),
        grad_query.astype(jnp.bfloat16).reshape(number, TILE * TILE, D),
        log_total[..., 0],
        row_dot[..., 0],
        probs_low,
        grad_scores,
    )


def local(query_grid, key_grid, value_grid, out_grad, tissue):
    tile_rows, tile_cols = tissue.shape
    token_rows = tile_rows * TILE
    token_cols = tile_cols * TILE
    expand = jnp.broadcast_to(tissue[:, None, :, None], (tile_rows, TILE, tile_cols, TILE)).reshape(
        token_rows, token_cols
    )
    masked_grad = out_grad * expand.astype(jnp.bfloat16)[..., None]
    key_value = jnp.stack((key_grid, value_grid), axis=2)
    pairs_near = with_halo(key_value, (("rows", 0), ("cols", 1)), TILE)
    marks_near = with_halo(tissue, (("rows", 0), ("cols", 1)), 1)
    row_list = jnp.arange(tile_rows, dtype=jnp.int32)

    def first_rows(row_index):
        first_row = row_index * TILE
        near_pairs = neighbour_tiles(
            lax.dynamic_slice_in_dim(pairs_near, first_row, 3 * TILE, 0), tile_cols
        )
        key_marks = neighbour_marks(
            lax.dynamic_slice_in_dim(marks_near, row_index, 3, 0), tile_cols
        )
        query_marks = lax.dynamic_slice_in_dim(tissue, row_index, 1, 0)[0]
        query_tiles = row_tiles(lax.dynamic_slice_in_dim(query_grid, first_row, TILE, 0), tile_cols)
        grad_tiles = row_tiles(lax.dynamic_slice_in_dim(masked_grad, first_row, TILE, 0), tile_cols)
        results = query_pass(
            query_tiles,
            grad_tiles,
            near_pairs[:, :, 0],
            near_pairs[:, :, 1],
            query_marks,
            key_marks,
        )
        return (query_tiles, grad_tiles, results)

    def step_sums(running, row_index):
        query_tiles, grad_tiles, results = first_rows(row_index)
        attended, grad_query, log_total, row_dot, probs_low, grad_scores = results
        key_part = jnp.einsum(
            "thqk,tqhd->tkhd",
            grad_scores,
            split_heads(query_tiles),
            preferred_element_type=jnp.float32,
        )
        value_part = jnp.einsum(
            "thqk,tqhd->tkhd",
            probs_low,
            split_heads(grad_tiles),
            preferred_element_type=jnp.float32,
        )
        key_parts = jnp.stack((key_part, value_part), axis=2).reshape(
            tile_cols, 9 * TILE * TILE, 2, D
        )
        stripe = stripe_sum(key_parts, tile_cols)
        first_row = row_index * TILE
        current = lax.dynamic_slice_in_dim(running, first_row, 3 * TILE, 0)
        running = lax.dynamic_update_slice_in_dim(running, current + stripe, first_row, 0)
        return (running, (tiles_rows(attended, tile_cols), tiles_rows(grad_query, tile_cols)))

    start_sums = jnp.zeros((token_rows + 2 * TILE, token_cols + 2 * TILE, 2, D), jnp.float32)
    summed, (attended_rows, query_rows) = lax.scan(step_sums, start_sums, row_list)
    inner_part = summed[:, TILE:-TILE]
    received = [
        from_behind(border, "cols", offset)
        for offset, border in ((-1, summed[:, :TILE]), (1, summed[:, -TILE:]))
    ]
    spare_cols = token_cols - TILE
    inner_part = (
        inner_part
        + jnp.pad(received[0], ((0, 0), (spare_cols, 0), (0, 0), (0, 0)))
        + jnp.pad(received[1], ((0, 0), (0, spare_cols), (0, 0), (0, 0)))
    )
    centre_part = inner_part[TILE:-TILE]
    arrived = [
        from_behind(border, "rows", offset)
        for offset, border in ((-1, inner_part[:TILE]), (1, inner_part[-TILE:]))
    ]
    spare_rows = token_rows - TILE
    centre_part = (
        centre_part
        + jnp.pad(arrived[0], ((spare_rows, 0), (0, 0), (0, 0), (0, 0)))
        + jnp.pad(arrived[1], ((0, spare_rows), (0, 0), (0, 0), (0, 0)))
    )
    grad_key = centre_part[:, :, 0].astype(jnp.bfloat16)
    grad_value = centre_part[:, :, 1].astype(jnp.bfloat16)
    attended = attended_rows.reshape(token_rows, token_cols, D)
    grad_query = query_rows.reshape(token_rows, token_cols, D)
    return (attended, grad_query, grad_key, grad_value)


def solution(mesh):
    placed = (
        P(("groups", "rows"), "cols", None),
        P(("groups", "rows"), "cols", None),
        P(("groups", "rows"), "cols", None),
        P(("groups", "rows"), "cols", None),
        P(("groups", "rows"), "cols"),
    )
    return jax.shard_map(
        local,
        mesh=mesh,
        in_specs=placed,
        out_specs=(
            P(("groups", "rows"), "cols", None),
            P(("groups", "rows"), "cols", None),
            P(("groups", "rows"), "cols", None),
            P(("groups", "rows"), "cols", None),
        ),
        check_vma=False,
    )
```

profile of v0, /device:TPU:1, one launch (start us, length us, event | category | flops | bytes accessed | tf_op | source)
XLA Modules:
  0.0 371.7 jit_solution(1557232416152591522)
XLA Ops:
  2.1 4.1 %collective-permute-start.4 = (bf16[8,24,2,768]{3,1,0,2:T(8,128)(2,1)S(1)}, bf16[8,24,2,768]{3,1,0,2:T(8,128)(2,1)S(1)}, u32[]{:S(2)}, u32[]{:S(2)}) collective-permute-start(bf16[8,24,2,768]{3,1,0,2:T(8,128)(2,1)S(1)} %get-tuple-element.203), channel_id=1, source_target_pairs={{0,4},{4,8},{8,12},{1,5},{5,9},{9,13},{2,6},{6,10},{10,14},{3,7},{... | collective-permute-start | bytes 1769480 | tf_op jit(solution)/shard_map/ppermute | solution.py:22
  7.5 10.6 %collective-permute-done.4 = bf16[8,24,2,768]{3,1,0,2:T(8,128)(2,1)S(1)} collective-permute-done((bf16[8,24,2,768]{3,1,0,2:T(8,128)(2,1)S(1)}, bf16[8,24,2,768]{3,1,0,2:T(8,128)(2,1)S(1)}, u32[]{:S(2)}, u32[]{:S(2)}) %collective-permute-start.4) | collective-permute-done | bytes 589856 | tf_op jit(solution)/shard_map/ppermute | solution.py:22
  18.2 3.8 %collective-permute-done.5 = bf16[8,24,2,768]{3,1,0,2:T(8,128)(2,1)S(1)} collective-permute-done((bf16[8,24,2,768]{3,1,0,2:T(8,128)(2,1)S(1)}, bf16[8,24,2,768]{3,1,0,2:T(8,128)(2,1)S(1)}, u32[]{:S(2)}, u32[]{:S(2)}) %collective-permute-start.5) | collective-permute-done | bytes 589856 | tf_op jit(solution)/shard_map/ppermute | solution.py:23
  24.5 4.9 %collective-permute-start.6 = (bf16[32,8,2,768]{3,1,0,2:T(8,128)(2,1)}, bf16[32,8,2,768]{3,1,0,2:T(8,128)(2,1)}, u32[]{:S(2)}, u32[]{:S(2)}) collective-permute-start(bf16[32,8,2,768]{3,1,0,2:T(8,128)(2,1)} %get-tuple-element.199), channel_id=1, source_target_pairs={{0,1},{1,2},{2,3},{4,5},{5,6},{6,7},{8,9},{9,10},{10,11},{12,13},{... | collective-permute-start | bytes 2359304 | tf_op jit(solution)/shard_map/ppermute | solution.py:22
  31.8 3.7 %collective-permute-start = (s32[1,3]{1,0:T(1,128)}, s32[1,3]{1,0:T(1,128)}, u32[]{:S(2)}, u32[]{:S(2)}) collective-permute-start(s32[1,3]{1,0:T(1,128)} %get-tuple-element.207), channel_id=1, source_target_pairs={{0,4},{4,8},{8,12},{1,5},{5,9},{9,13},{2,6},{6,10},{10,14},{3,7},{... | collective-permute-start | bytes 44 | tf_op jit(solution)/shard_map/ppermute | solution.py:22
  37.3 2.7 collective-permute-done.1
  40.8 4.9 %collective-permute-start.2 = (s32[4,1]{1,0:T(4,128)S(1)}, s32[4,1]{1,0:T(4,128)S(1)}, u32[]{:S(2)}, u32[]{:S(2)}) collective-permute-start(s32[4,1]{1,0:T(4,128)S(1)} %get-tuple-element.205), channel_id=1, source_target_pairs={{0,1},{1,2},{2,3},{4,5},{5,6},{6,7},{8,9},{9,10},{10,11},{12,13},{... | collective-permute-start | bytes 56 | tf_op jit(solution)/shard_map/ppermute | solution.py:22
  47.7 3.0 collective-permute-done.3
  51.4 3.3 pad_maximum_fusion
  54.7 3.6 broadcast_in_dim.74.clone
  58.3 265.2 %while.16 = (s32[]{:T(128)}, f32[32,40,2,768]{3,1,0,2:T(8,128)}, bf16[2,8,24,768]{3,2,1,0:T(8,128)(2,1)}, bf16[2,8,24,768]{3,2,1,0:T(8,128)(2,1)}, s32[2]{0:T(12...) while((s32[]{:T(128)}, f32[32,40,2,768]{3,1,0,2:T(8,128)}, ...), condition=%wide.region_4.5_spmd, body=%wide.region_0.4_spmd.sunk | while | flops 1064490688 | bytes 299773920 | solution.py:191
  74.0 4.0 %copy.109 = bf16[3,576,1,768]{1,3,0,2:T(8,128)(2,1)S(1)} copy(bf16[3,576,1,768]{3,1,2,0:T(8,128)(2,1)} %get-tuple-element.296) | data formatting | bytes 5308416 | tf_op jit(solution)/shard_map/while/body/eval_jaxpr/slice | solution.py:159
  78.0 5.4 %copy.112 = bf16[3,576,1,768]{1,3,0,2:T(8,128)(2,1)} copy(bf16[3,576,1,768]{3,1,2,0:T(8,128)(2,1)} %get-tuple-element.299) | data formatting | bytes 5308416 | tf_op jit(solution)/shard_map/while/body/eval_jaxpr/slice | solution.py:160
  86.6 2.8 multiply_reduce_fusion.2
  89.4 2.6 multiply_convert_fusion.2
  94.0 3.3 convolution_bitcast_fusion.5
  97.3 2.7 copy.117
  109.1 3.5 convolution_bitcast_fusion.4
  112.6 14.0 %copy.113 = f32[3,576,12,64]{3,2,1,0:T(8,128)} copy(f32[3,576,12,64]{1,3,2,0:T(8,128)} %convolution_bitcast_fusion.4) | data formatting | bytes 10616832 | tf_op jit(solution)/shard_map/while/body/eval_jaxpr/thqk,tqhd->tkhd/transpose | solution.py:169
  126.6 11.7 %stack.71 = f32[3,3,3,8,8,1,768]{6,4,3,2,1,0,5:T(8,128)} reshape(f32[3,576,12,64]{3,2,1,0:T(8,128)} %copy.113) | data formatting | bytes 10616832 | tf_op jit(solution)/shard_map/while/body/eval_jaxpr/stack | solution.py:181
  138.3 5.4 %constant_dynamic-update-slice_fusion.4 = f32[3,3,3,8,8,2,768]{6,4,3,2,1,0,5:T(8,128)} fusion(f32[3,3,3,8,8,1,768]{6,4,3,2,1,0,5:T(8,128)} %stack.71), kind=kLoop, calls=%fused_computation.36.clone.1 | loop fusion | bytes 10616832 | tf_op jit(solution)/shard_map/while
  143.7 13.9 %copy.114 = f32[3,576,12,64]{3,2,1,0:T(8,128)} copy(f32[3,576,12,64]{1,3,2,0:T(8,128)} %convolution_bitcast_fusion.5) | data formatting | bytes 10616832 | tf_op jit(solution)/shard_map/while/body/eval_jaxpr/thqk,tqhd->tkhd/transpose | solution.py:175
  157.6 11.7 %stack.72 = f32[3,3,3,8,8,1,768]{6,4,3,2,1,0,5:T(8,128)} reshape(f32[3,576,12,64]{3,2,1,0:T(8,128)} %copy.114) | data formatting | bytes 10616832 | tf_op jit(solution)/shard_map/while/body/eval_jaxpr/stack | solution.py:181
  169.3 5.4 %constant_dynamic-update-slice_fusion.5 = f32[3,3,3,8,8,2,768]{6,4,3,2,1,0,5:T(8,128)} fusion(f32[3,3,3,8,8,2,768]{6,4,3,2,1,0,5:T(8,128)} %constant_dynamic-update-slice_fusion.4, f32[3,3,3,8,8,1,768]{6,4,3,2,1,0,5:T(8,128)} %stack.72), kind=kLoop, calls=%fused_computation.35.clone.1 | loop fusion | bytes 10616832 | tf_op jit(solution)/shard_map/while/body/eval_jaxpr/stack | solution.py:181
  174.6 6.6 %slice_bitcast_fusion.16 = (f32[3,8,3,8,2,768]{5,3,1,0,2,4:T(8,128)S(1)}, f32[3,8,3,8,2,768]{5,3,1,0,2,4:T(8,128)S(1)}, f32[3,8,3,8,2,768]{5,3,1,0,2,4:T(8,128)}) fusion(f32[3,3,3,8,8,2,768]{6,4,3,2,1,0,5:T(8,128)} %constant_dynamic-update-slice_fusion.5), kind=kLoop, calls=%fused_computation.12.clone.1 | loop fusion | bytes 21233664 | tf_op jit(solution)/shard_map/while/body/eval_jaxpr/transpose | solution.py:68
  181.3 2.8 pad_add_fusion.5
  184.9 6.0 %copy_dynamic-update-slice_fusion.2 = f32[32,40,2,768]{3,1,0,2:T(8,128)} fusion(f32[32,40,2,768]{3,1,0,2:T(8,128)} %get-tuple-element.326, s32[]{:T(128)S(6)} %select_n.108, f32[24,40,2,768]{3,1,2,0:T(8,128)S(1)} %bitcast.154), kind=kLoop, calls=%fused_computation.clone.1 | loop fusion | flops 1474560 | bytes 17695744 | tf_op jit(solution)/shard_map/while/body/eval_jaxpr/dynamic_update_slice | solution.py:187
  206.6 4.0 %copy.109 = bf16[3,576,1,768]{1,3,0,2:T(8,128)(2,1)S(1)} copy(bf16[3,576,1,768]{3,1,2,0:T(8,128)(2,1)} %get-tuple-element.296) | data formatting | bytes 5308416 | tf_op jit(solution)/shard_map/while/body/eval_jaxpr/slice | solution.py:159
  210.7 5.4 %copy.112 = bf16[3,576,1,768]{1,3,0,2:T(8,128)(2,1)} copy(bf16[3,576,1,768]{3,1,2,0:T(8,128)(2,1)} %get-tuple-element.299) | data formatting | bytes 5308416 | tf_op jit(solution)/shard_map/while/body/eval_jaxpr/slice | solution.py:160
  219.3 2.8 multiply_reduce_fusion.2
  222.0 2.6 multiply_convert_fusion.2
  226.6 3.3 convolution_bitcast_fusion.5
  229.9 2.7 copy.117
  241.7 3.5 convolution_bitcast_fusion.4
  245.2 14.0 %copy.113 = f32[3,576,12,64]{3,2,1,0:T(8,128)} copy(f32[3,576,12,64]{1,3,2,0:T(8,128)} %convolution_bitcast_fusion.4) | data formatting | bytes 10616832 | tf_op jit(solution)/shard_map/while/body/eval_jaxpr/thqk,tqhd->tkhd/transpose | solution.py:169
  259.2 11.7 %stack.71 = f32[3,3,3,8,8,1,768]{6,4,3,2,1,0,5:T(8,128)} reshape(f32[3,576,12,64]{3,2,1,0:T(8,128)} %copy.113) | data formatting | bytes 10616832 | tf_op jit(solution)/shard_map/while/body/eval_jaxpr/stack | solution.py:181
  270.9 5.4 %constant_dynamic-update-slice_fusion.4 = f32[3,3,3,8,8,2,768]{6,4,3,2,1,0,5:T(8,128)} fusion(f32[3,3,3,8,8,1,768]{6,4,3,2,1,0,5:T(8,128)} %stack.71), kind=kLoop, calls=%fused_computation.36.clone.1 | loop fusion | bytes 10616832 | tf_op jit(solution)/shard_map/while
  276.3 13.9 %copy.114 = f32[3,576,12,64]{3,2,1,0:T(8,128)} copy(f32[3,576,12,64]{1,3,2,0:T(8,128)} %convolution_bitcast_fusion.5) | data formatting | bytes 10616832 | tf_op jit(solution)/shard_map/while/body/eval_jaxpr/thqk,tqhd->tkhd/transpose | solution.py:175
  290.2 11.7 %stack.72 = f32[3,3,3,8,8,1,768]{6,4,3,2,1,0,5:T(8,128)} reshape(f32[3,576,12,64]{3,2,1,0:T(8,128)} %copy.114) | data formatting | bytes 10616832 | tf_op jit(solution)/shard_map/while/body/eval_jaxpr/stack | solution.py:181
  301.9 5.4 %constant_dynamic-update-slice_fusion.5 = f32[3,3,3,8,8,2,768]{6,4,3,2,1,0,5:T(8,128)} fusion(f32[3,3,3,8,8,2,768]{6,4,3,2,1,0,5:T(8,128)} %constant_dynamic-update-slice_fusion.4, f32[3,3,3,8,8,1,768]{6,4,3,2,1,0,5:T(8,128)} %stack.72), kind=kLoop, calls=%fused_computation.35.clone.1 | loop fusion | bytes 10616832 | tf_op jit(solution)/shard_map/while/body/eval_jaxpr/stack | solution.py:181
  307.3 6.6 %slice_bitcast_fusion.16 = (f32[3,8,3,8,2,768]{5,3,1,0,2,4:T(8,128)S(1)}, f32[3,8,3,8,2,768]{5,3,1,0,2,4:T(8,128)S(1)}, f32[3,8,3,8,2,768]{5,3,1,0,2,4:T(8,128)}) fusion(f32[3,3,3,8,8,2,768]{6,4,3,2,1,0,5:T(8,128)} %constant_dynamic-update-slice_fusion.5), kind=kLoop, calls=%fused_computation.12.clone.1 | loop fusion | bytes 21233664 | tf_op jit(solution)/shard_map/while/body/eval_jaxpr/transpose | solution.py:68
  313.9 2.8 pad_add_fusion.5
  317.5 6.0 %copy_dynamic-update-slice_fusion.2 = f32[32,40,2,768]{3,1,0,2:T(8,128)} fusion(f32[32,40,2,768]{3,1,0,2:T(8,128)} %get-tuple-element.326, s32[]{:T(128)S(6)} %select_n.108, f32[24,40,2,768]{3,1,2,0:T(8,128)S(1)} %bitcast.154), kind=kLoop, calls=%fused_computation.clone.1 | loop fusion | flops 1474560 | bytes 17695744 | tf_op jit(solution)/shard_map/while/body/eval_jaxpr/dynamic_update_slice | solution.py:187
  327.6 3.6 collective-permute-start.9
  331.3 16.5 %collective-permute-done.8 = f32[32,8,2,768]{3,1,0,2:T(8,128)S(1)} collective-permute-done((f32[32,8,2,768]{3,1,0,2:T(8,128)S(1)}, f32[32,8,2,768]{3,1,0,2:T(8,128)S(1)}, u32[]{:S(2)}, u32[]{:S(2)}) %collective-permute-start.8) | collective-permute-done | bytes 1572896 | tf_op jit(solution)/shard_map/ppermute | solution.py:31
  348.6 3.0 pad_add_fusion.1
  353.1 4.1 %collective-permute-start.11 = (f32[8,24,2,768]{3,1,0,2:T(8,128)S(1)}, f32[8,24,2,768]{3,1,0,2:T(8,128)S(1)}, u32[]{:S(2)}, u32[]{:S(2)}) collective-permute-start(f32[8,24,2,768]{3,1,0,2:T(8,128)S(1)} %get-tuple-element.198), channel_id=1, source_target_pairs={{0,4},{4,8},{8,12},{1,5},{5,9},{9,13},{2,6},{6,10},{10,14},{3,7},{... | collective-permute-start | bytes 3538952 | tf_op jit(solution)/shard_map/ppermute | solution.py:31
  357.1 11.6 %collective-permute-done.10 = f32[8,24,2,768]{3,1,0,2:T(8,128)S(1)} collective-permute-done((f32[8,24,2,768]{3,1,0,2:T(8,128)S(1)}, f32[8,24,2,768]{3,1,0,2:T(8,128)S(1)}, u32[]{:S(2)}, u32[]{:S(2)}) %collective-permute-start.10) | collective-permute-done | bytes 1179680 | tf_op jit(solution)/shard_map/ppermute | solution.py:31
  (139 shorter events, 75.7 us)
Async XLA Ops:
  0.6 50.8 %copy-start.7 = (bf16[16,24,768]{2,1,0:T(8,128)(2,1)S(1)}, bf16[16,24,768]{2,1,0:T(8,128)(2,1)}, u32[]{:S(2)}) copy-start(bf16[16,24,768]{2,1,0:T(8,128)(2,1)} %param.9) | copy-start | bytes 1769476
  0.6 50.8 %copy-start.6 = (bf16[16,24,768]{2,1,0:T(8,128)(2,1)S(1)}, bf16[16,24,768]{2,1,0:T(8,128)(2,1)}, u32[]{:S(2)}) copy-start(bf16[16,24,768]{2,1,0:T(8,128)(2,1)} %param.8) | copy-start | bytes 1769476
  0.7 30.6 %copy-start.9 = (s32[2,3]{1,0:T(2,128)S(1)}, s32[2,3]{1,0:T(2,128)}, u32[]{:S(2)}) copy-start(s32[2,3]{1,0:T(2,128)} %param.11) | copy-start | bytes 76
  0.7 36.5 %copy-start.8 = (bf16[16,24,768]{2,1,0:T(8,128)(2,1)S(1)}, bf16[16,24,768]{2,1,0:T(8,128)(2,1)}, u32[]{:S(2)}) copy-start(bf16[16,24,768]{2,1,0:T(8,128)(2,1)} %param.10) | copy-start | bytes 1769476
  2.1 16.0 %collective-permute-start.4 = (bf16[8,24,2,768]{3,1,0,2:T(8,128)(2,1)S(1)}, bf16[8,24,2,768]{3,1,0,2:T(8,128)(2,1)S(1)}, u32[]{:S(2)}, u32[]{:S(2)}) collective-permute-start(bf16[8,24,2,768]{3,1,0,2:T(8,128)(2,1)S(1)} %get-tuple-element.203), channel_id=1, source_target_pairs={{0,4},{4,8},{8,12},{1,5},{5,9},{9,13},{2,6},{6,10},{10,14},{3,7},{... | collective-permute-start | bytes 1769480 | tf_op jit(solution)/shard_map/ppermute | solution.py:22
  6.2 15.8 %collective-permute-start.5 = (bf16[8,24,2,768]{3,1,0,2:T(8,128)(2,1)S(1)}, bf16[8,24,2,768]{3,1,0,2:T(8,128)(2,1)S(1)}, u32[]{:S(2)}, u32[]{:S(2)}) collective-permute-start(bf16[8,24,2,768]{3,1,0,2:T(8,128)(2,1)S(1)} %get-tuple-element.204), channel_id=1, source_target_pairs={{4,0},{8,4},{12,8},{5,1},{9,5},{13,9},{6,2},{10,6},{14,10},{7,3},{... | collective-permute-start | bytes 1769480 | tf_op jit(solution)/shard_map/ppermute | solution.py:23
  24.5 26.9 %collective-permute-start.6 = (bf16[32,8,2,768]{3,1,0,2:T(8,128)(2,1)}, bf16[32,8,2,768]{3,1,0,2:T(8,128)(2,1)}, u32[]{:S(2)}, u32[]{:S(2)}) collective-permute-start(bf16[32,8,2,768]{3,1,0,2:T(8,128)(2,1)} %get-tuple-element.199), channel_id=1, source_target_pairs={{0,1},{1,2},{2,3},{4,5},{5,6},{6,7},{8,9},{9,10},{10,11},{12,13},{... | collective-permute-start | bytes 2359304 | tf_op jit(solution)/shard_map/ppermute | solution.py:22
  29.3 22.1 %collective-permute-start.7 = (bf16[32,8,2,768]{3,1,0,2:T(8,128)(2,1)}, bf16[32,8,2,768]{3,1,0,2:T(8,128)(2,1)}, u32[]{:S(2)}, u32[]{:S(2)}) collective-permute-start(bf16[32,8,2,768]{3,1,0,2:T(8,128)(2,1)} %get-tuple-element.200), channel_id=1, source_target_pairs={{1,0},{2,1},{3,2},{5,4},{6,5},{7,6},{9,8},{10,9},{11,10},{13,12},{... | collective-permute-start | bytes 2359304 | tf_op jit(solution)/shard_map/ppermute | solution.py:23
  31.8 5.6 %collective-permute-start = (s32[1,3]{1,0:T(1,128)}, s32[1,3]{1,0:T(1,128)}, u32[]{:S(2)}, u32[]{:S(2)}) collective-permute-start(s32[1,3]{1,0:T(1,128)} %get-tuple-element.207), channel_id=1, source_target_pairs={{0,4},{4,8},{8,12},{1,5},{5,9},{9,13},{2,6},{6,10},{10,14},{3,7},{... | collective-permute-start | bytes 44 | tf_op jit(solution)/shard_map/ppermute | solution.py:22
  35.5 4.5 %collective-permute-start.1 = (s32[1,3]{1,0:T(1,128)}, s32[1,3]{1,0:T(1,128)}, u32[]{:S(2)}, u32[]{:S(2)}) collective-permute-start(s32[1,3]{1,0:T(1,128)} %get-tuple-element.208), channel_id=1, source_target_pairs={{4,0},{8,4},{12,8},{5,1},{9,5},{13,9},{6,2},{10,6},{14,10},{7,3},{... | collective-permute-start | bytes 44 | tf_op jit(solution)/shard_map/ppermute | solution.py:23
  40.8 6.8 %collective-permute-start.2 = (s32[4,1]{1,0:T(4,128)S(1)}, s32[4,1]{1,0:T(4,128)S(1)}, u32[]{:S(2)}, u32[]{:S(2)}) collective-permute-start(s32[4,1]{1,0:T(4,128)S(1)} %get-tuple-element.205), channel_id=1, source_target_pairs={{0,1},{1,2},{2,3},{4,5},{5,6},{6,7},{8,9},{9,10},{10,11},{12,13},{... | collective-permute-start | bytes 56 | tf_op jit(solution)/shard_map/ppermute | solution.py:22
  45.7 4.9 %collective-permute-start.3 = (s32[4,1]{1,0:T(4,128)S(1)}, s32[4,1]{1,0:T(4,128)S(1)}, u32[]{:S(2)}, u32[]{:S(2)}) collective-permute-start(s32[4,1]{1,0:T(4,128)S(1)} %get-tuple-element.206), channel_id=1, source_target_pairs={{1,0},{2,1},{3,2},{5,4},{6,5},{7,6},{9,8},{10,9},{11,10},{13,12},{... | collective-permute-start | bytes 56 | tf_op jit(solution)/shard_map/ppermute | solution.py:23
  58.3 4.7 %copy-start.10 = (s32[2]{0:T(128)}, s32[2]{0:T(128)S(1)}, u32[]{:S(2)}) copy-start(s32[2]{0:T(128)S(1)} %get-tuple-element.346) | copy-start | bytes 28 | tf_op jit(solution)/shard_map/while
  58.3 6.2 %copy-start.4 = (bf16[16,24,768]{2,1,0:T(8,128)(2,1)}, bf16[16,24,768]{2,1,0:T(8,128)(2,1)S(1)}, u32[]{:S(2)}) copy-start(bf16[16,24,768]{2,1,0:T(8,128)(2,1)S(1)} %get-tuple-element.351) | copy-start | bytes 1769476 | tf_op jit(solution)/shard_map/while
  84.6 1.8 copy-start.2
  84.6 2.0 copy-start.3
  92.0 1.9 copy-start
  97.3 11.8 %copy-start.1 = (bf16[3,12,64,576]{3,2,1,0:T(8,128)(2,1)S(1)}, bf16[3,12,64,576]{3,2,1,0:T(8,128)(2,1)}, u32[]{:S(2)}) copy-start(bf16[3,12,64,576]{3,2,1,0:T(8,128)(2,1)} %copy-done) | copy-start | bytes 7962628 | tf_op jit(solution)/shard_map/while
  184.9 6.0 %copy-start.5 = (bf16[16,24,768]{2,1,0:T(8,128)(2,1)S(1)}, bf16[16,24,768]{2,1,0:T(8,128)(2,1)}, u32[]{:S(2)}) copy-start(bf16[16,24,768]{2,1,0:T(8,128)(2,1)} %copy-done.4) | copy-start | bytes 1769476 | tf_op jit(solution)/shard_map/while
  184.9 6.0 %copy-start.11 = (s32[2]{0:T(128)S(1)}, s32[2]{0:T(128)}, u32[]{:S(2)}) copy-start(s32[2]{0:T(128)} %copy-done.10) | copy-start | bytes 28 | tf_op jit(solution)/shard_map/while
  190.9 4.7 %copy-start.10 = (s32[2]{0:T(128)}, s32[2]{0:T(128)S(1)}, u32[]{:S(2)}) copy-start(s32[2]{0:T(128)S(1)} %get-tuple-element.346) | copy-start | bytes 28 | tf_op jit(solution)/shard_map/while
  190.9 6.2 %copy-start.4 = (bf16[16,24,768]{2,1,0:T(8,128)(2,1)}, bf16[16,24,768]{2,1,0:T(8,128)(2,1)S(1)}, u32[]{:S(2)}) copy-start(bf16[16,24,768]{2,1,0:T(8,128)(2,1)S(1)} %get-tuple-element.351) | copy-start | bytes 1769476 | tf_op jit(solution)/shard_map/while
  217.2 1.8 copy-start.2
  217.2 2.0 copy-start.3
  224.7 1.9 copy-start
  229.9 11.8 %copy-start.1 = (bf16[3,12,64,576]{3,2,1,0:T(8,128)(2,1)S(1)}, bf16[3,12,64,576]{3,2,1,0:T(8,128)(2,1)}, u32[]{:S(2)}) copy-start(bf16[3,12,64,576]{3,2,1,0:T(8,128)(2,1)} %copy-done) | copy-start | bytes 7962628 | tf_op jit(solution)/shard_map/while
  317.5 6.0 %copy-start.5 = (bf16[16,24,768]{2,1,0:T(8,128)(2,1)S(1)}, bf16[16,24,768]{2,1,0:T(8,128)(2,1)}, u32[]{:S(2)}) copy-start(bf16[16,24,768]{2,1,0:T(8,128)(2,1)} %copy-done.4) | copy-start | bytes 1769476 | tf_op jit(solution)/shard_map/while
  317.5 6.0 %copy-start.11 = (s32[2]{0:T(128)S(1)}, s32[2]{0:T(128)}, u32[]{:S(2)}) copy-start(s32[2]{0:T(128)} %copy-done.10) | copy-start | bytes 28 | tf_op jit(solution)/shard_map/while
  325.7 22.0 %collective-permute-start.8 = (f32[32,8,2,768]{3,1,0,2:T(8,128)S(1)}, f32[32,8,2,768]{3,1,0,2:T(8,128)S(1)}, u32[]{:S(2)}, u32[]{:S(2)}) collective-permute-start(f32[32,8,2,768]{3,1,0,2:T(8,128)S(1)} %get-tuple-element.195), channel_id=1, source_target_pairs={{1,0},{2,1},{3,2},{5,4},{6,5},{7,6},{9,8},{10,9},{11,10},{13,12},{... | collective-permute-start | bytes 4718600 | tf_op jit(solution)/shard_map/ppermute | solution.py:31
  327.6 21.0 %collective-permute-start.9 = (f32[32,8,2,768]{3,1,0,2:T(8,128)S(1)}, f32[32,8,2,768]{3,1,0,2:T(8,128)S(1)}, u32[]{:S(2)}, u32[]{:S(2)}) collective-permute-start(f32[32,8,2,768]{3,1,0,2:T(8,128)S(1)} %get-tuple-element.196), channel_id=1, source_target_pairs={{0,1},{1,2},{2,3},{4,5},{5,6},{6,7},{8,9},{9,10},{10,11},{12,13},{... | collective-permute-start | bytes 4718600 | tf_op jit(solution)/shard_map/ppermute | solution.py:31
  351.8 16.9 %collective-permute-start.10 = (f32[8,24,2,768]{3,1,0,2:T(8,128)S(1)}, f32[8,24,2,768]{3,1,0,2:T(8,128)S(1)}, u32[]{:S(2)}, u32[]{:S(2)}) collective-permute-start(f32[8,24,2,768]{3,1,0,2:T(8,128)S(1)} %get-tuple-element.197), channel_id=1, source_target_pairs={{4,0},{8,4},{12,8},{5,1},{9,5},{13,9},{6,2},{10,6},{14,10},{7,3},{... | collective-permute-start | bytes 3538952 | tf_op jit(solution)/shard_map/ppermute | solution.py:31
  353.1 17.1 %collective-permute-start.11 = (f32[8,24,2,768]{3,1,0,2:T(8,128)S(1)}, f32[8,24,2,768]{3,1,0,2:T(8,128)S(1)}, u32[]{:S(2)}, u32[]{:S(2)}) collective-permute-start(f32[8,24,2,768]{3,1,0,2:T(8,128)S(1)} %get-tuple-element.198), channel_id=1, source_target_pairs={{0,4},{4,8},{8,12},{1,5},{5,9},{9,13},{2,6},{6,10},{10,14},{3,7},{... | collective-permute-start | bytes 3538952 | tf_op jit(solution)/shard_map/ppermute | solution.py:31
where the time goes:
time: 377 us; the launch traced here: 372 us
  local copies, waits for them, and re-layouts  212 us (56%)
  waiting for transfers between devices  50.5 us (13%)
  starting transfers between devices  34.9 us (9%)
  other arithmetic  34.7 us (9%)
  matrix products  30.5 us (8%)
  loops' own time  8.25 us (2%)
    another operation x6, local copies, waits for them, and re-layouts, step_sums(): jnp.stack((key_part, value_part), axis=2)  57.5 us
    ppermute x4, waiting for transfers between devices, from_behind(): return lax.ppermute(shard, axis, pairs)  30.4 us
    transpose x2, local copies, waits for them, and re-layouts, step_sums(): jnp.einsum('thqk,tqhd->tkhd', grad_scores, split_heads(query_tiles), pref...  28 us
    transpose x2, local copies, waits for them, and re-layouts, step_sums(): jnp.einsum('thqk,tqhd->tkhd', probs_low, split_heads(grad_tiles), preferr...  27.8 us
    ppermute x4, starting transfers between devices, with_halo(): before = lax.ppermute(last, axis, up)  17.6 us
    slice x4, local copies, waits for them, and re-layouts, first_rows(): near_pairs[:, :, 1]  16.1 us
    transpose x2, local copies, waits for them, and re-layouts, stripe_sum(): reordered = column_piece.transpose((1, 2, 0, 3) + trailing(4, column_piece))  13.3 us
    dynamic_update_slice x2, other arithmetic, step_sums(): lax.dynamic_update_slice_in_dim(running, current + stripe, first_row, 0)  12 us
  transfers between devices with their start and end apart: 12, of which 8 were waited for; matrix products, arithmetic and copies ran while one was open for 1% of the time, Pallas kernels for 0%

commit v1 on v0

v1 whole, which is shorter than its diff:
```python
import jax
import jax.numpy as jnp
from jax import lax
from jax.experimental import pallas as pl
from jax.experimental.pallas import tpu as pltpu
from jax.sharding import PartitionSpec as P

HEAD = 64
TILE = 8
TOKENS = TILE * TILE
LANES = 256
PER = LANES // HEAD
SCALE = HEAD ** -0.5
LOG2E = 1.4426950408889634
NEG = -1e30
BIG = 1e30
LIMIT = 56 * 1024 * 1024


def shift(array, axis, by):
    count = lax.axis_size(axis)
    pairs = [(i, i + by) for i in range(count) if 0 <= i + by < count]
    return lax.ppermute(array, axis, pairs)


def nt(a, b):
    return lax.dot_general(a, b, (((1,), (1,)), ((), ())), preferred_element_type=jnp.float32)


def nn(a, b):
    return lax.dot_general(a, b, (((1,), (0,)), ((), ())), preferred_element_type=jnp.float32)


def tn(a, b):
    return lax.dot_general(a, b, (((0,), (0,)), ((), ())), preferred_element_type=jnp.float32)


def tile_of(ref, a, b):
    block = ref[TILE * a : TILE * (a + 1), TILE * b : TILE * (b + 1), :]
    return block.astype(jnp.float32).reshape(TOKENS, block.shape[-1])


def put_tile(ref, a, b, value):
    shaped = value.reshape(TILE, TILE, value.shape[-1]).astype(ref.dtype)
    ref[TILE * a : TILE * (a + 1), TILE * b : TILE * (b + 1), :] = shaped


def pack(first, second, tissue, scaled):
    rows, cols = tissue.shape
    width = first.shape[-1]

    def body(mark_ref, first_ref, second_ref, *outs):
        row_refs, left_ref, right_ref = outs[:rows], outs[rows], outs[rows + 1]
        for a in range(rows):
            for b in range(cols):
                for n, ref in enumerate((first_ref, second_ref)):
                    tile = tile_of(ref, a, b)
                    if scaled:
                        tile = tile * (SCALE if n == 0 else mark_ref[a, b].astype(jnp.float32))
                    tile = tile.astype(jnp.bfloat16)
                    row_refs[a][n, b] = tile
                    if b == 0:
                        left_ref[n, a] = tile
                    if b == cols - 1:
                        right_ref[n, a] = tile

    row_shape = jax.ShapeDtypeStruct((2, cols, TOKENS, width), jnp.bfloat16)
    side_shape = jax.ShapeDtypeStruct((2, rows, TOKENS, width), jnp.bfloat16)
    vmem = pl.BlockSpec(memory_space=pltpu.VMEM)
    return pl.pallas_call(
        body,
        in_specs=[pl.BlockSpec(memory_space=pltpu.SMEM), vmem, vmem],
        out_specs=[vmem] * (rows + 2),
        out_shape=[row_shape] * rows + [side_shape] * 2,
        compiler_params=pltpu.CompilerParams(vmem_limit_bytes=LIMIT),
    )(tissue, first, second)


def halo(row_first, row_last, left, right):
    above = shift(row_last, "rows", 1)
    below = shift(row_first, "rows", -1)
    from_left = shift(right, "cols", 1)
    from_right = shift(left, "cols", -1)
    corner_left = shift(jnp.stack((above[:, -1], below[:, -1]), axis=1), "cols", 1)
    corner_right = shift(jnp.stack((above[:, 0], below[:, 0]), axis=1), "cols", -1)
    return above, below, from_left, from_right, corner_left, corner_right


def head_mask():
    row = lax.broadcasted_iota(jnp.int32, (LANES, LANES), 0) // HEAD
    lane = lax.broadcasted_iota(jnp.int32, (LANES, LANES), 1) // HEAD
    return row == lane


def spread(tile, mask):
    return jnp.where(mask, jnp.concatenate([tile] * PER, axis=0), jnp.zeros((), tile.dtype))


def gather_heads(full):
    lane = lax.broadcasted_iota(jnp.int32, (TOKENS, LANES), 1) // HEAD
    out = full[:TOKENS]
    for h in range(1, PER):
        out = jnp.where(lane == h, full[h * TOKENS : (h + 1) * TOKENS], out)
    return out


class Ext:
    def __init__(self, rows, cols, own, near):
        self.rows, self.cols, self.own, self.near = rows, cols, own, near

    def at(self, n, i, j):
        above, below, left, right, corner_left, corner_right = self.near
        if 0 <= i < self.rows:
            if j < 0:
                return left[n, i]
            if j >= self.cols:
                return right[n, i]
            return self.own[i][n, j]
        end = 0 if i < 0 else 1
        if j < 0:
            return corner_left[n, end]
        if j >= self.cols:
            return corner_right[n, end]
        return (above, below)[end][n, j]


def query_kernel(rows, cols):
    def body(mark_ref, *refs):
        own_kv, refs = refs[:rows], refs[rows:]
        near_kv, refs = refs[:6], refs[6:]
        own_qg, refs = refs[:rows], refs[rows:]
        att_ref, gq_ref, stat_refs = refs[0], refs[1], refs[2 : 2 + rows]
        sum_ref, s_ref, e_ref = refs[2 + rows :]
        keys = Ext(rows, cols, own_kv, near_kv)
        mask = head_mask()
        sum_ref[...] = jnp.zeros(sum_ref.shape, jnp.float32)
        for a in range(rows):
            for b in range(cols):
                places = [(a + i, b + j) for i in (-1, 0, 1) for j in (-1, 0, 1)]
                own_mark = mark_ref[a + 1, b + 1]
                allowed = [
                    True if (i, j) == (a, b) else own_mark * mark_ref[i + 1, j + 1] > 0
                    for i, j in places
                ]
                q = spread(own_qg[a][0, b], mask)
                g = spread(own_qg[a][1, b], mask)
                top = jnp.full((1, LANES), NEG, jnp.float32)
                for t, (i, j) in enumerate(places):
                    s = nt(keys.at(0, i, j), q)
                    s_ref[t * TOKENS : (t + 1) * TOKENS] = s
                    high = jnp.max(s, axis=0, keepdims=True)
                    top = jnp.maximum(top, jnp.where(allowed[t], high, NEG))
                top = top * LOG2E
                total = jnp.zeros((1, LANES), jnp.float32)
                for t in range(9):
                    e = jnp.exp2(s_ref[t * TOKENS : (t + 1) * TOKENS] * LOG2E - jnp.where(allowed[t], top, BIG))
                    s_ref[t * TOKENS : (t + 1) * TOKENS] = e
                    total = total + jnp.sum(e, axis=0, keepdims=True)
                inv = 1.0 / total
                for t in range(9):
                    p = s_ref[t * TOKENS : (t + 1) * TOKENS] * inv
                    s_ref[t * TOKENS : (t + 1) * TOKENS] = p
                    e_ref[t * TOKENS : (t + 1) * TOKENS] = p.astype(jnp.bfloat16)
                v_all = jnp.concatenate([keys.at(1, i, j) for i, j in places], axis=0)
                k_all = jnp.concatenate([keys.at(0, i, j) for i, j in places], axis=0)
                att = gather_heads(tn(e_ref[...], v_all)) * own_mark.astype(jnp.float32)
                att = att.astype(jnp.bfloat16)
                put_tile(att_ref, a, b, att.astype(jnp.float32))
                prod = (own_qg[a][1, b].astype(jnp.float32) * att.astype(jnp.float32)).T
                dot = jnp.concatenate(
                    [jnp.sum(prod[h * HEAD : (h + 1) * HEAD], axis=0, keepdims=True) for h in range(PER)],
                    axis=1,
                )
                stat_refs[a][0, b, 0:1] = top + jnp.log2(total)
                stat_refs[a][0, b, 1:2] = dot
                for t, (i, j) in enumerate(places):
                    if 0 <= i < rows and 0 <= j < cols:
                        sum_ref[1, i * cols + j] += nn(e_ref[t * TOKENS : (t + 1) * TOKENS], g)
                for t, (i, j) in enumerate(places):
                    gp = nt(keys.at(1, i, j), g)
                    ds = s_ref[t * TOKENS : (t + 1) * TOKENS] * (gp - dot)
                    e_ref[t * TOKENS : (t + 1) * TOKENS] = ds.astype(jnp.bfloat16)
                put_tile(gq_ref, a, b, gather_heads(tn(e_ref[...], k_all)) * SCALE)
                for t, (i, j) in enumerate(places):
                    if 0 <= i < rows and 0 <= j < cols:
                        sum_ref[0, i * cols + j] += nn(e_ref[t * TOKENS : (t + 1) * TOKENS], q)

    return body


def key_kernel(rows, cols):
    def body(mark_ref, *refs):
        own_kv, refs = refs[:rows], refs[rows:]
        near_qg, refs = refs[:6], refs[6:]
        near_stat, refs = refs[:6], refs[6:]
        sum_ref, gk_ref, gv_ref, acc_ref = refs
        queries = Ext(rows, cols, None, near_qg)
        above_s, below_s, left_s, right_s, corner_left_s, corner_right_s = near_stat
        mask = head_mask()
        acc_ref[...] = sum_ref[...]

        def stat_at(i, j):
            if 0 <= i < rows:
                return (left_s if j < 0 else right_s)[0, i]
            end = 0 if i < 0 else 1
            if j < 0:
                return corner_left_s[0, end]
            if j >= cols:
                return corner_right_s[0, end]
            return (above_s, below_s)[end][0, j]

        for i in range(-1, rows + 1):
            for j in range(-1, cols + 1):
                if 0 <= i < rows and 0 <= j < cols:
                    continue
                places = [
                    (x, y)
                    for x in range(max(i - 1, 0), min(i + 2, rows))
                    for y in range(max(j - 1, 0), min(j + 2, cols))
                ]
                q = spread(queries.at(0, i, j), mask)
                g = spread(queries.at(1, i, j), mask)
                stat = stat_at(i, j)
                own_mark = mark_ref[i + 1, j + 1]
                for x, y in places:
                    allowed = own_mark * mark_ref[x + 1, y + 1] > 0
                    s = nt(own_kv[x][0, y], q)
                    p = jnp.exp2(s * LOG2E - jnp.where(allowed, stat[0:1], BIG))
                    gp = nt(own_kv[x][1, y], g)
                    ds = (p * (gp - stat[1:2])).astype(jnp.bfloat16)
                    acc_ref[1, x * cols + y] += nn(p.astype(jnp.bfloat16), g)
                    acc_ref[0, x * cols + y] += nn(ds, q)
        for x in range(rows):
            for y in range(cols):
                put_tile(gk_ref, x, y, acc_ref[0, x * cols + y])
                put_tile(gv_ref, x, y, acc_ref[1, x * cols + y])

    return body


def tiles_spec(shape):
    return pl.BlockSpec(tuple(shape[:-1]) + (LANES,), lambda g: (0,) * (len(shape) - 1) + (g,))


def stat_spec(shape):
    return pl.BlockSpec((1,) + tuple(shape[1:]), lambda g: (g,) + (0,) * (len(shape) - 1))


def specs(arrays):
    return [tiles_spec(array.shape) for array in arrays]


def local(query_grid, key_grid, value_grid, out_grad, tissue):
    rows, cols = tissue.shape
    width = query_grid.shape[-1]
    groups = width // LANES
    own_kv = pack(key_grid, value_grid, tissue, False)
    near_kv = halo(own_kv[0], own_kv[rows - 1], own_kv[rows], own_kv[rows + 1])
    own_qg = pack(query_grid, out_grad, tissue, True)
    near_qg = halo(own_qg[0], own_qg[rows - 1], own_qg[rows], own_qg[rows + 1])
    marks = tissue
    for axis, dim in (("rows", 0), ("cols", 1)):
        length = marks.shape[dim]
        before = shift(lax.slice_in_dim(marks, length - 1, length, axis=dim), axis, 1)
        after = shift(lax.slice_in_dim(marks, 0, 1, axis=dim), axis, -1)
        marks = jnp.concatenate([before, marks, after], axis=dim)
    own_kv, own_qg = own_kv[:rows], own_qg[:rows]
    grid_out = jax.ShapeDtypeStruct(query_grid.shape, jnp.bfloat16)
    stat_out = jax.ShapeDtypeStruct((groups, cols, 2, LANES), jnp.float32)
    sum_out = jax.ShapeDtypeStruct((2, rows * cols, TOKENS, width), jnp.float32)
    smem = pl.BlockSpec(memory_space=pltpu.SMEM)
    attended, grad_query, *rest = pl.pallas_call(
        query_kernel(rows, cols),
        grid=(groups,),
        in_specs=[smem] + specs(own_kv) + specs(near_kv) + specs(own_qg),
        out_specs=[tiles_spec(grid_out.shape)] * 2 + [stat_spec(stat_out.shape)] * rows + [tiles_spec(sum_out.shape)],
        out_shape=[grid_out] * 2 + [stat_out] * rows + [sum_out],
        scratch_shapes=[pltpu.VMEM((9 * TOKENS, LANES), jnp.float32), pltpu.VMEM((9 * TOKENS, LANES), jnp.bfloat16)],
        compiler_params=pltpu.CompilerParams(vmem_limit_bytes=LIMIT),
    )(marks, *own_kv, *near_kv, *own_qg)
    stats, sums = rest[:rows], rest[rows]
    above = shift(stats[rows - 1], "rows", 1)
    below = shift(stats[0], "rows", -1)
    side = lambda j: jnp.stack([stat[:, j] for stat in stats] + [above[:, j], below[:, j]], axis=1)
    from_left = shift(side(cols - 1), "cols", 1)
    from_right = shift(side(0), "cols", -1)
    near_stat = (above, below, from_left[:, :rows], from_right[:, :rows], from_left[:, rows:], from_right[:, rows:])
    grad_key, grad_value = pl.pallas_call(
        key_kernel(rows, cols),
        grid=(groups,),
        in_specs=[smem] + specs(own_kv) + specs(near_qg) + [stat_spec(s.shape) for s in near_stat] + [tiles_spec(sums.shape)],
        out_specs=[tiles_spec(grid_out.shape)] * 2,
        out_shape=[grid_out] * 2,
        scratch_shapes=[pltpu.VMEM((2, rows * cols, TOKENS, LANES), jnp.float32)],
        compiler_params=pltpu.CompilerParams(vmem_limit_bytes=LIMIT),
    )(marks, *own_kv, *near_qg, *near_stat, sums)
    return attended, grad_query, grad_key, grad_value


def solution(mesh):
    grid = P(("groups", "rows"), "cols", None)
    return jax.shard_map(
        local,
        mesh=mesh,
        in_specs=(grid, grid, grid, grid, P(("groups", "rows"), "cols")),
        out_specs=(grid, grid, grid, grid),
        check_vma=False,
    )
```

time: 377 us -> 137 us (0.36); the launches traced: 372 us -> 137 us
  local copies, waits for them, and re-layouts: 212 us -> 4.8 us
  Pallas kernels: 0 us -> 54 us
  other arithmetic: 34.7 us -> 0.87 us
  matrix products: 30.5 us -> 0 us
  waiting for transfers between devices: 50.5 us -> 23.5 us
  starting transfers between devices: 34.9 us -> 52.2 us
  loops' own time: 8.25 us -> 0 us
    transpose x18 -> x0, local copies, waits for them, and re-layouts: 72.7 us -> none  [the longest x2 28 us: step_sums(): jnp.einsum('thqk,tqhd->tkhd', grad_scores, split_heads(query_tiles), pref...]
    another operation x10 -> x0, local copies, waits for them, and re-layouts: 58.5 us -> none  [the longest x6 57.5 us: step_sums(): jnp.stack((key_part, value_part), axis=2)]
    pallas_call x0 -> x4, Pallas kernels: none -> 54 us  [the longest x1 29.1 us: local(): pl.pallas_call(query_kernel(rows, cols), grid=(groups,), in_specs=[smem]...]
    dot_general x12 -> x0, matrix products: 30.5 us -> none  [the longest x2 6.97 us: step_sums(): jnp.einsum('thqk,tqhd->tkhd', grad_scores, split_heads(query_tiles), pref...]
    ppermute x12 -> x20, waiting for transfers between devices: 50.5 us -> 23.5 us  [shift(): return lax.ppermute(array, axis, pairs)]
    slice x10 -> x11, local copies, waits for them, and re-layouts: 27.1 us -> 2.92 us  [the longest x2 0.83 us: local(): lax.slice_in_dim(marks, length - 1, length, axis=dim)]
    ppermute x12 -> x20, starting transfers between devices: 34.9 us -> 52.2 us  [shift(): return lax.ppermute(array, axis, pairs)]
    reshape x14 -> x0, local copies, waits for them, and re-layouts: 15.2 us -> none  [the longest x4 9.36 us: tiles_rows(): shaped = tiles.reshape((number, TILE, TILE) + inner_shape)]
  transfers between devices with their start and end apart: 12 -> 20, of which waited for: 8 -> 8; matrix products, arithmetic and copies ran while one was open for 1% -> 3% of each run, Pallas kernels for 0% -> 23%
where the time goes in v1:
time: 137 us
  Pallas kernels  54 us (39%)
  starting transfers between devices  52.2 us (38%)
  waiting for transfers between devices  23.5 us (17%)
  local copies, waits for them, and re-layouts  4.8 us (4%)
    ppermute x20, starting transfers between devices, shift(): return lax.ppermute(array, axis, pairs)  52.2 us
    pallas_call x1, Pallas kernels, local(): pl.pallas_call(query_kernel(rows, cols), grid=(groups,), in_specs=[smem]...  29.1 us
    ppermute x20, waiting for transfers between devices, shift(): return lax.ppermute(array, axis, pairs)  23.5 us
    pallas_call x1, Pallas kernels, local(): pl.pallas_call(key_kernel(rows, cols), grid=(groups,), in_specs=[smem] +...  19.6 us
    pallas_call x2, Pallas kernels, pack(): pl.pallas_call(body, in_specs=[pl.BlockSpec(memory_space=pltpu.SMEM), vme...  5.23 us
  transfers between devices with their start and end apart: 20, of which 8 were waited for; matrix products, arithmetic and copies ran while one was open for 3% of the time, Pallas kernels for 23%

profile of v1, /device:TPU:1, one launch (start us, length us, event | category | flops | bytes accessed | tf_op | source)
XLA Modules:
  0.0 136.6 jit_solution(10156064067025488786)
XLA Ops:
  0.6 0.0 copy-start.14
  0.6 2.6 %shard_map.84 = (bf16[2,3,64,768]{3,2,1,0:T(8,128)(2,1)}, bf16[2,3,64,768]{3,2,1,0:T(8,128)(2,1)}, bf16[2,2,64,768]{3,2,1,0:T(8,128)(2,1)}, bf16[2,2,64,768]{3,2,1,0:T(8,128)(2,1)}) custom-call(s32[2,3]{1,0:T(2,128)} %mark_ref.3, bf16[16,24,768]{2,1,0:T(8,128)(2,1)} %first_ref.2, bf16[16,24,768]{2,1,0:T(8,128)(2,1)} %second_ref.2), custom_call_target="tpu_custom_call" | custom-call | tf_op jit(solution)/shard_map/pallas_call | solution.py:70
  3.2 4.1 %collective-permute-start.4 = (bf16[2,3,64,768]{3,2,1,0:T(8,128)(2,1)}, bf16[2,3,64,768]{3,2,1,0:T(8,128)(2,1)S(1)}, u32[]{:S(2)}, u32[]{:S(2)}) collective-permute-start(bf16[2,3,64,768]{3,2,1,0:T(8,128)(2,1)} %get-tuple-element.20.refs_1_), channel_id=1, source_target_pairs={{0,4},{4,8},{8,12},{1,5},{5,9},{9,13},{2,6},{6,10},{10,14},{3,7},{... | collective-permute-start | bytes 1769480 | tf_op jit(solution)/shard_map/ppermute | solution.py:23
  7.3 0.8 fusion.11
  8.0 3.2 %collective-permute-start = (s32[1,3]{1,0:T(1,128)S(1)}, s32[1,3]{1,0:T(1,128)S(1)}, u32[]{:S(2)}, u32[]{:S(2)}) collective-permute-start(s32[1,3]{1,0:T(1,128)S(1)} %get-tuple-element.56), channel_id=1, source_target_pairs={{0,4},{4,8},{8,12},{1,5},{5,9},{9,13},{2,6},{6,10},{10,14},{3,7},{... | collective-permute-start | bytes 44 | tf_op jit(solution)/shard_map/ppermute | solution.py:23
  11.2 1.3 collective-permute-start.1
  12.5 1.3 collective-permute-start.5
  13.8 4.2 %collective-permute-start.6 = (bf16[2,2,64,768]{3,2,1,0:T(8,128)(2,1)}, bf16[2,2,64,768]{3,2,1,0:T(8,128)(2,1)S(1)}, u32[]{:S(2)}, u32[]{:S(2)}) collective-permute-start(bf16[2,2,64,768]{3,2,1,0:T(8,128)(2,1)} %get-tuple-element.21), channel_id=1, source_target_pairs={{0,1},{1,2},{2,3},{4,5},{5,6},{6,7},{8,9},{9,10},{10,11},{12,13},{... | collective-permute-start | bytes 1179656 | tf_op jit(solution)/shard_map/ppermute | solution.py:23
  18.1 2.6 %shard_map.85 = (bf16[2,3,64,768]{3,2,1,0:T(8,128)(2,1)}, bf16[2,3,64,768]{3,2,1,0:T(8,128)(2,1)}, bf16[2,2,64,768]{3,2,1,0:T(8,128)(2,1)}, bf16[2,2,64,768]{3,2,1,0:T(8,128)(2,1)}) custom-call(s32[2,3]{1,0:T(2,128)} %mark_ref.3, bf16[16,24,768]{2,1,0:T(8,128)(2,1)} %first_ref.3, bf16[16,24,768]{2,1,0:T(8,128)(2,1)} %second_ref.3), custom_call_target="tpu_custom_call" | custom-call | tf_op jit(solution)/shard_map/pallas_call | solution.py:70
  20.7 2.3 %collective-permute-start.7 = (bf16[2,2,64,768]{3,2,1,0:T(8,128)(2,1)}, bf16[2,2,64,768]{3,2,1,0:T(8,128)(2,1)S(1)}, u32[]{:S(2)}, u32[]{:S(2)}) collective-permute-start(bf16[2,2,64,768]{3,2,1,0:T(8,128)(2,1)} %get-tuple-element.22), channel_id=1, source_target_pairs={{1,0},{2,1},{3,2},{5,4},{6,5},{7,6},{9,8},{10,9},{11,10},{13,12},{... | collective-permute-start | bytes 1179656 | tf_op jit(solution)/shard_map/ppermute | solution.py:23
  23.0 0.1 fusion.10
  23.1 3.3 %collective-permute-start.2 = (s32[4,1]{1,0:T(4,128)S(1)}, s32[4,1]{1,0:T(4,128)S(1)}, u32[]{:S(2)}, u32[]{:S(2)}) collective-permute-start(s32[4,1]{1,0:T(4,128)S(1)} %get-tuple-element.54), channel_id=1, source_target_pairs={{0,1},{1,2},{2,3},{4,5},{5,6},{6,7},{8,9},{9,10},{10,11},{12,13},{... | collective-permute-start | bytes 56 | tf_op jit(solution)/shard_map/ppermute | solution.py:23
  26.4 0.7 collective-permute-done.2
  27.1 1.9 %collective-permute-start.3 = (s32[4,1]{1,0:T(4,128)S(1)}, s32[4,1]{1,0:T(4,128)S(1)}, u32[]{:S(2)}, u32[]{:S(2)}) collective-permute-start(s32[4,1]{1,0:T(4,128)S(1)} %get-tuple-element.55), channel_id=1, source_target_pairs={{1,0},{2,1},{3,2},{5,4},{6,5},{7,6},{9,8},{10,9},{11,10},{13,12},{... | collective-permute-start | bytes 56 | tf_op jit(solution)/shard_map/ppermute | solution.py:23
  29.0 3.5 %collective-permute-done.3 = s32[4,1]{1,0:T(4,128)S(1)} collective-permute-done((s32[4,1]{1,0:T(4,128)S(1)}, s32[4,1]{1,0:T(4,128)S(1)}, u32[]{:S(2)}, u32[]{:S(2)}) %collective-permute-start.3) | collective-permute-done | bytes 48 | tf_op jit(solution)/shard_map/ppermute | solution.py:23
  32.5 4.9 %collective-permute-start.10 = (bf16[2,3,64,768]{3,2,1,0:T(8,128)(2,1)}, bf16[2,3,64,768]{3,2,1,0:T(8,128)(2,1)S(1)}, u32[]{:S(2)}, u32[]{:S(2)}) collective-permute-start(bf16[2,3,64,768]{3,2,1,0:T(8,128)(2,1)} %get-tuple-element.24.refs_9_), channel_id=1, source_target_pairs={{0,4},{4,8},{8,12},{1,5},{5,9},{9,13},{2,6},{6,10},{10,14},{3,7},{... | collective-permute-start | bytes 1769480 | tf_op jit(solution)/shard_map/ppermute | solution.py:23
  37.5 0.7 pad_add_fusion.1.mark_ref
  38.1 0.0 collective-permute-done.4.refs_2_
  38.1 1.3 collective-permute-start.11
  39.5 0.0 collective-permute-done.5.refs_3_
  39.5 0.0 copy-start.3
  39.5 2.2 %collective-permute-start.12 = (bf16[2,2,64,768]{3,2,1,0:T(8,128)(2,1)}, bf16[2,2,64,768]{3,2,1,0:T(8,128)(2,1)S(1)}, u32[]{:S(2)}, u32[]{:S(2)}) collective-permute-start(bf16[2,2,64,768]{3,2,1,0:T(8,128)(2,1)} %get-tuple-element.27), channel_id=1, source_target_pairs={{0,1},{1,2},{2,3},{4,5},{5,6},{6,7},{8,9},{9,10},{10,11},{12,13},{... | collective-permute-start | bytes 1179656 | tf_op jit(solution)/shard_map/ppermute | solution.py:23
  41.9 7.1 %collective-permute-done.10.refs_2_ = bf16[2,3,64,768]{3,2,1,0:T(8,128)(2,1)S(1)} collective-permute-done((bf16[2,3,64,768]{3,2,1,0:T(8,128)(2,1)}, bf16[2,3,64,768]{3,2,1,0:T(8,128)(2,1)S(1)}, u32[]{:S(2)}, u32[]{:S(2)}) %collective-permute-start.10) | collective-permute-done | bytes 589856 | tf_op jit(solution)/shard_map/ppermute | solution.py:23
  48.9 1.9 %collective-permute-start.9 = (bf16[2,2,64,768]{3,2,1,0:T(8,128)(2,1)S(1)}, bf16[2,2,64,768]{3,2,1,0:T(8,128)(2,1)S(1)}, u32[]{:S(2)}, u32[]{:S(2)}) collective-permute-start(bf16[2,2,64,768]{3,2,1,0:T(8,128)(2,1)S(1)} %pad_maximum_fusion.1), channel_id=1, source_target_pairs={{1,0},{2,1},{3,2},{5,4},{6,5},{7,6},{9,8},{10,9},{11,10},{13,12},{... | collective-permute-start | bytes 1179656 | tf_op jit(solution)/shard_map/ppermute | solution.py:23
  50.9 2.7 %collective-permute-done.11.refs_3_ = bf16[2,3,64,768]{3,2,1,0:T(8,128)(2,1)S(1)} collective-permute-done((bf16[2,3,64,768]{3,2,1,0:T(8,128)(2,1)}, bf16[2,3,64,768]{3,2,1,0:T(8,128)(2,1)S(1)}, u32[]{:S(2)}, u32[]{:S(2)}) %collective-permute-start.11) | collective-permute-done | bytes 589856 | tf_op jit(solution)/shard_map/ppermute | solution.py:23
  53.6 4.0 %collective-permute-start.8 = (bf16[2,2,64,768]{3,2,1,0:T(8,128)(2,1)S(1)}, bf16[2,2,64,768]{3,2,1,0:T(8,128)(2,1)S(1)}, u32[]{:S(2)}, u32[]{:S(2)}) collective-permute-start(bf16[2,2,64,768]{3,2,1,0:T(8,128)(2,1)S(1)} %pad_maximum_fusion), channel_id=1, source_target_pairs={{0,1},{1,2},{2,3},{4,5},{5,6},{6,7},{8,9},{9,10},{10,11},{12,13},{... | collective-permute-start | bytes 1179656 | tf_op jit(solution)/shard_map/ppermute | solution.py:23
  57.8 0.0 collective-permute-done.6.refs_4_
  57.8 1.9 %collective-permute-start.13 = (bf16[2,2,64,768]{3,2,1,0:T(8,128)(2,1)S(1)}, bf16[2,2,64,768]{3,2,1,0:T(8,128)(2,1)S(1)}, u32[]{:S(2)}, u32[]{:S(2)}) collective-permute-start(bf16[2,2,64,768]{3,2,1,0:T(8,128)(2,1)S(1)} %copy-done.15), channel_id=1, source_target_pairs={{1,0},{2,1},{3,2},{5,4},{6,5},{7,6},{9,8},{10,9},{11,10},{13,12},{... | collective-permute-start | bytes 1179656 | tf_op jit(solution)/shard_map/ppermute | solution.py:23
  59.8 3.6 %collective-permute-start.14 = (bf16[2,2,64,768]{3,2,1,0:T(8,128)(2,1)S(1)}, bf16[2,2,64,768]{3,2,1,0:T(8,128)(2,1)S(1)}, u32[]{:S(2)}, u32[]{:S(2)}) collective-permute-start(bf16[2,2,64,768]{3,2,1,0:T(8,128)(2,1)S(1)} %pad_maximum_fusion.2), channel_id=1, source_target_pairs={{0,1},{1,2},{2,3},{4,5},{5,6},{6,7},{8,9},{9,10},{10,11},{12,13},{... | collective-permute-start | bytes 1179656 | tf_op jit(solution)/shard_map/ppermute | solution.py:23
  63.5 1.9 %collective-permute-start.15 = (bf16[2,2,64,768]{3,2,1,0:T(8,128)(2,1)S(1)}, bf16[2,2,64,768]{3,2,1,0:T(8,128)(2,1)S(1)}, u32[]{:S(2)}, u32[]{:S(2)}) collective-permute-start(bf16[2,2,64,768]{3,2,1,0:T(8,128)(2,1)S(1)} %pad_maximum_fusion.3), channel_id=1, source_target_pairs={{1,0},{2,1},{3,2},{5,4},{6,5},{7,6},{9,8},{10,9},{11,10},{13,12},{... | collective-permute-start | bytes 1179656 | tf_op jit(solution)/shard_map/ppermute | solution.py:23
  65.4 0.7 copy-done.11
  66.2 29.1 %shard_map.86 = (bf16[16,24,768]{2,1,0:T(8,128)(2,1)}, bf16[16,24,768]{2,1,0:T(8,128)(2,1)}, f32[3,3,2,256]{3,2,1,0:T(2,128)}, f32[3,3,2,256]{3,2,1,0:T(2,128)}, f32[2,6,64,768]{3,2,1,0:T(8,128)}) custom-call(s32[4,5]{1,0:T(4,128)} %pad_add_fusion.1.mark_ref, bf16[2,3,64,768]{3,2,1,0:T(8,128)(2,1)} %get-tuple-element.19.refs_0_, ...), custom_call_target="tpu_custom_call" | custom-call | tf_op jit(solution)/shard_map/pallas_call | solution.py:272
  95.3 3.4 %collective-permute-start.16 = (f32[3,3,2,256]{3,2,1,0:T(2,128)}, f32[3,3,2,256]{3,2,1,0:T(2,128)S(1)}, u32[]{:S(2)}, u32[]{:S(2)}) collective-permute-start(f32[3,3,2,256]{3,2,1,0:T(2,128)} %get-tuple-element.29), channel_id=1, source_target_pairs={{0,4},{4,8},{8,12},{1,5},{5,9},{9,13},{2,6},{6,10},{10,14},{3,7},{... | collective-permute-start | bytes 55304 | tf_op jit(solution)/shard_map/ppermute | solution.py:23
  98.7 0.7 fusion.6
  99.4 0.3 collective-permute-done.16.refs_8_
  99.8 1.3 collective-permute-start.17
  101.1 3.7 %collective-permute-done.17.refs_9_ = f32[3,3,2,256]{3,2,1,0:T(2,128)S(1)} collective-permute-done((f32[3,3,2,256]{3,2,1,0:T(2,128)}, f32[3,3,2,256]{3,2,1,0:T(2,128)S(1)}, u32[]{:S(2)}, u32[]{:S(2)}) %collective-permute-start.17) | collective-permute-done | bytes 18464 | tf_op jit(solution)/shard_map/ppermute | solution.py:23
  104.8 2.1 %collective-permute-start.19 = (f32[3,4,2,256]{3,2,1,0:T(2,128)S(1)}, f32[3,4,2,256]{3,2,1,0:T(2,128)S(1)}, u32[]{:S(2)}, u32[]{:S(2)}) collective-permute-start(f32[3,4,2,256]{3,2,1,0:T(2,128)S(1)} %pad_maximum_fusion.5), channel_id=1, source_target_pairs={{1,0},{2,1},{3,2},{5,4},{6,5},{7,6},{9,8},{10,9},{11,10},{13,12},{... | collective-permute-start | bytes 73736 | tf_op jit(solution)/shard_map/ppermute | solution.py:23
  106.9 5.0 %collective-permute-done.19 = f32[3,4,2,256]{3,2,1,0:T(2,128)S(1)} collective-permute-done((f32[3,4,2,256]{3,2,1,0:T(2,128)S(1)}, f32[3,4,2,256]{3,2,1,0:T(2,128)S(1)}, u32[]{:S(2)}, u32[]{:S(2)}) %collective-permute-start.19) | collective-permute-done | bytes 24608 | tf_op jit(solution)/shard_map/ppermute | solution.py:23
  111.9 2.1 %collective-permute-start.18 = (f32[3,4,2,256]{3,2,1,0:T(2,128)S(1)}, f32[3,4,2,256]{3,2,1,0:T(2,128)S(1)}, u32[]{:S(2)}, u32[]{:S(2)}) collective-permute-start(f32[3,4,2,256]{3,2,1,0:T(2,128)S(1)} %pad_maximum_fusion.4), channel_id=1, source_target_pairs={{0,1},{1,2},{2,3},{4,5},{5,6},{6,7},{8,9},{9,10},{10,11},{12,13},{... | collective-permute-start | bytes 73736 | tf_op jit(solution)/shard_map/ppermute | solution.py:23
  114.0 0.6 fusion.4
  114.6 0.4 collective-permute-done.18
  115.0 0.6 fusion.5
  115.7 0.7 copy-done.4
  116.4 0.1 copy-done.7
  116.6 0.1 copy-done.8
  116.7 0.1 copy-done.9
  116.8 19.6 %shard_map.87 = (bf16[16,24,768]{2,1,0:T(8,128)(2,1)}, bf16[16,24,768]{2,1,0:T(8,128)(2,1)}) custom-call(s32[4,5]{1,0:T(4,128)} %pad_add_fusion.1.mark_ref, bf16[2,3,64,768]{3,2,1,0:T(8,128)(2,1)} %get-tuple-element.19.refs_0_, bf16[2,3,64,768]{3,2,1,0:T(8,128)(2,1)} %get-tuple-element.20.refs_1_, bf16[2,3,64,768]{3,2,1,0:T(8,128)(2,1)} %copy-done, ...), custom_call_target="tpu_custom_call" | custom-call | tf_op jit(solution)/shard_map/pallas_call | solution.py:288
  (47 shorter events, 0.4 us)
Async XLA Ops:
  0.6 22.4 %copy-start.14 = (s32[2,3]{1,0:T(2,128)S(1)}, s32[2,3]{1,0:T(2,128)}, u32[]{:S(2)}) copy-start(s32[2,3]{1,0:T(2,128)} %mark_ref.3) | copy-start | bytes 76
  3.2 34.9 %collective-permute-start.4 = (bf16[2,3,64,768]{3,2,1,0:T(8,128)(2,1)}, bf16[2,3,64,768]{3,2,1,0:T(8,128)(2,1)S(1)}, u32[]{:S(2)}, u32[]{:S(2)}) collective-permute-start(bf16[2,3,64,768]{3,2,1,0:T(8,128)(2,1)} %get-tuple-element.20.refs_1_), channel_id=1, source_target_pairs={{0,4},{4,8},{8,12},{1,5},{5,9},{9,13},{2,6},{6,10},{10,14},{3,7},{... | collective-permute-start | bytes 1769480 | tf_op jit(solution)/shard_map/ppermute | solution.py:23
  8.0 12.7 %collective-permute-start = (s32[1,3]{1,0:T(1,128)S(1)}, s32[1,3]{1,0:T(1,128)S(1)}, u32[]{:S(2)}, u32[]{:S(2)}) collective-permute-start(s32[1,3]{1,0:T(1,128)S(1)} %get-tuple-element.56), channel_id=1, source_target_pairs={{0,4},{4,8},{8,12},{1,5},{5,9},{9,13},{2,6},{6,10},{10,14},{3,7},{... | collective-permute-start | bytes 44 | tf_op jit(solution)/shard_map/ppermute | solution.py:23
  11.2 11.8 %collective-permute-start.1 = (s32[1,3]{1,0:T(1,128)S(1)}, s32[1,3]{1,0:T(1,128)S(1)}, u32[]{:S(2)}, u32[]{:S(2)}) collective-permute-start(s32[1,3]{1,0:T(1,128)S(1)} %get-tuple-element.57), channel_id=1, source_target_pairs={{4,0},{8,4},{12,8},{5,1},{9,5},{13,9},{6,2},{10,6},{14,10},{7,3},{... | collective-permute-start | bytes 44 | tf_op jit(solution)/shard_map/ppermute | solution.py:23
  12.5 26.9 %collective-permute-start.5 = (bf16[2,3,64,768]{3,2,1,0:T(8,128)(2,1)}, bf16[2,3,64,768]{3,2,1,0:T(8,128)(2,1)S(1)}, u32[]{:S(2)}, u32[]{:S(2)}) collective-permute-start(bf16[2,3,64,768]{3,2,1,0:T(8,128)(2,1)} %get-tuple-element.19.refs_0_), channel_id=1, source_target_pairs={{4,0},{8,4},{12,8},{5,1},{9,5},{13,9},{6,2},{10,6},{14,10},{7,3},{... | collective-permute-start | bytes 1769480 | tf_op jit(solution)/shard_map/ppermute | solution.py:23
  13.8 44.0 %collective-permute-start.6 = (bf16[2,2,64,768]{3,2,1,0:T(8,128)(2,1)}, bf16[2,2,64,768]{3,2,1,0:T(8,128)(2,1)S(1)}, u32[]{:S(2)}, u32[]{:S(2)}) collective-permute-start(bf16[2,2,64,768]{3,2,1,0:T(8,128)(2,1)} %get-tuple-element.21), channel_id=1, source_target_pairs={{0,1},{1,2},{2,3},{4,5},{5,6},{6,7},{8,9},{9,10},{10,11},{12,13},{... | collective-permute-start | bytes 1179656 | tf_op jit(solution)/shard_map/ppermute | solution.py:23
  20.7 39.1 %collective-permute-start.7 = (bf16[2,2,64,768]{3,2,1,0:T(8,128)(2,1)}, bf16[2,2,64,768]{3,2,1,0:T(8,128)(2,1)S(1)}, u32[]{:S(2)}, u32[]{:S(2)}) collective-permute-start(bf16[2,2,64,768]{3,2,1,0:T(8,128)(2,1)} %get-tuple-element.22), channel_id=1, source_target_pairs={{1,0},{2,1},{3,2},{5,4},{6,5},{7,6},{9,8},{10,9},{11,10},{13,12},{... | collective-permute-start | bytes 1179656 | tf_op jit(solution)/shard_map/ppermute | solution.py:23
  23.1 4.0 %collective-permute-start.2 = (s32[4,1]{1,0:T(4,128)S(1)}, s32[4,1]{1,0:T(4,128)S(1)}, u32[]{:S(2)}, u32[]{:S(2)}) collective-permute-start(s32[4,1]{1,0:T(4,128)S(1)} %get-tuple-element.54), channel_id=1, source_target_pairs={{0,1},{1,2},{2,3},{4,5},{5,6},{6,7},{8,9},{9,10},{10,11},{12,13},{... | collective-permute-start | bytes 56 | tf_op jit(solution)/shard_map/ppermute | solution.py:23
  27.1 5.4 %collective-permute-start.3 = (s32[4,1]{1,0:T(4,128)S(1)}, s32[4,1]{1,0:T(4,128)S(1)}, u32[]{:S(2)}, u32[]{:S(2)}) collective-permute-start(s32[4,1]{1,0:T(4,128)S(1)} %get-tuple-element.55), channel_id=1, source_target_pairs={{1,0},{2,1},{3,2},{5,4},{6,5},{7,6},{9,8},{10,9},{11,10},{13,12},{... | collective-permute-start | bytes 56 | tf_op jit(solution)/shard_map/ppermute | solution.py:23
  32.5 16.4 %collective-permute-start.10 = (bf16[2,3,64,768]{3,2,1,0:T(8,128)(2,1)}, bf16[2,3,64,768]{3,2,1,0:T(8,128)(2,1)S(1)}, u32[]{:S(2)}, u32[]{:S(2)}) collective-permute-start(bf16[2,3,64,768]{3,2,1,0:T(8,128)(2,1)} %get-tuple-element.24.refs_9_), channel_id=1, source_target_pairs={{0,4},{4,8},{8,12},{1,5},{5,9},{9,13},{2,6},{6,10},{10,14},{3,7},{... | collective-permute-start | bytes 1769480 | tf_op jit(solution)/shard_map/ppermute | solution.py:23
  38.1 19.6 %copy-start.2 = (bf16[2,3,64,768]{3,2,1,0:T(8,128)(2,1)}, bf16[2,3,64,768]{3,2,1,0:T(8,128)(2,1)S(1)}, u32[]{:S(2)}) copy-start(bf16[2,3,64,768]{3,2,1,0:T(8,128)(2,1)S(1)} %collective-permute-done.4.refs_2_) | copy-start | bytes 1769476
  38.1 15.5 %collective-permute-start.11 = (bf16[2,3,64,768]{3,2,1,0:T(8,128)(2,1)}, bf16[2,3,64,768]{3,2,1,0:T(8,128)(2,1)S(1)}, u32[]{:S(2)}, u32[]{:S(2)}) collective-permute-start(bf16[2,3,64,768]{3,2,1,0:T(8,128)(2,1)} %get-tuple-element.23.refs_8_), channel_id=1, source_target_pairs={{4,0},{8,4},{12,8},{5,1},{9,5},{13,9},{6,2},{10,6},{14,10},{7,3},{... | collective-permute-start | bytes 1769480 | tf_op jit(solution)/shard_map/ppermute | solution.py:23
  39.5 18.3 %copy-start.3 = (bf16[2,3,64,768]{3,2,1,0:T(8,128)(2,1)}, bf16[2,3,64,768]{3,2,1,0:T(8,128)(2,1)S(1)}, u32[]{:S(2)}) copy-start(bf16[2,3,64,768]{3,2,1,0:T(8,128)(2,1)S(1)} %collective-permute-done.5.refs_3_) | copy-start | bytes 1769476
  39.5 76.2 %collective-permute-start.12 = (bf16[2,2,64,768]{3,2,1,0:T(8,128)(2,1)}, bf16[2,2,64,768]{3,2,1,0:T(8,128)(2,1)S(1)}, u32[]{:S(2)}, u32[]{:S(2)}) collective-permute-start(bf16[2,2,64,768]{3,2,1,0:T(8,128)(2,1)} %get-tuple-element.27), channel_id=1, source_target_pairs={{0,1},{1,2},{2,3},{4,5},{5,6},{6,7},{8,9},{9,10},{10,11},{12,13},{... | collective-permute-start | bytes 1179656 | tf_op jit(solution)/shard_map/ppermute | solution.py:23
  41.8 16.1 %copy-start.15 = (bf16[2,2,64,768]{3,2,1,0:T(8,128)(2,1)S(1)}, bf16[2,2,64,768]{3,2,1,0:T(8,128)(2,1)}, u32[]{:S(2)}) copy-start(bf16[2,2,64,768]{3,2,1,0:T(8,128)(2,1)} %get-tuple-element.28) | copy-start | bytes 1179652
  48.9 46.4 %copy-start = (bf16[2,3,64,768]{3,2,1,0:T(8,128)(2,1)}, bf16[2,3,64,768]{3,2,1,0:T(8,128)(2,1)S(1)}, u32[]{:S(2)}) copy-start(bf16[2,3,64,768]{3,2,1,0:T(8,128)(2,1)S(1)} %collective-permute-done.10.refs_2_) | copy-start | bytes 1769476
  48.9 14.5 %collective-permute-start.9 = (bf16[2,2,64,768]{3,2,1,0:T(8,128)(2,1)S(1)}, bf16[2,2,64,768]{3,2,1,0:T(8,128)(2,1)S(1)}, u32[]{:S(2)}, u32[]{:S(2)}) collective-permute-start(bf16[2,2,64,768]{3,2,1,0:T(8,128)(2,1)S(1)} %pad_maximum_fusion.1), channel_id=1, source_target_pairs={{1,0},{2,1},{3,2},{5,4},{6,5},{7,6},{9,8},{10,9},{11,10},{13,12},{... | collective-permute-start | bytes 1179656 | tf_op jit(solution)/shard_map/ppermute | solution.py:23
  53.6 41.7 %copy-start.1 = (bf16[2,3,64,768]{3,2,1,0:T(8,128)(2,1)}, bf16[2,3,64,768]{3,2,1,0:T(8,128)(2,1)S(1)}, u32[]{:S(2)}) copy-start(bf16[2,3,64,768]{3,2,1,0:T(8,128)(2,1)S(1)} %collective-permute-done.11.refs_3_) | copy-start | bytes 1769476
  53.6 11.8 %collective-permute-start.8 = (bf16[2,2,64,768]{3,2,1,0:T(8,128)(2,1)S(1)}, bf16[2,2,64,768]{3,2,1,0:T(8,128)(2,1)S(1)}, u32[]{:S(2)}, u32[]{:S(2)}) collective-permute-start(bf16[2,2,64,768]{3,2,1,0:T(8,128)(2,1)S(1)} %pad_maximum_fusion), channel_id=1, source_target_pairs={{0,1},{1,2},{2,3},{4,5},{5,6},{6,7},{8,9},{9,10},{10,11},{12,13},{... | collective-permute-start | bytes 1179656 | tf_op jit(solution)/shard_map/ppermute | solution.py:23
  57.8 7.6 %copy-start.5 = (bf16[2,2,64,768]{3,2,1,0:T(8,128)(2,1)}, bf16[2,2,64,768]{3,2,1,0:T(8,128)(2,1)S(1)}, u32[]{:S(2)}) copy-start(bf16[2,2,64,768]{3,2,1,0:T(8,128)(2,1)S(1)} %collective-permute-done.6.refs_4_) | copy-start | bytes 1179652
  57.8 57.8 %collective-permute-start.13 = (bf16[2,2,64,768]{3,2,1,0:T(8,128)(2,1)S(1)}, bf16[2,2,64,768]{3,2,1,0:T(8,128)(2,1)S(1)}, u32[]{:S(2)}, u32[]{:S(2)}) collective-permute-start(bf16[2,2,64,768]{3,2,1,0:T(8,128)(2,1)S(1)} %copy-done.15), channel_id=1, source_target_pairs={{1,0},{2,1},{3,2},{5,4},{6,5},{7,6},{9,8},{10,9},{11,10},{13,12},{... | collective-permute-start | bytes 1179656 | tf_op jit(solution)/shard_map/ppermute | solution.py:23
  59.8 5.6 %copy-start.6 = (bf16[2,2,64,768]{3,2,1,0:T(8,128)(2,1)}, bf16[2,2,64,768]{3,2,1,0:T(8,128)(2,1)S(1)}, u32[]{:S(2)}) copy-start(bf16[2,2,64,768]{3,2,1,0:T(8,128)(2,1)S(1)} %collective-permute-done.7.refs_5_) | copy-start | bytes 1179652
  59.8 55.9 %collective-permute-start.14 = (bf16[2,2,64,768]{3,2,1,0:T(8,128)(2,1)S(1)}, bf16[2,2,64,768]{3,2,1,0:T(8,128)(2,1)S(1)}, u32[]{:S(2)}, u32[]{:S(2)}) collective-permute-start(bf16[2,2,64,768]{3,2,1,0:T(8,128)(2,1)S(1)} %pad_maximum_fusion.2), channel_id=1, source_target_pairs={{0,1},{1,2},{2,3},{4,5},{5,6},{6,7},{8,9},{9,10},{10,11},{12,13},{... | collective-permute-start | bytes 1179656 | tf_op jit(solution)/shard_map/ppermute | solution.py:23
  63.5 2.0 %copy-start.10 = (bf16[2,2,64,768]{3,2,1,0:T(8,128)(2,1)}, bf16[2,2,64,768]{3,2,1,0:T(8,128)(2,1)S(1)}, u32[]{:S(2)}) copy-start(bf16[2,2,64,768]{3,2,1,0:T(8,128)(2,1)S(1)} %collective-permute-done.9.refs_7_) | copy-start | bytes 1179652
  63.5 52.2 %collective-permute-start.15 = (bf16[2,2,64,768]{3,2,1,0:T(8,128)(2,1)S(1)}, bf16[2,2,64,768]{3,2,1,0:T(8,128)(2,1)S(1)}, u32[]{:S(2)}, u32[]{:S(2)}) collective-permute-start(bf16[2,2,64,768]{3,2,1,0:T(8,128)(2,1)S(1)} %pad_maximum_fusion.3), channel_id=1, source_target_pairs={{1,0},{2,1},{3,2},{5,4},{6,5},{7,6},{9,8},{10,9},{11,10},{13,12},{... | collective-permute-start | bytes 1179656 | tf_op jit(solution)/shard_map/ppermute | solution.py:23
  65.4 0.8 copy-start.11
  95.3 4.4 %collective-permute-start.16 = (f32[3,3,2,256]{3,2,1,0:T(2,128)}, f32[3,3,2,256]{3,2,1,0:T(2,128)S(1)}, u32[]{:S(2)}, u32[]{:S(2)}) collective-permute-start(f32[3,3,2,256]{3,2,1,0:T(2,128)} %get-tuple-element.29), channel_id=1, source_target_pairs={{0,4},{4,8},{8,12},{1,5},{5,9},{9,13},{2,6},{6,10},{10,14},{3,7},{... | collective-permute-start | bytes 55304 | tf_op jit(solution)/shard_map/ppermute | solution.py:23
  99.8 15.9 %copy-start.12 = (f32[3,3,2,256]{3,2,1,0:T(2,128)}, f32[3,3,2,256]{3,2,1,0:T(2,128)S(1)}, u32[]{:S(2)}) copy-start(f32[3,3,2,256]{3,2,1,0:T(2,128)S(1)} %collective-permute-done.16.refs_8_) | copy-start | bytes 55300
  99.8 5.0 %collective-permute-start.17 = (f32[3,3,2,256]{3,2,1,0:T(2,128)}, f32[3,3,2,256]{3,2,1,0:T(2,128)S(1)}, u32[]{:S(2)}, u32[]{:S(2)}) collective-permute-start(f32[3,3,2,256]{3,2,1,0:T(2,128)} %get-tuple-element.30), channel_id=1, source_target_pairs={{4,0},{8,4},{12,8},{5,1},{9,5},{13,9},{6,2},{10,6},{14,10},{7,3},{... | collective-permute-start | bytes 55304 | tf_op jit(solution)/shard_map/ppermute | solution.py:23
  104.7 11.0 %copy-start.13 = (f32[3,3,2,256]{3,2,1,0:T(2,128)}, f32[3,3,2,256]{3,2,1,0:T(2,128)S(1)}, u32[]{:S(2)}) copy-start(f32[3,3,2,256]{3,2,1,0:T(2,128)S(1)} %collective-permute-done.17.refs_9_) | copy-start | bytes 55300
  104.8 7.2 %collective-permute-start.19 = (f32[3,4,2,256]{3,2,1,0:T(2,128)S(1)}, f32[3,4,2,256]{3,2,1,0:T(2,128)S(1)}, u32[]{:S(2)}, u32[]{:S(2)}) collective-permute-start(f32[3,4,2,256]{3,2,1,0:T(2,128)S(1)} %pad_maximum_fusion.5), channel_id=1, source_target_pairs={{1,0},{2,1},{3,2},{5,4},{6,5},{7,6},{9,8},{10,9},{11,10},{13,12},{... | collective-permute-start | bytes 73736 | tf_op jit(solution)/shard_map/ppermute | solution.py:23
  111.9 3.1 %collective-permute-start.18 = (f32[3,4,2,256]{3,2,1,0:T(2,128)S(1)}, f32[3,4,2,256]{3,2,1,0:T(2,128)S(1)}, u32[]{:S(2)}, u32[]{:S(2)}) collective-permute-start(f32[3,4,2,256]{3,2,1,0:T(2,128)S(1)} %pad_maximum_fusion.4), channel_id=1, source_target_pairs={{0,1},{1,2},{2,3},{4,5},{5,6},{6,7},{8,9},{9,10},{10,11},{12,13},{... | collective-permute-start | bytes 73736 | tf_op jit(solution)/shard_map/ppermute | solution.py:23
  115.6 0.8 copy-start.4
  115.6 0.9 copy-start.7
  115.7 1.0 copy-start.8
  115.7 1.1 copy-start.9

commit v2 on v1

v2 whole, which is shorter than its diff:
```python
import jax
import jax.numpy as jnp
from jax import lax
from jax.experimental import pallas as pl
from jax.experimental.pallas import tpu as pltpu
from jax.sharding import PartitionSpec as P

HEAD = 64
TILE = 8
TOKENS = TILE * TILE
LANES = 256
PER = LANES // HEAD
MARKS = 16
SCALE = HEAD ** -0.5
LOG2E = 1.4426950408889634
NEG = -1e30
BIG = 1e30
LIMIT = 56 * 1024 * 1024
VMEM = pl.BlockSpec(memory_space=pltpu.VMEM)
SMEM = pl.BlockSpec(memory_space=pltpu.SMEM)
BF16 = jnp.bfloat16
F32 = jnp.float32


def shift(array, axis, by):
    count = lax.axis_size(axis)
    pairs = [(i, i + by) for i in range(count) if 0 <= i + by < count]
    return lax.ppermute(array, axis, pairs)


def nt(a, b):
    return lax.dot_general(a, b, (((1,), (1,)), ((), ())), preferred_element_type=F32)


def nn(a, b):
    return lax.dot_general(a, b, (((1,), (0,)), ((), ())), preferred_element_type=F32)


def tn(a, b):
    return lax.dot_general(a, b, (((0,), (0,)), ((), ())), preferred_element_type=F32)


def call(body, out_shape, args, marks_first=True, flops=0, exps=0):
    size = sum(array.size * array.dtype.itemsize for array in args)
    return pl.pallas_call(
        body,
        in_specs=[SMEM if marks_first and n == 0 else VMEM for n in range(len(args))],
        out_specs=[VMEM] * len(out_shape),
        out_shape=out_shape,
        compiler_params=pltpu.CompilerParams(vmem_limit_bytes=LIMIT),
        cost_estimate=pl.CostEstimate(flops=flops, transcendentals=exps, bytes_accessed=size),
    )(*args)


def tile_of(ref, a, b):
    block = ref[TILE * a : TILE * (a + 1), TILE * b : TILE * (b + 1), :]
    return block.astype(F32).reshape(TOKENS, block.shape[-1])


def put_tile(ref, a, b, lanes, value):
    shaped = value.reshape(TILE, TILE, value.shape[-1]).astype(ref.dtype)
    ref[TILE * a : TILE * (a + 1), TILE * b : TILE * (b + 1), lanes] = shaped


def rows_of(index):
    return slice(index * TOKENS, (index + 1) * TOKENS)


def mark_row(ref, start, index, lanes):
    return ref[start : start + MARKS, lanes].astype(F32)[index : index + 1]


def pack(first, second, tissue, scaled):
    rows, cols = tissue.shape
    width = first.shape[-1]

    def body(mark_ref, first_ref, second_ref, *row_refs):
        for a in range(rows):
            for b in range(cols):
                mark = mark_ref[a, b].astype(F32)
                for n, ref in enumerate((first_ref, second_ref)):
                    tile = tile_of(ref, a, b)
                    if scaled:
                        tile = tile * (SCALE if n == 0 else mark)
                    row_refs[a][rows_of(n * cols + b), :] = tile.astype(BF16)
            if not scaled:
                which = lax.broadcasted_iota(jnp.int32, (MARKS, width), 0)
                marks = jnp.zeros((MARKS, width), F32)
                for b in range(cols):
                    marks = jnp.where(which == b, mark_ref[a, b].astype(F32), marks)
                row_refs[a][2 * cols * TOKENS :, :] = marks.astype(BF16)

    height = 2 * cols * TOKENS + (0 if scaled else MARKS)
    shape = jax.ShapeDtypeStruct((height, width), BF16)
    return call(body, [shape] * rows, (tissue, first, second))


def pack_sides(own_kv, own_qg, cols):
    rows = len(own_kv)
    width = own_kv[0].shape[1]

    def body(*refs):
        kv, qg, outs = refs[:rows], refs[rows : 2 * rows], refs[2 * rows :]
        for b, out in zip((0, cols - 1), outs):
            for n in range(4):
                src = kv if n < 2 else qg
                for a in range(rows):
                    out[rows_of(n * rows + a), :] = src[a][rows_of((n % 2) * cols + b), :]
            which = lax.broadcasted_iota(jnp.int32, (MARKS, width), 0)
            marks = jnp.zeros((MARKS, width), F32)
            for a in range(rows):
                marks = jnp.where(which == a, mark_row(kv[a], 2 * cols * TOKENS, b, slice(None)), marks)
            out[4 * rows * TOKENS :, :] = marks.astype(BF16)

    shape = jax.ShapeDtypeStruct((4 * rows * TOKENS + MARKS, width), BF16)
    return call(body, [shape] * 2, (*own_kv, *own_qg), marks_first=False)


def pack_corners(above, below, cols, marked):
    width = above.shape[1]

    def body(above_ref, below_ref, *outs):
        for b, out in zip((0, cols - 1), outs):
            for n in range(2):
                for end, ref in enumerate((above_ref, below_ref)):
                    out[rows_of(n * 2 + end), :] = ref[rows_of(n * cols + b), :]
            if marked:
                which = lax.broadcasted_iota(jnp.int32, (MARKS, width), 0)
                marks = jnp.zeros((MARKS, width), F32)
                for end, ref in enumerate((above_ref, below_ref)):
                    marks = jnp.where(which == end, mark_row(ref, 2 * cols * TOKENS, b, slice(None)), marks)
                out[4 * TOKENS :, :] = marks.astype(BF16)

    shape = jax.ShapeDtypeStruct((4 * TOKENS + (MARKS if marked else 0), width), BF16)
    return call(body, [shape] * 2, (above, below), marks_first=False)


def pack_stats(own, above, below, cols):
    rows = len(own)

    def body(*refs):
        sources, outs = refs[: rows + 2], refs[rows + 2 :]
        for b, out in zip((0, cols - 1), outs):
            for n, ref in enumerate(sources):
                out[2 * n : 2 * n + 2, :] = ref[2 * b : 2 * b + 2, :]

    shape = jax.ShapeDtypeStruct((2 * (rows + 2), own[0].shape[1]), F32)
    return call(body, [shape] * 2, (*own, above, below), marks_first=False)


def head_mask():
    row = lax.broadcasted_iota(jnp.int32, (LANES, LANES), 0) // HEAD
    lane = lax.broadcasted_iota(jnp.int32, (LANES, LANES), 1) // HEAD
    return row == lane


def spread(tile, mask):
    return jnp.where(mask, jnp.concatenate([tile] * PER, axis=0), jnp.zeros((), tile.dtype))


def gather_heads(full):
    lane = lax.broadcasted_iota(jnp.int32, (TOKENS, LANES), 1) // HEAD
    out = full[:TOKENS]
    for h in range(1, PER):
        out = jnp.where(lane == h, full[h * TOKENS : (h + 1) * TOKENS], out)
    return out


def fold(x, op):
    return op(x.reshape(x.shape[0] // 8, 8, x.shape[1]), axis=0)


class Block:
    def __init__(self, rows, cols, own, near, lanes):
        self.rows, self.cols, self.own, self.lanes = rows, cols, own, lanes
        self.above, self.below, self.left, self.right, self.corner_left, self.corner_right = near

    def tile(self, n, i, j, side):
        ends = {-1: (self.above, 0), self.rows: (self.below, 1)}
        if 0 <= j < self.cols:
            ref = ends[i][0] if i in ends else self.own[i]
            return ref[rows_of(n * self.cols + j), self.lanes]
        if i in ends:
            ref = self.corner_left if j < 0 else self.corner_right
            return ref[rows_of(n * 2 + ends[i][1]), self.lanes]
        ref = self.left if j < 0 else self.right
        return ref[rows_of((side + n) * self.rows + i), self.lanes]

    def mark(self, marks, i, j):
        ends = {-1: (self.above, 0), self.rows: (self.below, 1)}
        if 0 <= j < self.cols:
            if i not in ends:
                return marks[i, j].astype(F32)
            return mark_row(ends[i][0], 2 * self.cols * TOKENS, j, self.lanes)
        if i in ends:
            ref = self.corner_left if j < 0 else self.corner_right
            return mark_row(ref, 4 * TOKENS, ends[i][1], self.lanes)
        ref = self.left if j < 0 else self.right
        return mark_row(ref, 4 * self.rows * TOKENS, i, self.lanes)


def around(a, b):
    return [(a + i, b + j) for j in (-1, 0, 1) for i in (-1, 0, 1)]


def each_group(width, step):
    def one(g, carry):
        step(pl.ds(pl.multiple_of(g * LANES, LANES), LANES))
        return carry

    lax.fori_loop(0, width // LANES, one, 0)


def forward(rows, cols, width):
    def body(mark_ref, *refs):
        own_kv, near, own_qg = refs[:rows], refs[rows : rows + 6], refs[rows + 6 : 2 * rows + 6]
        att_ref, *stat_refs = refs[2 * rows + 6 :]
        mask = head_mask()

        def step(lanes):
            block = Block(rows, cols, own_kv, near, lanes)
            for a in range(rows):
                for b in range(cols):
                    places = around(a, b)
                    own_mark = mark_ref[a, b].astype(F32)
                    allowed = [
                        None if place == (a, b) else own_mark * block.mark(mark_ref, *place) > 0
                        for place in places
                    ]
                    q = spread(own_qg[a][rows_of(b), lanes], mask)
                    keys = jnp.concatenate([block.tile(0, i, j, 0) for i, j in places], axis=0)
                    values = jnp.concatenate([block.tile(1, i, j, 0) for i, j in places], axis=0)
                    scores = nt(keys, q)
                    top = None
                    for t, ok in enumerate(allowed):
                        high = fold(scores[rows_of(t)], jnp.max)
                        if ok is not None:
                            high = jnp.where(ok, high, NEG)
                        top = high if top is None else jnp.maximum(top, high)
                    top = jnp.max(top, axis=0, keepdims=True) * LOG2E
                    total = jnp.zeros((8, LANES), F32)
                    low = []
                    for t, ok in enumerate(allowed):
                        less = top if ok is None else jnp.where(ok, top, BIG)
                        e = jnp.exp2(scores[rows_of(t)] * LOG2E - less)
                        total = total + fold(e, jnp.sum)
                        low.append(e.astype(BF16))
                    total = jnp.sum(total, axis=0, keepdims=True)
                    inverse = jnp.broadcast_to(own_mark / total, (8, LANES)).T[:, :1]
                    att = gather_heads(tn(jnp.concatenate(low, axis=0), values) * inverse).astype(BF16).astype(F32)
                    put_tile(att_ref, a, b, lanes, att)
                    prod = (own_qg[a][rows_of(cols + b), lanes].astype(F32) * att).T
                    dot = [jnp.sum(prod[rows_of(h)], axis=0, keepdims=True) for h in range(PER)]
                    stat_refs[a][2 * b : 2 * b + 1, lanes] = top + jnp.log2(total)
                    stat_refs[a][2 * b + 1 : 2 * b + 2, lanes] = jnp.concatenate(dot, axis=1)

        each_group(width, step)

    return body


def backward(rows, cols, width):
    def body(mark_ref, *refs):
        own_kv, near, own_qg = refs[:rows], refs[rows : rows + 6], refs[rows + 6 : 2 * rows + 6]
        stat_refs = refs[2 * rows + 6 : 3 * rows + 6]
        gq_ref, sum_ref = refs[3 * rows + 6 :]
        mask = head_mask()
        sum_ref[...] = jnp.zeros(sum_ref.shape, F32)

        def step(lanes):
            block = Block(rows, cols, own_kv, near, lanes)
            for a in range(rows):
                for b in range(cols):
                    places = around(a, b)
                    own_mark = mark_ref[a, b].astype(F32)
                    q = spread(own_qg[a][rows_of(b), lanes], mask)
                    g = spread(own_qg[a][rows_of(cols + b), lanes], mask)
                    keys = jnp.concatenate([block.tile(0, i, j, 0) for i, j in places], axis=0)
                    values = jnp.concatenate([block.tile(1, i, j, 0) for i, j in places], axis=0)
                    level = stat_refs[a][2 * b : 2 * b + 1, lanes]
                    dot = stat_refs[a][2 * b + 1 : 2 * b + 2, lanes]
                    scores, grads = nt(keys, q), nt(values, g)
                    probs, slopes = [], []
                    for t, place in enumerate(places):
                        less = level
                        if place != (a, b):
                            less = jnp.where(own_mark * block.mark(mark_ref, *place) > 0, level, BIG)
                        p = jnp.exp2(scores[rows_of(t)] * LOG2E - less)
                        probs.append(p.astype(BF16))
                        slopes.append((p * (grads[rows_of(t)] - dot)).astype(BF16))
                    gq = gather_heads(tn(jnp.concatenate(slopes, axis=0), keys)) * SCALE
                    put_tile(gq_ref, a, b, lanes, gq)
                    inside = [t for t, (i, j) in enumerate(places) if 0 <= i < rows and 0 <= j < cols]
                    for n, (parts, right) in enumerate(((slopes, q), (probs, g))):
                        part = nn(jnp.concatenate([parts[t] for t in inside], axis=0), right)
                        for u, t in enumerate(inside):
                            i, j = places[t]
                            sum_ref[n, rows_of(i * cols + j), lanes] += part[rows_of(u)]

        each_group(width, step)

    return body


def key_side(rows, cols, width):
    def body(mark_ref, *refs):
        own_kv, near_kv, near_qg = refs[:rows], refs[rows : rows + 6], refs[rows + 6 : rows + 12]
        above_s, below_s, left_s, right_s, sum_ref, gk_ref, gv_ref, acc_ref = refs[rows + 12 :]
        mask = head_mask()
        acc_ref[...] = sum_ref[...]

        def stat_at(i, j, lanes):
            if 0 <= j < cols:
                ref, start = (above_s if i < 0 else below_s), j
            else:
                ref, start = (left_s if j < 0 else right_s), (rows if i < 0 else rows + 1 if i >= rows else i)
            return ref[2 * start : 2 * start + 1, lanes], ref[2 * start + 1 : 2 * start + 2, lanes]

        def step(lanes):
            marks = Block(rows, cols, own_kv, near_kv, lanes)
            queries = Block(rows, cols, None, near_qg, lanes)
            for i in range(-1, rows + 1):
                for j in range(-1, cols + 1):
                    if 0 <= i < rows and 0 <= j < cols:
                        continue
                    places = [(x, y) for x, y in around(i, j) if 0 <= x < rows and 0 <= y < cols]
                    q = spread(queries.tile(0, i, j, 2), mask)
                    g = spread(queries.tile(1, i, j, 2), mask)
                    level, dot = stat_at(i, j, lanes)
                    mark = marks.mark(mark_ref, i, j)
                    keys = jnp.concatenate([marks.tile(0, x, y, 0) for x, y in places], axis=0)
                    values = jnp.concatenate([marks.tile(1, x, y, 0) for x, y in places], axis=0)
                    scores, grads = nt(keys, q), nt(values, g)
                    probs, slopes = [], []
                    for t, (x, y) in enumerate(places):
                        less = jnp.where(mark * mark_ref[x, y].astype(F32) > 0, level, BIG)
                        p = jnp.exp2(scores[rows_of(t)] * LOG2E - less)
                        probs.append(p.astype(BF16))
                        slopes.append((p * (grads[rows_of(t)] - dot)).astype(BF16))
                    for n, (parts, right) in enumerate(((slopes, q), (probs, g))):
                        part = nn(jnp.concatenate(parts, axis=0), right)
                        for t, (x, y) in enumerate(places):
                            acc_ref[n, rows_of(x * cols + y), lanes] += part[rows_of(t)]
            for x in range(rows):
                for y in range(cols):
                    put_tile(gk_ref, x, y, lanes, acc_ref[0, rows_of(x * cols + y), lanes])
                    put_tile(gv_ref, x, y, lanes, acc_ref[1, rows_of(x * cols + y), lanes])

        each_group(width, step)

    return body


def local(query_grid, key_grid, value_grid, out_grad, tissue):
    rows, cols = tissue.shape
    width = query_grid.shape[-1]
    own_kv = pack(key_grid, value_grid, tissue, False)
    above_kv = shift(own_kv[-1], "rows", 1)
    below_kv = shift(own_kv[0], "rows", -1)
    own_qg = pack(query_grid, out_grad, tissue, True)
    above_qg = shift(own_qg[-1], "rows", 1)
    below_qg = shift(own_qg[0], "rows", -1)
    first_side, last_side = pack_sides(own_kv, own_qg, cols)
    left = shift(last_side, "cols", 1)
    right = shift(first_side, "cols", -1)
    first_kv, last_kv = pack_corners(above_kv, below_kv, cols, True)
    near_kv = (above_kv, below_kv, left, right, shift(last_kv, "cols", 1), shift(first_kv, "cols", -1))
    grid_out = jax.ShapeDtypeStruct(query_grid.shape, BF16)
    stat_out = jax.ShapeDtypeStruct((2 * cols, width), F32)
    sum_out = jax.ShapeDtypeStruct((2, rows * cols * TOKENS, width), F32)
    pairs = 9 * rows * cols * TOKENS * TOKENS * width
    attended, *stats = call(
        forward(rows, cols, width), [grid_out] + [stat_out] * rows,
        (tissue, *own_kv, *near_kv, *own_qg), flops=16 * pairs, exps=pairs // HEAD,
    )
    above_s = shift(stats[-1], "rows", 1)
    below_s = shift(stats[0], "rows", -1)
    first_s, last_s = pack_stats(stats, above_s, below_s, cols)
    left_s = shift(last_s, "cols", 1)
    right_s = shift(first_s, "cols", -1)
    first_qg, last_qg = pack_corners(above_qg, below_qg, cols, False)
    near_qg = (above_qg, below_qg, left, right, shift(last_qg, "cols", 1), shift(first_qg, "cols", -1))
    grad_query, sums = call(
        backward(rows, cols, width), [grid_out, sum_out],
        (tissue, *own_kv, *near_kv, *own_qg, *stats), flops=32 * pairs, exps=pairs // HEAD,
    )
    args = (tissue, *own_kv, *near_kv, *near_qg, above_s, below_s, left_s, right_s, sums)
    grad_key, grad_value = pl.pallas_call(
        key_side(rows, cols, width),
        in_specs=[SMEM] + [VMEM] * (len(args) - 1),
        out_specs=[VMEM] * 2,
        out_shape=[grid_out] * 2,
        scratch_shapes=[pltpu.VMEM(sum_out.shape, F32)],
        compiler_params=pltpu.CompilerParams(vmem_limit_bytes=LIMIT),
        cost_estimate=pl.CostEstimate(flops=8 * pairs, transcendentals=pairs // (2 * HEAD), bytes_accessed=1 << 20),
    )(*args)
    return attended, grad_query, grad_key, grad_value


def solution(mesh):
    grid = P(("groups", "rows"), "cols", None)
    return jax.shard_map(
        local,
        mesh=mesh,
        in_specs=(grid, grid, grid, grid, P(("groups", "rows"), "cols")),
        out_specs=(grid, grid, grid, grid),
        check_vma=False,
    )
```

time: 137 us -> 111 us (0.81)
  starting transfers between devices: 52.2 us -> 35 us
  waiting for transfers between devices: 23.5 us -> 16.3 us
  Pallas kernels: 54 us -> 52.2 us
    ppermute x20 -> x14, starting transfers between devices: 52.2 us -> 35 us  [shift(): return lax.ppermute(array, axis, pairs)]
    ppermute x20 -> x14, waiting for transfers between devices: 23.5 us -> 16.3 us  [shift(): return lax.ppermute(array, axis, pairs)]
    unnamed x32 -> x36, local copies, waits for them, and re-layouts: 1.88 us -> 5.28 us
    slice x11 -> x0, local copies, waits for them, and re-layouts: 2.92 us -> none  [the longest x2 0.83 us: local(): lax.slice_in_dim(marks, length - 1, length, axis=dim)]
    pallas_call x4 -> x9, Pallas kernels: 54 us -> 52.2 us  [the longest x8 37.2 us: call(): pl.pallas_call(body, in_specs=[SMEM if marks_first and n == 0 else VMEM f...]
  transfers between devices with their start and end apart: 20 -> 14, of which waited for: 8 -> 3; matrix products, arithmetic and copies ran while one was open for 3% -> 0% of each run, Pallas kernels for 23% -> 27%
where the time goes in v2:
time: 111 us; the launch traced here: 110 us
  Pallas kernels  52.2 us (47%)
  starting transfers between devices  35 us (32%)
  waiting for transfers between devices  16.3 us (15%)
  local copies, waits for them, and re-layouts  5.28 us (5%)
    pallas_call x8, Pallas kernels, call(): pl.pallas_call(body, in_specs=[SMEM if marks_first and n == 0 else VMEM f...  37.2 us
    ppermute x14, starting transfers between devices, shift(): return lax.ppermute(array, axis, pairs)  35 us
    ppermute x14, waiting for transfers between devices, shift(): return lax.ppermute(array, axis, pairs)  16.3 us
    pallas_call x1, Pallas kernels, local(): pl.pallas_call(key_side(rows, cols, width), in_specs=[SMEM] + [VMEM] * (l...  15.1 us
    unnamed x36, local copies, waits for them, and re-layouts  5.28 us
  transfers between devices with their start and end apart: 14, of which 3 were waited for; matrix products, arithmetic and copies ran while one was open for 0% of the time, Pallas kernels for 27%

profile of v2, /device:TPU:1, one launch (start us, length us, event | category | flops | bytes accessed | tf_op | source)
XLA Modules:
  0.0 109.8 jit_solution(16888840704986980215)
XLA Ops:
  0.6 2.3 %shard_map.84 = (bf16[400,768]{1,0:T(8,128)(2,1)}, bf16[400,768]{1,0:T(8,128)(2,1)}) custom-call(s32[2,3]{1,0:T(2,128)} %mark_ref.9, bf16[16,24,768]{2,1,0:T(8,128)(2,1)} %first_ref.2, bf16[16,24,768]{2,1,0:T(8,128)(2,1)} %second_ref.2), custom_call_target="tpu_custom_call" | custom-call | bytes 1179672 | tf_op jit(solution)/shard_map/pallas_call | solution.py:45
  3.0 2.5 %shard_map.85 = (bf16[384,768]{1,0:T(8,128)(2,1)}, bf16[384,768]{1,0:T(8,128)(2,1)}) custom-call(s32[2,3]{1,0:T(2,128)} %mark_ref.9, bf16[16,24,768]{2,1,0:T(8,128)(2,1)} %first_ref.3, bf16[16,24,768]{2,1,0:T(8,128)(2,1)} %second_ref.3), custom_call_target="tpu_custom_call" | custom-call | bytes 1179672 | tf_op jit(solution)/shard_map/pallas_call | solution.py:45
  5.4 3.0 %shard_map.86 = (bf16[528,768]{1,0:T(8,128)(2,1)}, bf16[528,768]{1,0:T(8,128)(2,1)}) custom-call(bf16[400,768]{1,0:T(8,128)(2,1)} %get-tuple-element.23.refs_0_, bf16[400,768]{1,0:T(8,128)(2,1)} %get-tuple-element.24.refs_1_, bf16[384,768]{1,0:T(8,128)(2,1)} %get-tuple-element.25.refs_2_.refs_8_, bf16[384,768]{1,0:T(8,128)(2,1)} %get-tuple-element.26.refs_3_.refs_9_), custom_call_target="tpu_custom_call" | custom-call | bytes 2408448 | tf_op jit(solution)/shard_map/pallas_call | solution.py:45
  8.4 4.5 %collective-permute-start.2 = (bf16[528,768]{1,0:T(8,128)(2,1)}, bf16[528,768]{1,0:T(8,128)(2,1)S(1)}, u32[]{:S(2)}, u32[]{:S(2)}) collective-permute-start(bf16[528,768]{1,0:T(8,128)(2,1)} %get-tuple-element.27), channel_id=1, source_target_pairs={{0,1},{1,2},{2,3},{4,5},{5,6},{6,7},{8,9},{9,10},{10,11},{12,13},{... | collective-permute-start | bytes 2433032 | tf_op jit(solution)/shard_map/ppermute | solution.py:28
  12.9 0.0 copy-done.3
  12.9 3.2 %collective-permute-start = (bf16[400,768]{1,0:T(8,128)(2,1)S(1)}, bf16[400,768]{1,0:T(8,128)(2,1)S(1)}, u32[]{:S(2)}, u32[]{:S(2)}) collective-permute-start(bf16[400,768]{1,0:T(8,128)(2,1)S(1)} %copy-done.3), channel_id=1, source_target_pairs={{0,4},{4,8},{8,12},{1,5},{5,9},{9,13},{2,6},{6,10},{10,14},{3,7},{... | collective-permute-start | bytes 1843208 | tf_op jit(solution)/shard_map/ppermute | solution.py:28
  16.2 0.0 copy-done.2
  16.2 1.3 %collective-permute-start.1 = (bf16[400,768]{1,0:T(8,128)(2,1)S(1)}, bf16[400,768]{1,0:T(8,128)(2,1)S(1)}, u32[]{:S(2)}, u32[]{:S(2)}) collective-permute-start(bf16[400,768]{1,0:T(8,128)(2,1)S(1)} %copy-done.2), channel_id=1, source_target_pairs={{4,0},{8,4},{12,8},{5,1},{9,5},{13,9},{6,2},{10,6},{14,10},{7,3},{... | collective-permute-start | bytes 1843208 | tf_op jit(solution)/shard_map/ppermute | solution.py:28
  17.5 1.9 %collective-permute-start.3 = (bf16[528,768]{1,0:T(8,128)(2,1)}, bf16[528,768]{1,0:T(8,128)(2,1)S(1)}, u32[]{:S(2)}, u32[]{:S(2)}) collective-permute-start(bf16[528,768]{1,0:T(8,128)(2,1)} %get-tuple-element.28), channel_id=1, source_target_pairs={{1,0},{2,1},{3,2},{5,4},{6,5},{7,6},{9,8},{10,9},{11,10},{13,12},{... | collective-permute-start | bytes 2433032 | tf_op jit(solution)/shard_map/ppermute | solution.py:28
  19.4 9.6 %collective-permute-done.above_ref.refs_2_ = bf16[400,768]{1,0:T(8,128)(2,1)S(1)} collective-permute-done((bf16[400,768]{1,0:T(8,128)(2,1)S(1)}, bf16[400,768]{1,0:T(8,128)(2,1)S(1)}, u32[]{:S(2)}, u32[]{:S(2)}) %collective-permute-start) | collective-permute-done | bytes 614432 | tf_op jit(solution)/shard_map/ppermute | solution.py:28
  29.0 4.1 %collective-permute-done.1.below_ref.refs_3_ = bf16[400,768]{1,0:T(8,128)(2,1)S(1)} collective-permute-done((bf16[400,768]{1,0:T(8,128)(2,1)S(1)}, bf16[400,768]{1,0:T(8,128)(2,1)S(1)}, u32[]{:S(2)}, u32[]{:S(2)}) %collective-permute-start.1) | collective-permute-done | bytes 614432 | tf_op jit(solution)/shard_map/ppermute | solution.py:28
  33.2 0.0 copy-done.4
  33.2 0.8 copy-done.5
  34.0 2.2 %shard_map.87 = (bf16[272,768]{1,0:T(8,128)(2,1)}, bf16[272,768]{1,0:T(8,128)(2,1)}) custom-call(bf16[400,768]{1,0:T(8,128)(2,1)} %copy-done.4, bf16[400,768]{1,0:T(8,128)(2,1)} %copy-done.5), custom_call_target="tpu_custom_call" | custom-call | bytes 1228800 | tf_op jit(solution)/shard_map/pallas_call | solution.py:45
  36.2 1.9 %collective-permute-start.4 = (bf16[272,768]{1,0:T(8,128)(2,1)}, bf16[272,768]{1,0:T(8,128)(2,1)S(1)}, u32[]{:S(2)}, u32[]{:S(2)}) collective-permute-start(bf16[272,768]{1,0:T(8,128)(2,1)} %get-tuple-element.29), channel_id=1, source_target_pairs={{0,1},{1,2},{2,3},{4,5},{5,6},{6,7},{8,9},{9,10},{10,11},{12,13},{... | collective-permute-start | bytes 1253384 | tf_op jit(solution)/shard_map/ppermute | solution.py:28
  38.1 2.4 %collective-permute-start.5 = (bf16[272,768]{1,0:T(8,128)(2,1)}, bf16[272,768]{1,0:T(8,128)(2,1)S(1)}, u32[]{:S(2)}, u32[]{:S(2)}) collective-permute-start(bf16[272,768]{1,0:T(8,128)(2,1)} %get-tuple-element.30), channel_id=1, source_target_pairs={{1,0},{2,1},{3,2},{5,4},{6,5},{7,6},{9,8},{10,9},{11,10},{13,12},{... | collective-permute-start | bytes 1253384 | tf_op jit(solution)/shard_map/ppermute | solution.py:28
  40.6 3.2 %collective-permute-start.6 = (bf16[384,768]{1,0:T(8,128)(2,1)S(1)}, bf16[384,768]{1,0:T(8,128)(2,1)S(1)}, u32[]{:S(2)}, u32[]{:S(2)}) collective-permute-start(bf16[384,768]{1,0:T(8,128)(2,1)S(1)} %copy-done.9), channel_id=1, source_target_pairs={{0,4},{4,8},{8,12},{1,5},{5,9},{9,13},{2,6},{6,10},{10,14},{3,7},{... | collective-permute-start | bytes 1769480 | tf_op jit(solution)/shard_map/ppermute | solution.py:28
  43.8 0.0 collective-permute-done.2.refs_4_.refs_10_
  43.8 1.3 %collective-permute-start.7 = (bf16[384,768]{1,0:T(8,128)(2,1)S(1)}, bf16[384,768]{1,0:T(8,128)(2,1)S(1)}, u32[]{:S(2)}, u32[]{:S(2)}) collective-permute-start(bf16[384,768]{1,0:T(8,128)(2,1)S(1)} %copy-done.8), channel_id=1, source_target_pairs={{4,0},{8,4},{12,8},{5,1},{9,5},{13,9},{6,2},{10,6},{14,10},{7,3},{... | collective-permute-start | bytes 1769480 | tf_op jit(solution)/shard_map/ppermute | solution.py:28
  45.1 0.0 collective-permute-done.3.refs_5_.refs_11_
  45.1 0.0 collective-permute-done.4.refs_6_
  45.1 2.5 %collective-permute-done.5.refs_7_ = bf16[272,768]{1,0:T(8,128)(2,1)S(1)} collective-permute-done((bf16[272,768]{1,0:T(8,128)(2,1)}, bf16[272,768]{1,0:T(8,128)(2,1)S(1)}, u32[]{:S(2)}, u32[]{:S(2)}) %collective-permute-start.5) | collective-permute-done | bytes 417824 | tf_op jit(solution)/shard_map/ppermute | solution.py:28
  47.7 0.8 copy-done.11
  48.5 11.0 %shard_map.88 = (bf16[16,24,768]{2,1,0:T(8,128)(2,1)}, f32[6,768]{1,0:T(8,128)}, f32[6,768]{1,0:T(8,128)}) custom-call(s32[2,3]{1,0:T(2,128)} %mark_ref.9, bf16[400,768]{1,0:T(8,128)(2,1)} %get-tuple-element.23.refs_0_, bf16[400,768]{1,0:T(8,128)(2,1)} %get-tuple-element.24.refs_1_, bf16[400,768]{1,0:T(8,128)(2,1)} %copy-done.4, bf16[400,768]{1,0:T(8,128)(2,1)} %copy-done.5, ...), custom_call_target="tpu_custom_call" | custom-call | flops 2717908992 | bytes 6094872 | tf_op jit(solution)/shard_map/pallas_call | solution.py:45
  59.5 3.5 %collective-permute-start.10 = (f32[6,768]{1,0:T(8,128)}, f32[6,768]{1,0:T(8,128)S(1)}, u32[]{:S(2)}, u32[]{:S(2)}) collective-permute-start(f32[6,768]{1,0:T(8,128)} %get-tuple-element.33.refs_11_.refs_1_), channel_id=1, source_target_pairs={{0,4},{4,8},{8,12},{1,5},{5,9},{9,13},{2,6},{6,10},{10,14},{3,7},{... | collective-permute-start | bytes 55304 | tf_op jit(solution)/shard_map/ppermute | solution.py:28
  62.9 1.3 %collective-permute-start.11 = (f32[6,768]{1,0:T(8,128)}, f32[6,768]{1,0:T(8,128)S(1)}, u32[]{:S(2)}, u32[]{:S(2)}) collective-permute-start(f32[6,768]{1,0:T(8,128)} %get-tuple-element.32.refs_10_.refs_0_), channel_id=1, source_target_pairs={{4,0},{8,4},{12,8},{5,1},{9,5},{13,9},{6,2},{10,6},{14,10},{7,3},{... | collective-permute-start | bytes 55304 | tf_op jit(solution)/shard_map/ppermute | solution.py:28
  64.2 0.0 collective-permute-done.6.above_ref.refs_8_
  64.3 0.0 collective-permute-done.7.below_ref.refs_9_
  64.3 0.8 copy-done.6
  65.1 0.8 copy-done.7
  65.9 2.2 %shard_map.90 = (bf16[256,768]{1,0:T(8,128)(2,1)}, bf16[256,768]{1,0:T(8,128)(2,1)}) custom-call(bf16[384,768]{1,0:T(8,128)(2,1)} %copy-done.6, bf16[384,768]{1,0:T(8,128)(2,1)} %copy-done.7), custom_call_target="tpu_custom_call" | custom-call | bytes 1179648 | tf_op jit(solution)/shard_map/pallas_call | solution.py:45
  68.1 3.0 %collective-permute-start.8 = (bf16[256,768]{1,0:T(8,128)(2,1)}, bf16[256,768]{1,0:T(8,128)(2,1)S(1)}, u32[]{:S(2)}, u32[]{:S(2)}) collective-permute-start(bf16[256,768]{1,0:T(8,128)(2,1)} %get-tuple-element.35), channel_id=1, source_target_pairs={{0,1},{1,2},{2,3},{4,5},{5,6},{6,7},{8,9},{9,10},{10,11},{12,13},{... | collective-permute-start | bytes 1179656 | tf_op jit(solution)/shard_map/ppermute | solution.py:28
  71.0 1.9 %collective-permute-start.9 = (bf16[256,768]{1,0:T(8,128)(2,1)}, bf16[256,768]{1,0:T(8,128)(2,1)S(1)}, u32[]{:S(2)}, u32[]{:S(2)}) collective-permute-start(bf16[256,768]{1,0:T(8,128)(2,1)} %get-tuple-element.36), channel_id=1, source_target_pairs={{1,0},{2,1},{3,2},{5,4},{6,5},{7,6},{9,8},{10,9},{11,10},{13,12},{... | collective-permute-start | bytes 1179656 | tf_op jit(solution)/shard_map/ppermute | solution.py:28
  73.0 0.0 collective-permute-done.10.refs_2_.refs_14_
  73.0 0.0 collective-permute-done.11.refs_3_.refs_15_
  73.0 0.6 copy-done.14
  73.6 0.6 copy-done.15
  74.2 1.4 %shard_map.91 = (f32[8,768]{1,0:T(8,128)}, f32[8,768]{1,0:T(8,128)}) custom-call(f32[6,768]{1,0:T(8,128)} %get-tuple-element.32.refs_10_.refs_0_, f32[6,768]{1,0:T(8,128)} %get-tuple-element.33.refs_11_.refs_1_, f32[6,768]{1,0:T(8,128)} %copy-done.14, f32[6,768]{1,0:T(8,128)} %copy-done.15), custom_call_target="tpu_custom_call" | custom-call | bytes 73728 | tf_op jit(solution)/shard_map/pallas_call | solution.py:45
  75.6 3.6 %collective-permute-start.12 = (f32[8,768]{1,0:T(8,128)}, f32[8,768]{1,0:T(8,128)S(1)}, u32[]{:S(2)}, u32[]{:S(2)}) collective-permute-start(f32[8,768]{1,0:T(8,128)} %get-tuple-element.37), channel_id=1, source_target_pairs={{0,1},{1,2},{2,3},{4,5},{5,6},{6,7},{8,9},{9,10},{10,11},{12,13},{... | collective-permute-start | bytes 73736 | tf_op jit(solution)/shard_map/ppermute | solution.py:28
  79.3 1.9 %collective-permute-start.13 = (f32[8,768]{1,0:T(8,128)}, f32[8,768]{1,0:T(8,128)S(1)}, u32[]{:S(2)}, u32[]{:S(2)}) collective-permute-start(f32[8,768]{1,0:T(8,128)} %get-tuple-element.38), channel_id=1, source_target_pairs={{1,0},{2,1},{3,2},{5,4},{6,5},{7,6},{9,8},{10,9},{11,10},{13,12},{... | collective-permute-start | bytes 73736 | tf_op jit(solution)/shard_map/ppermute | solution.py:28
  81.2 12.6 %shard_map.89 = (bf16[16,24,768]{2,1,0:T(8,128)(2,1)}, f32[2,384,768]{2,1,0:T(8,128)}) custom-call(s32[2,3]{1,0:T(2,128)} %mark_ref.9, bf16[400,768]{1,0:T(8,128)(2,1)} %get-tuple-element.23.refs_0_, bf16[400,768]{1,0:T(8,128)(2,1)} %get-tuple-element.24.refs_1_, bf16[400,768]{1,0:T(8,128)(2,1)} %copy-done.4, bf16[400,768]{1,0:T(8,128)(2,1)} %copy-done.5, ...), custom_call_target="tpu_custom_call" | custom-call | flops 5435817984 | bytes 6131736 | tf_op jit(solution)/shard_map/pallas_call | solution.py:45
  93.8 0.0 collective-permute-done.8.refs_12_
  93.8 0.0 collective-permute-done.9.refs_13_
  93.8 0.0 collective-permute-done.12.refs_16_
  93.8 0.0 collective-permute-done.13.refs_17_
  93.8 0.7 copy-done.12
  94.6 0.1 copy-done.13
  94.7 15.1 %shard_map.92 = (bf16[16,24,768]{2,1,0:T(8,128)(2,1)}, bf16[16,24,768]{2,1,0:T(8,128)(2,1)}) custom-call(s32[2,3]{1,0:T(2,128)} %mark_ref.9, bf16[400,768]{1,0:T(8,128)(2,1)} %get-tuple-element.23.refs_0_, bf16[400,768]{1,0:T(8,128)(2,1)} %get-tuple-element.24.refs_1_, bf16[400,768]{1,0:T(8,128)(2,1)} %copy-done.4, bf16[400,768]{1,0:T(8,128)(2,1)} %copy-done.5, ...), custom_call_target="tpu_custom_call" | custom-call | flops 1358954496 | bytes 1048576 | tf_op jit(solution)/shard_map/pallas_call | solution.py:388
  (25 shorter events, 0.0 us)
Async XLA Ops:
  3.0 9.9 %copy-start.3 = (bf16[400,768]{1,0:T(8,128)(2,1)S(1)}, bf16[400,768]{1,0:T(8,128)(2,1)}, u32[]{:S(2)}) copy-start(bf16[400,768]{1,0:T(8,128)(2,1)} %get-tuple-element.24.refs_1_) | copy-start | bytes 1843204
  3.0 13.2 %copy-start.2 = (bf16[400,768]{1,0:T(8,128)(2,1)S(1)}, bf16[400,768]{1,0:T(8,128)(2,1)}, u32[]{:S(2)}) copy-start(bf16[400,768]{1,0:T(8,128)(2,1)} %get-tuple-element.23.refs_0_) | copy-start | bytes 1843204
  5.4 35.1 %copy-start.9 = (bf16[384,768]{1,0:T(8,128)(2,1)S(1)}, bf16[384,768]{1,0:T(8,128)(2,1)}, u32[]{:S(2)}) copy-start(bf16[384,768]{1,0:T(8,128)(2,1)} %get-tuple-element.26.refs_3_.refs_9_) | copy-start | bytes 1769476
  5.4 38.3 %copy-start.8 = (bf16[384,768]{1,0:T(8,128)(2,1)S(1)}, bf16[384,768]{1,0:T(8,128)(2,1)}, u32[]{:S(2)}) copy-start(bf16[384,768]{1,0:T(8,128)(2,1)} %get-tuple-element.25.refs_2_.refs_8_) | copy-start | bytes 1769476
  8.4 35.4 %collective-permute-start.2 = (bf16[528,768]{1,0:T(8,128)(2,1)}, bf16[528,768]{1,0:T(8,128)(2,1)S(1)}, u32[]{:S(2)}, u32[]{:S(2)}) collective-permute-start(bf16[528,768]{1,0:T(8,128)(2,1)} %get-tuple-element.27), channel_id=1, source_target_pairs={{0,1},{1,2},{2,3},{4,5},{5,6},{6,7},{8,9},{9,10},{10,11},{12,13},{... | collective-permute-start | bytes 2433032 | tf_op jit(solution)/shard_map/ppermute | solution.py:28
  12.9 16.1 %collective-permute-start = (bf16[400,768]{1,0:T(8,128)(2,1)S(1)}, bf16[400,768]{1,0:T(8,128)(2,1)S(1)}, u32[]{:S(2)}, u32[]{:S(2)}) collective-permute-start(bf16[400,768]{1,0:T(8,128)(2,1)S(1)} %copy-done.3), channel_id=1, source_target_pairs={{0,4},{4,8},{8,12},{1,5},{5,9},{9,13},{2,6},{6,10},{10,14},{3,7},{... | collective-permute-start | bytes 1843208 | tf_op jit(solution)/shard_map/ppermute | solution.py:28
  16.2 17.0 %collective-permute-start.1 = (bf16[400,768]{1,0:T(8,128)(2,1)S(1)}, bf16[400,768]{1,0:T(8,128)(2,1)S(1)}, u32[]{:S(2)}, u32[]{:S(2)}) collective-permute-start(bf16[400,768]{1,0:T(8,128)(2,1)S(1)} %copy-done.2), channel_id=1, source_target_pairs={{4,0},{8,4},{12,8},{5,1},{9,5},{13,9},{6,2},{10,6},{14,10},{7,3},{... | collective-permute-start | bytes 1843208 | tf_op jit(solution)/shard_map/ppermute | solution.py:28
  17.5 27.6 %collective-permute-start.3 = (bf16[528,768]{1,0:T(8,128)(2,1)}, bf16[528,768]{1,0:T(8,128)(2,1)S(1)}, u32[]{:S(2)}, u32[]{:S(2)}) collective-permute-start(bf16[528,768]{1,0:T(8,128)(2,1)} %get-tuple-element.28), channel_id=1, source_target_pairs={{1,0},{2,1},{3,2},{5,4},{6,5},{7,6},{9,8},{10,9},{11,10},{13,12},{... | collective-permute-start | bytes 2433032 | tf_op jit(solution)/shard_map/ppermute | solution.py:28
  29.0 4.1 %copy-start.4 = (bf16[400,768]{1,0:T(8,128)(2,1)}, bf16[400,768]{1,0:T(8,128)(2,1)S(1)}, u32[]{:S(2)}) copy-start(bf16[400,768]{1,0:T(8,128)(2,1)S(1)} %collective-permute-done.above_ref.refs_2_) | copy-start | bytes 1843204
  33.2 0.8 copy-start.5
  36.2 8.9 %collective-permute-start.4 = (bf16[272,768]{1,0:T(8,128)(2,1)}, bf16[272,768]{1,0:T(8,128)(2,1)S(1)}, u32[]{:S(2)}, u32[]{:S(2)}) collective-permute-start(bf16[272,768]{1,0:T(8,128)(2,1)} %get-tuple-element.29), channel_id=1, source_target_pairs={{0,1},{1,2},{2,3},{4,5},{5,6},{6,7},{8,9},{9,10},{10,11},{12,13},{... | collective-permute-start | bytes 1253384 | tf_op jit(solution)/shard_map/ppermute | solution.py:28
  38.1 9.6 %collective-permute-start.5 = (bf16[272,768]{1,0:T(8,128)(2,1)}, bf16[272,768]{1,0:T(8,128)(2,1)S(1)}, u32[]{:S(2)}, u32[]{:S(2)}) collective-permute-start(bf16[272,768]{1,0:T(8,128)(2,1)} %get-tuple-element.30), channel_id=1, source_target_pairs={{1,0},{2,1},{3,2},{5,4},{6,5},{7,6},{9,8},{10,9},{11,10},{13,12},{... | collective-permute-start | bytes 1253384 | tf_op jit(solution)/shard_map/ppermute | solution.py:28
  40.6 23.7 %collective-permute-start.6 = (bf16[384,768]{1,0:T(8,128)(2,1)S(1)}, bf16[384,768]{1,0:T(8,128)(2,1)S(1)}, u32[]{:S(2)}, u32[]{:S(2)}) collective-permute-start(bf16[384,768]{1,0:T(8,128)(2,1)S(1)} %copy-done.9), channel_id=1, source_target_pairs={{0,4},{4,8},{8,12},{1,5},{5,9},{9,13},{2,6},{6,10},{10,14},{3,7},{... | collective-permute-start | bytes 1769480 | tf_op jit(solution)/shard_map/ppermute | solution.py:28
  43.8 3.9 %copy-start = (bf16[528,768]{1,0:T(8,128)(2,1)}, bf16[528,768]{1,0:T(8,128)(2,1)S(1)}, u32[]{:S(2)}) copy-start(bf16[528,768]{1,0:T(8,128)(2,1)S(1)} %collective-permute-done.2.refs_4_.refs_10_) | copy-start | bytes 2433028
  43.8 20.5 %collective-permute-start.7 = (bf16[384,768]{1,0:T(8,128)(2,1)S(1)}, bf16[384,768]{1,0:T(8,128)(2,1)S(1)}, u32[]{:S(2)}, u32[]{:S(2)}) collective-permute-start(bf16[384,768]{1,0:T(8,128)(2,1)S(1)} %copy-done.8), channel_id=1, source_target_pairs={{4,0},{8,4},{12,8},{5,1},{9,5},{13,9},{6,2},{10,6},{14,10},{7,3},{... | collective-permute-start | bytes 1769480 | tf_op jit(solution)/shard_map/ppermute | solution.py:28
  45.1 2.6 %copy-start.1 = (bf16[528,768]{1,0:T(8,128)(2,1)}, bf16[528,768]{1,0:T(8,128)(2,1)S(1)}, u32[]{:S(2)}) copy-start(bf16[528,768]{1,0:T(8,128)(2,1)S(1)} %collective-permute-done.3.refs_5_.refs_11_) | copy-start | bytes 2433028
  45.1 2.6 %copy-start.10 = (bf16[272,768]{1,0:T(8,128)(2,1)}, bf16[272,768]{1,0:T(8,128)(2,1)S(1)}, u32[]{:S(2)}) copy-start(bf16[272,768]{1,0:T(8,128)(2,1)S(1)} %collective-permute-done.4.refs_6_) | copy-start | bytes 1253380
  47.7 0.8 copy-start.11
  59.5 13.5 %collective-permute-start.10 = (f32[6,768]{1,0:T(8,128)}, f32[6,768]{1,0:T(8,128)S(1)}, u32[]{:S(2)}, u32[]{:S(2)}) collective-permute-start(f32[6,768]{1,0:T(8,128)} %get-tuple-element.33.refs_11_.refs_1_), channel_id=1, source_target_pairs={{0,4},{4,8},{8,12},{1,5},{5,9},{9,13},{2,6},{6,10},{10,14},{3,7},{... | collective-permute-start | bytes 55304 | tf_op jit(solution)/shard_map/ppermute | solution.py:28
  62.9 10.1 %collective-permute-start.11 = (f32[6,768]{1,0:T(8,128)}, f32[6,768]{1,0:T(8,128)S(1)}, u32[]{:S(2)}, u32[]{:S(2)}) collective-permute-start(f32[6,768]{1,0:T(8,128)} %get-tuple-element.32.refs_10_.refs_0_), channel_id=1, source_target_pairs={{4,0},{8,4},{12,8},{5,1},{9,5},{13,9},{6,2},{10,6},{14,10},{7,3},{... | collective-permute-start | bytes 55304 | tf_op jit(solution)/shard_map/ppermute | solution.py:28
  64.2 0.8 copy-start.6
  65.1 0.8 copy-start.7
  68.1 25.7 %collective-permute-start.8 = (bf16[256,768]{1,0:T(8,128)(2,1)}, bf16[256,768]{1,0:T(8,128)(2,1)S(1)}, u32[]{:S(2)}, u32[]{:S(2)}) collective-permute-start(bf16[256,768]{1,0:T(8,128)(2,1)} %get-tuple-element.35), channel_id=1, source_target_pairs={{0,1},{1,2},{2,3},{4,5},{5,6},{6,7},{8,9},{9,10},{10,11},{12,13},{... | collective-permute-start | bytes 1179656 | tf_op jit(solution)/shard_map/ppermute | solution.py:28
  71.0 22.7 %collective-permute-start.9 = (bf16[256,768]{1,0:T(8,128)(2,1)}, bf16[256,768]{1,0:T(8,128)(2,1)S(1)}, u32[]{:S(2)}, u32[]{:S(2)}) collective-permute-start(bf16[256,768]{1,0:T(8,128)(2,1)} %get-tuple-element.36), channel_id=1, source_target_pairs={{1,0},{2,1},{3,2},{5,4},{6,5},{7,6},{9,8},{10,9},{11,10},{13,12},{... | collective-permute-start | bytes 1179656 | tf_op jit(solution)/shard_map/ppermute | solution.py:28
  73.0 0.6 copy-start.14
  73.6 0.6 copy-start.15
  75.6 18.2 %collective-permute-start.12 = (f32[8,768]{1,0:T(8,128)}, f32[8,768]{1,0:T(8,128)S(1)}, u32[]{:S(2)}, u32[]{:S(2)}) collective-permute-start(f32[8,768]{1,0:T(8,128)} %get-tuple-element.37), channel_id=1, source_target_pairs={{0,1},{1,2},{2,3},{4,5},{5,6},{6,7},{8,9},{9,10},{10,11},{12,13},{... | collective-permute-start | bytes 73736 | tf_op jit(solution)/shard_map/ppermute | solution.py:28
  79.3 14.6 %collective-permute-start.13 = (f32[8,768]{1,0:T(8,128)}, f32[8,768]{1,0:T(8,128)S(1)}, u32[]{:S(2)}, u32[]{:S(2)}) collective-permute-start(f32[8,768]{1,0:T(8,128)} %get-tuple-element.38), channel_id=1, source_target_pairs={{1,0},{2,1},{3,2},{5,4},{6,5},{7,6},{9,8},{10,9},{11,10},{13,12},{... | collective-permute-start | bytes 73736 | tf_op jit(solution)/shard_map/ppermute | solution.py:28
  93.8 0.8 copy-start.12
  93.8 0.9 copy-start.13
  93.8 0.9 copy-start.16
  93.8 0.8 copy-start.17

commit v3 on v2

v3 whole, which is shorter than its diff:
```python
import jax
import jax.numpy as jnp
from jax import lax
from jax.experimental import pallas as pl
from jax.experimental.pallas import tpu as pltpu
from jax.sharding import PartitionSpec as P

HEAD = 64
TILE = 8
TOKENS = TILE * TILE
LANES = 256
PER = LANES // HEAD
MARKS = 16
SCALE = HEAD ** -0.5
LOG2E = 1.4426950408889634
NEG = -1e30
BIG = 1e30
LIMIT = 20 * 1024 * 1024
VMEM = pl.BlockSpec(memory_space=pltpu.VMEM)
SMEM = pl.BlockSpec(memory_space=pltpu.SMEM)
BF16 = jnp.bfloat16
F32 = jnp.float32


def shift(array, axis, by):
    count = lax.axis_size(axis)
    pairs = [(i, i + by) for i in range(count) if 0 <= i + by < count]
    return lax.ppermute(array, axis, pairs)


def nt(a, b):
    return lax.dot_general(a, b, (((1,), (1,)), ((), ())), preferred_element_type=F32)


def nn(a, b):
    return lax.dot_general(a, b, (((1,), (0,)), ((), ())), preferred_element_type=F32)


def tn(a, b):
    return lax.dot_general(a, b, (((0,), (0,)), ((), ())), preferred_element_type=F32)


def call(body, out_shape, args, marks_first=True, flops=0, exps=0):
    size = sum(array.size * array.dtype.itemsize for array in args)
    return pl.pallas_call(
        body,
        in_specs=[SMEM if marks_first and n == 0 else VMEM for n in range(len(args))],
        out_specs=[VMEM] * len(out_shape),
        out_shape=out_shape,
        compiler_params=pltpu.CompilerParams(vmem_limit_bytes=LIMIT),
        cost_estimate=pl.CostEstimate(flops=flops, transcendentals=exps, bytes_accessed=size),
    )(*args)


def tile_of(ref, a, b):
    block = ref[TILE * a : TILE * (a + 1), TILE * b : TILE * (b + 1), :]
    return block.astype(F32).reshape(TOKENS, block.shape[-1])


def put_tile(ref, a, b, lanes, value):
    shaped = value.reshape(TILE, TILE, value.shape[-1]).astype(ref.dtype)
    ref[TILE * a : TILE * (a + 1), TILE * b : TILE * (b + 1), lanes] = shaped


def rows_of(index):
    return slice(index * TOKENS, (index + 1) * TOKENS)


def mark_row(ref, start, index, lanes):
    return ref[start : start + MARKS, lanes].astype(F32)[index : index + 1]


def write_marks(out, start, marks, width):
    which = lax.broadcasted_iota(jnp.int32, (MARKS, width), 0)
    rows = jnp.zeros((MARKS, width), F32)
    for n, mark in enumerate(marks):
        rows = jnp.where(which == n, mark, rows)
    out[start : start + MARKS, :] = rows.astype(BF16)


def pack(grids, tissue):
    rows, cols = tissue.shape
    width = grids[0].shape[-1]

    def body(mark_ref, *refs):
        sources, refs = refs[:4], refs[4:]
        kv_refs, qg_refs, side_refs = refs[:rows], refs[rows : 2 * rows], refs[2 * rows : 2 * rows + 2]
        grid_refs, sems = refs[2 * rows + 2 : 2 * rows + 6], refs[2 * rows + 6]

        def copies(a):
            span = slice(TILE * a, TILE * (a + 1))
            return [
                pltpu.make_async_copy(source.at[span], ref.at[span], sems.at[a, n])
                for n, (source, ref) in enumerate(zip(sources, grid_refs))
            ]

        for a in range(rows):
            for copy in copies(a):
                copy.start()
        for a in range(rows):
            for copy in copies(a):
                copy.wait()
            marks = [mark_ref[a, b].astype(F32) for b in range(cols)]
            for n, ref in enumerate(grid_refs):
                out = (kv_refs if n < 2 else qg_refs)[a]
                for b in range(cols):
                    tile = tile_of(ref, a, b)
                    if n >= 2:
                        tile = tile * (SCALE if n == 2 else marks[b])
                    tile = tile.astype(BF16)
                    out[rows_of(n % 2 * cols + b), :] = tile
                    for end, side in zip((0, cols - 1), side_refs):
                        if b == end:
                            side[rows_of(n * rows + a), :] = tile
            write_marks(kv_refs[a], 2 * cols * TOKENS, marks, width)
        for b, side in zip((0, cols - 1), side_refs):
            write_marks(side, 4 * rows * TOKENS, [mark_ref[a, b].astype(F32) for a in range(rows)], width)

    shapes = [2 * cols * TOKENS + MARKS] * rows + [2 * cols * TOKENS] * rows + [4 * rows * TOKENS + MARKS] * 2
    shapes = [jax.ShapeDtypeStruct((height, width), BF16) for height in shapes]
    outs = pl.pallas_call(
        body,
        in_specs=[SMEM] + [pl.BlockSpec(memory_space=pltpu.HBM)] * 4,
        out_specs=[VMEM] * len(shapes),
        out_shape=shapes,
        scratch_shapes=[pltpu.VMEM(grid.shape, grid.dtype) for grid in grids] + [pltpu.SemaphoreType.DMA((rows, 4))],
        compiler_params=pltpu.CompilerParams(vmem_limit_bytes=LIMIT),
        cost_estimate=pl.CostEstimate(flops=0, transcendentals=0, bytes_accessed=1 << 20),
    )(tissue, *(pltpu.with_memory_space_constraint(grid, pltpu.HBM) for grid in grids))
    return outs[:rows], outs[rows : 2 * rows], outs[2 * rows :]


def pack_corners(above, below, cols):
    width = above.shape[1]

    def body(above_ref, below_ref, *outs):
        for b, out in zip((0, cols - 1), outs):
            for n in range(2):
                for end, ref in enumerate((above_ref, below_ref)):
                    out[rows_of(n * 2 + end), :] = ref[rows_of(n * cols + b), :]
            ends = [mark_row(ref, 2 * cols * TOKENS, b, slice(None)) for ref in (above_ref, below_ref)]
            write_marks(out, 4 * TOKENS, ends, width)

    shape = jax.ShapeDtypeStruct((4 * TOKENS + MARKS, width), BF16)
    return call(body, [shape] * 2, (above, below), marks_first=False)


def pieces(x):
    out = []
    for _ in range(3):
        out.append(x.astype(BF16))
        x = x - out[-1].astype(F32)
    return out


def pack_queries(stats, above_s, below_s, above_qg, below_qg, cols):
    rows = len(stats)
    width = above_s.shape[1]
    height = -(-6 * (rows + 2) // MARKS) * MARKS

    def body(*refs):
        stat_refs, ends, outs = refs[: rows + 2], refs[rows + 2 : rows + 4], refs[rows + 4 :]
        for b, out in zip((0, cols - 1), outs):
            for n in range(2):
                for end, ref in enumerate(ends):
                    out[rows_of(n * 2 + end), :] = ref[rows_of(n * cols + b), :]
            parts = pieces(jnp.concatenate([ref[2 * b : 2 * b + 2, :] for ref in stat_refs], axis=0))
            parts = [part.astype(F32) for part in parts]
            rest = height - 6 * (rows + 2)
            if rest:
                parts.append(jnp.zeros((rest, width), F32))
            out[4 * TOKENS :, :] = jnp.concatenate(parts, axis=0).astype(BF16)

    shape = jax.ShapeDtypeStruct((4 * TOKENS + height, width), BF16)
    return call(body, [shape] * 2, (*stats, above_s, below_s, above_qg, below_qg), marks_first=False)


def head_mask():
    row = lax.broadcasted_iota(jnp.int32, (LANES, LANES), 0) // HEAD
    lane = lax.broadcasted_iota(jnp.int32, (LANES, LANES), 1) // HEAD
    return row == lane


def spread(tile, mask):
    return jnp.where(mask, jnp.concatenate([tile] * PER, axis=0), jnp.zeros((), tile.dtype))


def gather_heads(full):
    lane = lax.broadcasted_iota(jnp.int32, (TOKENS, LANES), 1) // HEAD
    out = full[:TOKENS]
    for h in range(1, PER):
        out = jnp.where(lane == h, full[h * TOKENS : (h + 1) * TOKENS], out)
    return out


def fold(x, op):
    return op(x.reshape(x.shape[0] // 8, 8, x.shape[1]), axis=0)


class Block:
    def __init__(self, rows, cols, own, near, lanes):
        self.rows, self.cols, self.own, self.lanes = rows, cols, own, lanes
        self.above, self.below, self.left, self.right, self.corner_left, self.corner_right = near

    def tile(self, n, i, j, side):
        ends = {-1: (self.above, 0), self.rows: (self.below, 1)}
        if 0 <= j < self.cols:
            ref = ends[i][0] if i in ends else self.own[i]
            return ref[rows_of(n * self.cols + j), self.lanes]
        if i in ends:
            ref = self.corner_left if j < 0 else self.corner_right
            return ref[rows_of(n * 2 + ends[i][1]), self.lanes]
        ref = self.left if j < 0 else self.right
        return ref[rows_of((side + n) * self.rows + i), self.lanes]

    def mark(self, marks, i, j):
        ends = {-1: (self.above, 0), self.rows: (self.below, 1)}
        if 0 <= j < self.cols:
            if i not in ends:
                return marks[i, j].astype(F32)
            return mark_row(ends[i][0], 2 * self.cols * TOKENS, j, self.lanes)
        if i in ends:
            ref = self.corner_left if j < 0 else self.corner_right
            return mark_row(ref, 4 * TOKENS, ends[i][1], self.lanes)
        ref = self.left if j < 0 else self.right
        return mark_row(ref, 4 * self.rows * TOKENS, i, self.lanes)


def drive(programs):
    active = list(programs)
    while active:
        active = [program for program in active if next(program, True) is None]


def around(a, b):
    return [(a + i, b + j) for j in (-1, 0, 1) for i in (-1, 0, 1)]


def each_group(width, step):
    def one(g, carry):
        step(pl.ds(pl.multiple_of(g * LANES, LANES), LANES))
        return carry

    lax.fori_loop(0, width // LANES, one, 0)


def columns(first, second):
    rows = jnp.concatenate(
        [part.astype(F32) for row in (first, second) for part in pieces(row) + [jnp.zeros_like(row)] * 5], axis=0
    )
    index = lax.broadcasted_iota(jnp.int32, (MARKS, LANES), 0) // 8
    lane = lax.broadcasted_iota(jnp.int32, (MARKS, LANES), 1) // 128
    full = tn(rows.astype(BF16), jnp.where(index == lane, 1.0, 0.0).astype(BF16))
    return [
        gather_heads(jnp.concatenate([full[:, 128 * n : 128 * (n + 1)]] * (LANES // 128), axis=1)) for n in range(2)
    ]


def softmax_part(scores, allowed, top):
    for t, ok in enumerate(allowed):
        high = fold(scores[rows_of(t)], jnp.max)
        if ok is not None:
            high = jnp.where(ok, high, NEG)
        high = high * LOG2E
        top = high if top is None else jnp.maximum(top, high)
    return jnp.max(top, axis=0, keepdims=True)


def exponentials(scores, allowed, top):
    total = jnp.zeros((8, LANES), F32)
    low = []
    for t, ok in enumerate(allowed):
        less = top if ok is None else jnp.where(ok, top, BIG)
        e = jnp.exp2(scores[rows_of(t)] * LOG2E - less)
        total = total + fold(e, jnp.sum)
        low.append(e.astype(BF16))
    return jnp.concatenate(low, axis=0), jnp.sum(total, axis=0, keepdims=True)


def split_places(a, b, rows, cols):
    inside = [(i, j) for i, j in around(a, b) if 0 <= i < rows and 0 <= j < cols]
    return inside, [place for place in around(a, b) if place not in inside]


def forward_own(rows, cols, width):
    def body(mark_ref, *refs):
        own_kv, own_qg = refs[:rows], refs[rows : 2 * rows]
        part_ref, level_ref = refs[2 * rows :]
        mask = head_mask()

        def tile(block, lanes, a, b):
            places, _ = split_places(a, b, rows, cols)
            allowed = [None if place == (a, b) else mark_ref[a, b] * mark_ref[place] > 0 for place in places]
            q = spread(own_qg[a][rows_of(b), lanes], mask)
            scores = nt(jnp.concatenate([block.tile(0, i, j, 0) for i, j in places], axis=0), q)
            yield
            top = softmax_part(scores, allowed, None)
            yield
            low, total = exponentials(scores, allowed, top)
            yield
            full = tn(low, jnp.concatenate([block.tile(1, i, j, 0) for i, j in places], axis=0))
            yield
            index = a * cols + b
            part_ref[rows_of(index), lanes] = gather_heads(full)
            level_ref[2 * index : 2 * index + 1, lanes] = top
            level_ref[2 * index + 1 : 2 * index + 2, lanes] = total

        def step(lanes):
            block = Block(rows, cols, own_kv, (None,) * 6, lanes)
            drive(tile(block, lanes, a, b) for a in range(rows) for b in range(cols))

        each_group(width, step)

    return body


def forward(rows, cols, width):
    def body(mark_ref, *refs):
        own_kv, near, own_qg = refs[:rows], refs[rows : rows + 6], refs[rows + 6 : 2 * rows + 6]
        part_ref, level_ref, att_ref, *stat_refs = refs[2 * rows + 6 :]
        mask = head_mask()

        def tile(block, lanes, a, b):
            _, places = split_places(a, b, rows, cols)
            index = a * cols + b
            own_mark = mark_ref[a, b].astype(F32)
            allowed = [own_mark * block.mark(mark_ref, *place) > 0 for place in places]
            q = spread(own_qg[a][rows_of(b), lanes], mask)
            scores = nt(jnp.concatenate([block.tile(0, i, j, 0) for i, j in places], axis=0), q)
            yield
            first = level_ref[2 * index : 2 * index + 1, lanes]
            top = softmax_part(scores, allowed, jnp.broadcast_to(first, (8, LANES)))
            yield
            low, total = exponentials(scores, allowed, top)
            less = jnp.exp2(first - top)
            total = total + less * level_ref[2 * index + 1 : 2 * index + 2, lanes]
            yield
            full = tn(low, jnp.concatenate([block.tile(1, i, j, 0) for i, j in places], axis=0))
            inverse = own_mark / total
            near_by, own_by = columns(inverse, inverse * less)
            yield
            att = (gather_heads(full) * near_by + part_ref[rows_of(index), lanes] * own_by).astype(BF16).astype(F32)
            put_tile(att_ref, a, b, lanes, att)
            prod = (own_qg[a][rows_of(cols + b), lanes].astype(F32) * att).T
            dot = [jnp.sum(prod[rows_of(h)], axis=0, keepdims=True) for h in range(PER)]
            stat_refs[a][2 * b : 2 * b + 1, lanes] = top + jnp.log2(total)
            stat_refs[a][2 * b + 1 : 2 * b + 2, lanes] = jnp.concatenate(dot, axis=1)

        def step(lanes):
            block = Block(rows, cols, own_kv, near, lanes)
            drive(tile(block, lanes, a, b) for a in range(rows) for b in range(cols))

        each_group(width, step)

    return body


def backward(rows, cols, width, a):
    def body(mark_ref, *refs):
        all_refs = refs
        own_kv, near, own_qg = refs[:rows], refs[rows : rows + 6], refs[rows + 6 : 2 * rows + 6]
        stat_ref, refs = refs[2 * rows + 6], refs[2 * rows + 7 + (2 if a else 0) :]
        before_ref = None if a == 0 else all_refs[2 * rows + 8]
        gq_ref, sum_ref, out_ref, sem = refs
        mask = head_mask()
        sum_ref[...] = jnp.zeros(sum_ref.shape, F32) if a == 0 else before_ref[...]

        def tile(block, lanes, b):
            places = around(a, b)
            own_mark = mark_ref[a, b].astype(F32)
            q = spread(own_qg[a][rows_of(b), lanes], mask)
            g = spread(own_qg[a][rows_of(cols + b), lanes], mask)
            keys = jnp.concatenate([block.tile(0, i, j, 0) for i, j in places], axis=0)
            values = jnp.concatenate([block.tile(1, i, j, 0) for i, j in places], axis=0)
            level = stat_ref[2 * b : 2 * b + 1, lanes]
            dot = stat_ref[2 * b + 1 : 2 * b + 2, lanes]
            scores, grads = nt(keys, q), nt(values, g)
            yield
            probs, slopes = [], []
            for t, place in enumerate(places):
                less = level
                if place != (a, b):
                    less = jnp.where(own_mark * block.mark(mark_ref, *place) > 0, level, BIG)
                p = jnp.exp2(scores[rows_of(t)] * LOG2E - less)
                probs.append(p.astype(BF16))
                slopes.append((p * (grads[rows_of(t)] - dot)).astype(BF16))
            yield
            gq = gather_heads(tn(jnp.concatenate(slopes, axis=0), keys)) * SCALE
            put_tile(out_ref, 0, b, lanes, gq)
            inside = [t for t, (i, j) in enumerate(places) if 0 <= i < rows and 0 <= j < cols]
            for n, (parts, right) in enumerate(((slopes, q), (probs, g))):
                part = nn(jnp.concatenate([parts[t] for t in inside], axis=0), right)
                for u, t in enumerate(inside):
                    i, j = places[t]
                    sum_ref[n, rows_of(i * cols + j), lanes] += part[rows_of(u)]

        def step(lanes):
            block = Block(rows, cols, own_kv, near, lanes)
            drive(tile(block, lanes, b) for b in range(cols))

        each_group(width, step)
        copy = pltpu.make_async_copy(out_ref, gq_ref.at[TILE * a : TILE * (a + 1)], sem)
        copy.start()
        copy.wait()

    return body


def key_side(rows, cols, width):
    def body(mark_ref, *refs):
        own_kv, near_kv, near_qg = refs[:rows], refs[rows : rows + 6], refs[rows + 6 : rows + 12]
        above_s, below_s, sum_ref, gk_ref, gv_ref, acc_ref = refs[rows + 12 :]
        mask = head_mask()
        acc_ref[...] = sum_ref[...]

        def stat_at(i, j, lanes):
            if 0 <= j < cols:
                ref = above_s if i < 0 else below_s
                return ref[2 * j : 2 * j + 1, lanes], ref[2 * j + 1 : 2 * j + 2, lanes]
            ref = near_qg[4 if j < 0 else 5]
            parts = ref[4 * TOKENS :, lanes].astype(F32)
            count = 2 * (rows + 2)
            stats = parts[:count] + parts[count : 2 * count] + parts[2 * count : 3 * count]
            n = rows if i < 0 else rows + 1 if i >= rows else i
            return stats[2 * n : 2 * n + 1], stats[2 * n + 1 : 2 * n + 2]

        def tile(marks, queries, lanes, i, j):
            places = [(x, y) for x, y in around(i, j) if 0 <= x < rows and 0 <= y < cols]
            q = spread(queries.tile(0, i, j, 2), mask)
            g = spread(queries.tile(1, i, j, 2), mask)
            level, dot = stat_at(i, j, lanes)
            mark = marks.mark(mark_ref, i, j)
            keys = jnp.concatenate([marks.tile(0, x, y, 0) for x, y in places], axis=0)
            values = jnp.concatenate([marks.tile(1, x, y, 0) for x, y in places], axis=0)
            scores, grads = nt(keys, q), nt(values, g)
            yield
            probs, slopes = [], []
            for t, (x, y) in enumerate(places):
                less = jnp.where(mark * mark_ref[x, y].astype(F32) > 0, level, BIG)
                p = jnp.exp2(scores[rows_of(t)] * LOG2E - less)
                probs.append(p.astype(BF16))
                slopes.append((p * (grads[rows_of(t)] - dot)).astype(BF16))
            yield
            for n, (parts, right) in enumerate(((slopes, q), (probs, g))):
                part = nn(jnp.concatenate(parts, axis=0), right)
                for t, (x, y) in enumerate(places):
                    acc_ref[n, rows_of(x * cols + y), lanes] += part[rows_of(t)]

        def step(lanes):
            marks = Block(rows, cols, own_kv, near_kv, lanes)
            queries = Block(rows, cols, None, near_qg, lanes)
            outside = [
                (i, j) for i in range(-1, rows + 1) for j in range(-1, cols + 1)
                if not (0 <= i < rows and 0 <= j < cols)
            ]
            drive(tile(marks, queries, lanes, i, j) for i, j in outside)
            for x in range(rows):
                for y in range(cols):
                    put_tile(gk_ref, x, y, lanes, acc_ref[0, rows_of(x * cols + y), lanes])
                    put_tile(gv_ref, x, y, lanes, acc_ref[1, rows_of(x * cols + y), lanes])

        each_group(width, step)

    return body


def local(query_grid, key_grid, value_grid, out_grad, tissue):
    rows, cols = tissue.shape
    width = query_grid.shape[-1]
    own_kv, own_qg, (first_side, last_side) = pack((key_grid, value_grid, query_grid, out_grad), tissue)
    above_kv = shift(own_kv[-1], "rows", 1)
    below_kv = shift(own_kv[0], "rows", -1)
    grid_out = jax.ShapeDtypeStruct(query_grid.shape, BF16)
    stat_out = jax.ShapeDtypeStruct((2 * cols, width), F32)
    sum_out = jax.ShapeDtypeStruct((2, rows * cols * TOKENS, width), F32)
    part_out = jax.ShapeDtypeStruct((rows * cols * TOKENS, width), F32)
    level_out = jax.ShapeDtypeStruct((2 * rows * cols, width), F32)
    pairs = 9 * rows * cols * TOKENS * TOKENS * width
    part, level = call(
        forward_own(rows, cols, width), [part_out, level_out], (tissue, *own_kv, *own_qg),
        flops=8 * pairs, exps=pairs // (2 * HEAD),
    )
    first_side, last_side, *sent_qg, level = lax.optimization_barrier((first_side, last_side, own_qg[0], own_qg[-1], level))
    left = shift(last_side, "cols", 1)
    right = shift(first_side, "cols", -1)
    above_qg = shift(sent_qg[1], "rows", 1)
    below_qg = shift(sent_qg[0], "rows", -1)
    first_kv, last_kv = pack_corners(above_kv, below_kv, cols)
    near_kv = (above_kv, below_kv, left, right, shift(last_kv, "cols", 1), shift(first_kv, "cols", -1))
    attended, *stats = call(
        forward(rows, cols, width), [grid_out] + [stat_out] * rows,
        (tissue, *own_kv, *near_kv, *own_qg, part, level), flops=8 * pairs, exps=pairs // (2 * HEAD),
    )
    above_s = shift(stats[-1], "rows", 1)
    below_s = shift(stats[0], "rows", -1)
    query_parts = None
    for a in range(rows):
        args = (tissue, *own_kv, *near_kv, *own_qg, stats[a]) + (query_parts or ())
        query_parts = tuple(pl.pallas_call(
            backward(rows, cols, width, a),
            in_specs=[SMEM] + [VMEM] * (2 * rows + 7) + ([pl.BlockSpec(memory_space=pl.ANY), VMEM] if a else []),
            out_specs=[pl.BlockSpec(memory_space=pl.ANY), VMEM],
            out_shape=[grid_out, sum_out],
            scratch_shapes=[pltpu.VMEM((TILE,) + grid_out.shape[1:], BF16), pltpu.SemaphoreType.DMA],
            input_output_aliases={2 * rows + 8: 0} if a else {},
            compiler_params=pltpu.CompilerParams(vmem_limit_bytes=LIMIT),
            cost_estimate=pl.CostEstimate(flops=16 * pairs, transcendentals=pairs // (2 * HEAD), bytes_accessed=1 << 20),
        )(*args))
        if a == 0:
            above_s, below_s, sums = lax.optimization_barrier((above_s, below_s, query_parts[1]))
            query_parts = (query_parts[0], sums)
            first_q, last_q = pack_queries(stats, above_s, below_s, above_qg, below_qg, cols)
            near_qg = (above_qg, below_qg, left, right, shift(last_q, "cols", 1), shift(first_q, "cols", -1))
    grad_query, sums = query_parts
    args = (tissue, *own_kv, *near_kv, *near_qg, above_s, below_s, sums)
    grad_key, grad_value = pl.pallas_call(
        key_side(rows, cols, width),
        in_specs=[SMEM] + [VMEM] * (len(args) - 1),
        out_specs=[VMEM] * 2,
        out_shape=[grid_out] * 2,
        scratch_shapes=[pltpu.VMEM(sum_out.shape, F32)],
        compiler_params=pltpu.CompilerParams(vmem_limit_bytes=LIMIT),
        cost_estimate=pl.CostEstimate(flops=8 * pairs, transcendentals=pairs // (2 * HEAD), bytes_accessed=1 << 20),
    )(*args)
    return attended, grad_query, grad_key, grad_value


def solution(mesh):
    grid = P(("groups", "rows"), "cols", None)
    return jax.shard_map(
        local,
        mesh=mesh,
        in_specs=(grid, grid, grid, grid, P(("groups", "rows"), "cols")),
        out_specs=(grid, grid, grid, grid),
        check_vma=False,
    )
```

time: 111 us -> 74 us (0.67)
  Pallas kernels: 52.2 us -> 29.7 us
  waiting for transfers between devices: 16.3 us -> 10.8 us
  local copies, waits for them, and re-layouts: 5.28 us -> 0.68 us
  starting transfers between devices: 35 us -> 31.3 us
    pallas_call x8 -> x4, Pallas kernels: 37.2 us -> 8.98 us  [call(): pl.pallas_call(body, in_specs=[SMEM if marks_first and n == 0 else VMEM f...]
    pallas_call x0 -> x3, Pallas kernels: none -> 13.2 us  [the longest x2 10.9 us: local(): pl.pallas_call(backward(rows, cols, width, a), in_specs=[SMEM] + [VMEM] *...]
    pallas_call x1, Pallas kernels: 15.1 us -> 7.51 us  [local(): pl.pallas_call(key_side(rows, cols, width), in_specs=[SMEM] + [VMEM] * (l...]
    ppermute x14 -> x12, waiting for transfers between devices: 16.3 us -> 10.8 us  [shift(): return lax.ppermute(array, axis, pairs)]
    unnamed x36 -> x4, local copies, waits for them, and re-layouts: 5.28 us -> 0.68 us
    ppermute x14 -> x12, starting transfers between devices: 35 us -> 31.3 us  [shift(): return lax.ppermute(array, axis, pairs)]
  transfers between devices with their start and end apart: 14 -> 12, of which waited for: 3 -> 4; matrix products, arithmetic and copies ran while one was open for 0% -> 0% of each run, Pallas kernels for 27% -> 27%
where the time goes in v3:
time: 74 us; the launch traced here: 73.3 us
  starting transfers between devices  31.3 us (42%)
  Pallas kernels  29.7 us (40%)
  waiting for transfers between devices  10.8 us (15%)
  between operations  0.85 us (1%)
    ppermute x12, starting transfers between devices, shift(): return lax.ppermute(array, axis, pairs)  31.3 us
    pallas_call x2, Pallas kernels, local(): pl.pallas_call(backward(rows, cols, width, a), in_specs=[SMEM] + [VMEM] *...  10.9 us
    ppermute x12, waiting for transfers between devices, shift(): return lax.ppermute(array, axis, pairs)  10.8 us
    pallas_call x4, Pallas kernels, call(): pl.pallas_call(body, in_specs=[SMEM if marks_first and n == 0 else VMEM f...  8.98 us
    pallas_call x1, Pallas kernels, local(): pl.pallas_call(key_side(rows, cols, width), in_specs=[SMEM] + [VMEM] * (l...  7.51 us
    pallas_call x1, Pallas kernels, pack(): pl.pallas_call(body, in_specs=[SMEM] + [pl.BlockSpec(memory_space=pltpu.H...  2.36 us
  transfers between devices with their start and end apart: 12, of which 4 were waited for; matrix products, arithmetic and copies ran while one was open for 0% of the time, Pallas kernels for 27%

profile of v3, /device:TPU:1, one launch (start us, length us, event | category | flops | bytes accessed | tf_op | source)
XLA Modules:
  0.0 73.3 jit_solution(7386122849302015016)
XLA Ops:
  0.6 0.0 copy-start
  0.6 0.7 copy-done
  1.3 0.0 copy-start.1
  1.3 2.4 %shard_map.84 = (bf16[400,768]{1,0:T(8,128)(2,1)S(1)}, bf16[400,768]{1,0:T(8,128)(2,1)S(1)}, bf16[384,768]{1,0:T(8,128)(2,1)S(1)}, bf16[384,768]{1,0:T(8,128)(2,...) custom-call(s32[2,3]{1,0:T(2,128)S(1)} %copy-done, bf16[16,24,768]{2,1,0:T(8,128)(2,1)} %refs_0_.1, ...), custom_call_target="tpu_custom_call" | custom-call | bytes 1048576 | tf_op jit(solution)/shard_map/pallas_call | solution.py:121
  3.7 4.1 %collective-permute-start = (bf16[400,768]{1,0:T(8,128)(2,1)S(1)}, bf16[400,768]{1,0:T(8,128)(2,1)S(1)}, u32[]{:S(2)}, u32[]{:S(2)}) collective-permute-start(bf16[400,768]{1,0:T(8,128)(2,1)S(1)} %get-tuple-element.34.refs_1_), channel_id=1, source_target_pairs={{0,4},{4,8},{8,12},{1,5},{5,9},{9,13},{2,6},{6,10},{10,14},{3,7},{... | collective-permute-start | bytes 1843208 | tf_op jit(solution)/shard_map/ppermute | solution.py:28
  7.8 1.3 %collective-permute-start.1 = (bf16[400,768]{1,0:T(8,128)(2,1)S(1)}, bf16[400,768]{1,0:T(8,128)(2,1)S(1)}, u32[]{:S(2)}, u32[]{:S(2)}) collective-permute-start(bf16[400,768]{1,0:T(8,128)(2,1)S(1)} %get-tuple-element.33.refs_0_), channel_id=1, source_target_pairs={{4,0},{8,4},{12,8},{5,1},{9,5},{13,9},{6,2},{10,6},{14,10},{7,3},{... | collective-permute-start | bytes 1843208 | tf_op jit(solution)/shard_map/ppermute | solution.py:28
  9.1 0.0 copy-done.1
  9.1 3.5 %shard_map.85 = (f32[384,768]{1,0:T(8,128)S(1)}, f32[12,768]{1,0:T(8,128)S(1)}) custom-call(s32[2,3]{1,0:T(2,128)S(1)} %copy-done.1, bf16[400,768]{1,0:T(8,128)(2,1)S(1)} %get-tuple-element.33.refs_0_, bf16[400,768]{1,0:T(8,128)(2,1)S(1)} %get-tuple-element.34.refs_1_, bf16[384,768]{1,0:T(8,128)(2,1)S(1)} %get-tuple-element.54.refs_2_.refs_8_, ...), custom_call_target="tpu_custom_call" | custom-call | flops 1358954496 | bytes 2408472 | tf_op jit(solution)/shard_map/pallas_call | solution.py:45
  12.5 4.0 %collective-permute-start.2 = (bf16[528,768]{1,0:T(8,128)(2,1)S(1)}, bf16[528,768]{1,0:T(8,128)(2,1)S(1)}, u32[]{:S(2)}, u32[]{:S(2)}) collective-permute-start(bf16[528,768]{1,0:T(8,128)(2,1)S(1)} %get-tuple-element.40), channel_id=1, source_target_pairs={{0,1},{1,2},{2,3},{4,5},{5,6},{6,7},{8,9},{9,10},{10,11},{12,13},{... | collective-permute-start | bytes 2433032 | tf_op jit(solution)/shard_map/ppermute | solution.py:28
  16.5 1.9 %collective-permute-start.3 = (bf16[528,768]{1,0:T(8,128)(2,1)S(1)}, bf16[528,768]{1,0:T(8,128)(2,1)S(1)}, u32[]{:S(2)}, u32[]{:S(2)}) collective-permute-start(bf16[528,768]{1,0:T(8,128)(2,1)S(1)} %get-tuple-element.41), channel_id=1, source_target_pairs={{1,0},{2,1},{3,2},{5,4},{6,5},{7,6},{9,8},{10,9},{11,10},{13,12},{... | collective-permute-start | bytes 2433032 | tf_op jit(solution)/shard_map/ppermute | solution.py:28
  18.4 1.8 %collective-permute-done.above_ref.refs_2_ = bf16[400,768]{1,0:T(8,128)(2,1)S(1)} collective-permute-done((bf16[400,768]{1,0:T(8,128)(2,1)S(1)}, bf16[400,768]{1,0:T(8,128)(2,1)S(1)}, u32[]{:S(2)}, u32[]{:S(2)}) %collective-permute-start) | collective-permute-done | bytes 614432 | tf_op jit(solution)/shard_map/ppermute | solution.py:28
  20.2 3.8 %collective-permute-done.1.below_ref.refs_3_ = bf16[400,768]{1,0:T(8,128)(2,1)S(1)} collective-permute-done((bf16[400,768]{1,0:T(8,128)(2,1)S(1)}, bf16[400,768]{1,0:T(8,128)(2,1)S(1)}, u32[]{:S(2)}, u32[]{:S(2)}) %collective-permute-start.1) | collective-permute-done | bytes 614432 | tf_op jit(solution)/shard_map/ppermute | solution.py:28
  24.1 0.1 shard_map.86
  24.1 4.9 %collective-permute-start.4 = (bf16[272,768]{1,0:T(8,128)(2,1)S(1)}, bf16[272,768]{1,0:T(8,128)(2,1)S(1)}, u32[]{:S(2)}, u32[]{:S(2)}) collective-permute-start(bf16[272,768]{1,0:T(8,128)(2,1)S(1)} %get-tuple-element.42), channel_id=1, source_target_pairs={{0,1},{1,2},{2,3},{4,5},{5,6},{6,7},{8,9},{9,10},{10,11},{12,13},{... | collective-permute-start | bytes 1253384 | tf_op jit(solution)/shard_map/ppermute | solution.py:28
  29.0 1.9 %collective-permute-start.5 = (bf16[272,768]{1,0:T(8,128)(2,1)S(1)}, bf16[272,768]{1,0:T(8,128)(2,1)S(1)}, u32[]{:S(2)}, u32[]{:S(2)}) collective-permute-start(bf16[272,768]{1,0:T(8,128)(2,1)S(1)} %get-tuple-element.43), channel_id=1, source_target_pairs={{1,0},{2,1},{3,2},{5,4},{6,5},{7,6},{9,8},{10,9},{11,10},{13,12},{... | collective-permute-start | bytes 1253384 | tf_op jit(solution)/shard_map/ppermute | solution.py:28
  30.9 3.2 %collective-permute-start.8 = (bf16[384,768]{1,0:T(8,128)(2,1)S(1)}, bf16[384,768]{1,0:T(8,128)(2,1)S(1)}, u32[]{:S(2)}, u32[]{:S(2)}) collective-permute-start(bf16[384,768]{1,0:T(8,128)(2,1)S(1)} %get-tuple-element.53.refs_3_.refs_9_), channel_id=1, source_target_pairs={{0,4},{4,8},{8,12},{1,5},{5,9},{9,13},{2,6},{6,10},{10,14},{3,7},{... | collective-permute-start | bytes 1769480 | tf_op jit(solution)/shard_map/ppermute | solution.py:28
  34.1 0.0 collective-permute-done.2.refs_4_.refs_10_
  34.1 1.3 %collective-permute-start.9 = (bf16[384,768]{1,0:T(8,128)(2,1)S(1)}, bf16[384,768]{1,0:T(8,128)(2,1)S(1)}, u32[]{:S(2)}, u32[]{:S(2)}) collective-permute-start(bf16[384,768]{1,0:T(8,128)(2,1)S(1)} %get-tuple-element.54.refs_2_.refs_8_), channel_id=1, source_target_pairs={{4,0},{8,4},{12,8},{5,1},{9,5},{13,9},{6,2},{10,6},{14,10},{7,3},{... | collective-permute-start | bytes 1769480 | tf_op jit(solution)/shard_map/ppermute | solution.py:28
  35.4 0.0 collective-permute-done.3.refs_5_.refs_11_
  35.5 0.0 collective-permute-done.4.refs_6_
  35.5 3.2 %collective-permute-done.5.refs_7_ = bf16[272,768]{1,0:T(8,128)(2,1)S(1)} collective-permute-done((bf16[272,768]{1,0:T(8,128)(2,1)S(1)}, bf16[272,768]{1,0:T(8,128)(2,1)S(1)}, u32[]{:S(2)}, u32[]{:S(2)}) %collective-permute-start.5) | collective-permute-done | bytes 417824 | tf_op jit(solution)/shard_map/ppermute | solution.py:28
  38.6 5.4 %shard_map.87 = (bf16[16,24,768]{2,1,0:T(8,128)(2,1)}, f32[6,768]{1,0:T(8,128)S(1)}, f32[6,768]{1,0:T(8,128)S(1)}) custom-call(s32[2,3]{1,0:T(2,128)S(1)} %copy-done.1, bf16[400,768]{1,0:T(8,128)(2,1)S(1)} %get-tuple-element.33.refs_0_, bf16[400,768]{1,0:T(8,128)(2,1)S(1)} %get-tuple-element.34.refs_1_, ...), custom_call_target="tpu_custom_call" | custom-call | flops 1358954496 | bytes 7311384 | tf_op jit(solution)/shard_map/pallas_call | solution.py:45
  44.0 3.1 %collective-permute-start.6 = (f32[6,768]{1,0:T(8,128)S(1)}, f32[6,768]{1,0:T(8,128)S(1)}, u32[]{:S(2)}, u32[]{:S(2)}) collective-permute-start(f32[6,768]{1,0:T(8,128)S(1)} %get-tuple-element.47.refs_10_.refs_1_), channel_id=1, source_target_pairs={{0,4},{4,8},{8,12},{1,5},{5,9},{9,13},{2,6},{6,10},{10,14},{3,7},{... | collective-permute-start | bytes 55304 | tf_op jit(solution)/shard_map/ppermute | solution.py:28
  47.2 1.3 %collective-permute-start.7 = (f32[6,768]{1,0:T(8,128)S(1)}, f32[6,768]{1,0:T(8,128)S(1)}, u32[]{:S(2)}, u32[]{:S(2)}) collective-permute-start(f32[6,768]{1,0:T(8,128)S(1)} %get-tuple-element.48.refs_10_.refs_0_), channel_id=1, source_target_pairs={{4,0},{8,4},{12,8},{5,1},{9,5},{13,9},{6,2},{10,6},{14,10},{7,3},{... | collective-permute-start | bytes 55304 | tf_op jit(solution)/shard_map/ppermute | solution.py:28
  48.5 5.4 %shard_map.88 = (bf16[16,24,768]{2,1,0:T(8,128)(2,1)}, f32[2,384,768]{2,1,0:T(8,128)S(1)}) custom-call(s32[2,3]{1,0:T(2,128)S(1)} %copy-done.1, bf16[400,768]{1,0:T(8,128)(2,1)S(1)} %get-tuple-element.33.refs_0_, bf16[400,768]{1,0:T(8,128)(2,1)S(1)} %get-tuple-element.34.refs_1_, bf16[400,768]{1,0:T(8,128)(2,1)S(1)} %collective-permute-done.above_ref.refs_2_, ...), custom_call_target="tpu_custom_call" | custom-call | flops 2717908992 | bytes 1048576 | tf_op jit(solution)/shard_map/pallas_call | solution.py:499
  53.9 0.0 collective-permute-done.6.refs_2_.refs_14_
  53.9 0.0 collective-permute-done.7.refs_3_.refs_15_
  54.0 0.0 collective-permute-done.8.refs_4_.refs_8_
  54.0 0.0 collective-permute-done.9.refs_5_.refs_9_
  54.0 0.1 shard_map.90
  54.1 2.1 %collective-permute-start.10 = (bf16[288,768]{1,0:T(8,128)(2,1)S(1)}, bf16[288,768]{1,0:T(8,128)(2,1)S(1)}, u32[]{:S(2)}, u32[]{:S(2)}) collective-permute-start(bf16[288,768]{1,0:T(8,128)(2,1)S(1)} %get-tuple-element.57), channel_id=1, source_target_pairs={{0,1},{1,2},{2,3},{4,5},{5,6},{6,7},{8,9},{9,10},{10,11},{12,13},{... | collective-permute-start | bytes 1327112 | tf_op jit(solution)/shard_map/ppermute | solution.py:28
  56.2 2.2 %collective-permute-start.11 = (bf16[288,768]{1,0:T(8,128)(2,1)S(1)}, bf16[288,768]{1,0:T(8,128)(2,1)S(1)}, u32[]{:S(2)}, u32[]{:S(2)}) collective-permute-start(bf16[288,768]{1,0:T(8,128)(2,1)S(1)} %get-tuple-element.58), channel_id=1, source_target_pairs={{1,0},{2,1},{3,2},{5,4},{6,5},{7,6},{9,8},{10,9},{11,10},{13,12},{... | collective-permute-start | bytes 1327112 | tf_op jit(solution)/shard_map/ppermute | solution.py:28
  58.4 5.4 %shard_map.89 = (bf16[16,24,768]{2,1,0:T(8,128)(2,1)}, f32[2,384,768]{2,1,0:T(8,128)S(1)}) custom-call(s32[2,3]{1,0:T(2,128)S(1)} %copy-done.1, bf16[400,768]{1,0:T(8,128)(2,1)S(1)} %get-tuple-element.33.refs_0_, bf16[400,768]{1,0:T(8,128)(2,1)S(1)} %get-tuple-element.34.refs_1_, ...), custom_call_target="tpu_custom_call", output_to_operand_aliasing={{0}: (12, {})} | custom-call | flops 2717908992 | bytes 1048576 | tf_op jit(solution)/shard_map/pallas_call | solution.py:499
  63.9 0.0 collective-permute-done.10.refs_12_
  63.9 1.9 %collective-permute-done.11.refs_13_ = bf16[288,768]{1,0:T(8,128)(2,1)S(1)} collective-permute-done((bf16[288,768]{1,0:T(8,128)(2,1)S(1)}, bf16[288,768]{1,0:T(8,128)(2,1)S(1)}, u32[]{:S(2)}, u32[]{:S(2)}) %collective-permute-start.11) | collective-permute-done | bytes 442400 | tf_op jit(solution)/shard_map/ppermute | solution.py:28
  65.8 7.5 %shard_map.91 = (bf16[16,24,768]{2,1,0:T(8,128)(2,1)}, bf16[16,24,768]{2,1,0:T(8,128)(2,1)}) custom-call(s32[2,3]{1,0:T(2,128)S(1)} %copy-done.1, bf16[400,768]{1,0:T(8,128)(2,1)S(1)} %get-tuple-element.33.refs_0_, bf16[400,768]{1,0:T(8,128)(2,1)S(1)} %get-tuple-element.34.refs_1_, bf16[400,768]{1,0:T(8,128)(2,1)S(1)} %collective-permute-done.above_ref.refs_2_, ...), custom_call_target="tpu_custom_call" | custom-call | flops 1358954496 | bytes 1048576 | tf_op jit(solution)/shard_map/pallas_call | solution.py:516
Async XLA Ops:
  0.6 0.7 copy-start
  1.3 7.7 %copy-start.1 = (s32[2,3]{1,0:T(2,128)S(1)}, s32[2,3]{1,0:T(2,128)}, u32[]{:S(2)}) copy-start(s32[2,3]{1,0:T(2,128)} %mark_ref.11) | copy-start | bytes 76
  3.7 16.5 %collective-permute-start = (bf16[400,768]{1,0:T(8,128)(2,1)S(1)}, bf16[400,768]{1,0:T(8,128)(2,1)S(1)}, u32[]{:S(2)}, u32[]{:S(2)}) collective-permute-start(bf16[400,768]{1,0:T(8,128)(2,1)S(1)} %get-tuple-element.34.refs_1_), channel_id=1, source_target_pairs={{0,4},{4,8},{8,12},{1,5},{5,9},{9,13},{2,6},{6,10},{10,14},{3,7},{... | collective-permute-start | bytes 1843208 | tf_op jit(solution)/shard_map/ppermute | solution.py:28
  7.8 16.3 %collective-permute-start.1 = (bf16[400,768]{1,0:T(8,128)(2,1)S(1)}, bf16[400,768]{1,0:T(8,128)(2,1)S(1)}, u32[]{:S(2)}, u32[]{:S(2)}) collective-permute-start(bf16[400,768]{1,0:T(8,128)(2,1)S(1)} %get-tuple-element.33.refs_0_), channel_id=1, source_target_pairs={{4,0},{8,4},{12,8},{5,1},{9,5},{13,9},{6,2},{10,6},{14,10},{7,3},{... | collective-permute-start | bytes 1843208 | tf_op jit(solution)/shard_map/ppermute | solution.py:28
  12.5 21.6 %collective-permute-start.2 = (bf16[528,768]{1,0:T(8,128)(2,1)S(1)}, bf16[528,768]{1,0:T(8,128)(2,1)S(1)}, u32[]{:S(2)}, u32[]{:S(2)}) collective-permute-start(bf16[528,768]{1,0:T(8,128)(2,1)S(1)} %get-tuple-element.40), channel_id=1, source_target_pairs={{0,1},{1,2},{2,3},{4,5},{5,6},{6,7},{8,9},{9,10},{10,11},{12,13},{... | collective-permute-start | bytes 2433032 | tf_op jit(solution)/shard_map/ppermute | solution.py:28
  16.5 18.9 %collective-permute-start.3 = (bf16[528,768]{1,0:T(8,128)(2,1)S(1)}, bf16[528,768]{1,0:T(8,128)(2,1)S(1)}, u32[]{:S(2)}, u32[]{:S(2)}) collective-permute-start(bf16[528,768]{1,0:T(8,128)(2,1)S(1)} %get-tuple-element.41), channel_id=1, source_target_pairs={{1,0},{2,1},{3,2},{5,4},{6,5},{7,6},{9,8},{10,9},{11,10},{13,12},{... | collective-permute-start | bytes 2433032 | tf_op jit(solution)/shard_map/ppermute | solution.py:28
  24.1 11.3 %collective-permute-start.4 = (bf16[272,768]{1,0:T(8,128)(2,1)S(1)}, bf16[272,768]{1,0:T(8,128)(2,1)S(1)}, u32[]{:S(2)}, u32[]{:S(2)}) collective-permute-start(bf16[272,768]{1,0:T(8,128)(2,1)S(1)} %get-tuple-element.42), channel_id=1, source_target_pairs={{0,1},{1,2},{2,3},{4,5},{5,6},{6,7},{8,9},{9,10},{10,11},{12,13},{... | collective-permute-start | bytes 1253384 | tf_op jit(solution)/shard_map/ppermute | solution.py:28
  29.0 9.7 %collective-permute-start.5 = (bf16[272,768]{1,0:T(8,128)(2,1)S(1)}, bf16[272,768]{1,0:T(8,128)(2,1)S(1)}, u32[]{:S(2)}, u32[]{:S(2)}) collective-permute-start(bf16[272,768]{1,0:T(8,128)(2,1)S(1)} %get-tuple-element.43), channel_id=1, source_target_pairs={{1,0},{2,1},{3,2},{5,4},{6,5},{7,6},{9,8},{10,9},{11,10},{13,12},{... | collective-permute-start | bytes 1253384 | tf_op jit(solution)/shard_map/ppermute | solution.py:28
  30.9 23.0 %collective-permute-start.8 = (bf16[384,768]{1,0:T(8,128)(2,1)S(1)}, bf16[384,768]{1,0:T(8,128)(2,1)S(1)}, u32[]{:S(2)}, u32[]{:S(2)}) collective-permute-start(bf16[384,768]{1,0:T(8,128)(2,1)S(1)} %get-tuple-element.53.refs_3_.refs_9_), channel_id=1, source_target_pairs={{0,4},{4,8},{8,12},{1,5},{5,9},{9,13},{2,6},{6,10},{10,14},{3,7},{... | collective-permute-start | bytes 1769480 | tf_op jit(solution)/shard_map/ppermute | solution.py:28
  34.1 19.8 %collective-permute-start.9 = (bf16[384,768]{1,0:T(8,128)(2,1)S(1)}, bf16[384,768]{1,0:T(8,128)(2,1)S(1)}, u32[]{:S(2)}, u32[]{:S(2)}) collective-permute-start(bf16[384,768]{1,0:T(8,128)(2,1)S(1)} %get-tuple-element.54.refs_2_.refs_8_), channel_id=1, source_target_pairs={{4,0},{8,4},{12,8},{5,1},{9,5},{13,9},{6,2},{10,6},{14,10},{7,3},{... | collective-permute-start | bytes 1769480 | tf_op jit(solution)/shard_map/ppermute | solution.py:28
  44.0 9.9 %collective-permute-start.6 = (f32[6,768]{1,0:T(8,128)S(1)}, f32[6,768]{1,0:T(8,128)S(1)}, u32[]{:S(2)}, u32[]{:S(2)}) collective-permute-start(f32[6,768]{1,0:T(8,128)S(1)} %get-tuple-element.47.refs_10_.refs_1_), channel_id=1, source_target_pairs={{0,4},{4,8},{8,12},{1,5},{5,9},{9,13},{2,6},{6,10},{10,14},{3,7},{... | collective-permute-start | bytes 55304 | tf_op jit(solution)/shard_map/ppermute | solution.py:28
  47.2 6.8 %collective-permute-start.7 = (f32[6,768]{1,0:T(8,128)S(1)}, f32[6,768]{1,0:T(8,128)S(1)}, u32[]{:S(2)}, u32[]{:S(2)}) collective-permute-start(f32[6,768]{1,0:T(8,128)S(1)} %get-tuple-element.48.refs_10_.refs_0_), channel_id=1, source_target_pairs={{4,0},{8,4},{12,8},{5,1},{9,5},{13,9},{6,2},{10,6},{14,10},{7,3},{... | collective-permute-start | bytes 55304 | tf_op jit(solution)/shard_map/ppermute | solution.py:28
  54.1 9.8 %collective-permute-start.10 = (bf16[288,768]{1,0:T(8,128)(2,1)S(1)}, bf16[288,768]{1,0:T(8,128)(2,1)S(1)}, u32[]{:S(2)}, u32[]{:S(2)}) collective-permute-start(bf16[288,768]{1,0:T(8,128)(2,1)S(1)} %get-tuple-element.57), channel_id=1, source_target_pairs={{0,1},{1,2},{2,3},{4,5},{5,6},{6,7},{8,9},{9,10},{10,11},{12,13},{... | collective-permute-start | bytes 1327112 | tf_op jit(solution)/shard_map/ppermute | solution.py:28
  56.2 9.6 %collective-permute-start.11 = (bf16[288,768]{1,0:T(8,128)(2,1)S(1)}, bf16[288,768]{1,0:T(8,128)(2,1)S(1)}, u32[]{:S(2)}, u32[]{:S(2)}) collective-permute-start(bf16[288,768]{1,0:T(8,128)(2,1)S(1)} %get-tuple-element.58), channel_id=1, source_target_pairs={{1,0},{2,1},{3,2},{5,4},{6,5},{7,6},{9,8},{10,9},{11,10},{13,12},{... | collective-permute-start | bytes 1327112 | tf_op jit(solution)/shard_map/ppermute | solution.py:28

commit v4 on v3

--- a/solution.py
+++ b/solution.py
@@ -87,32 +87,32 @@
         kv_refs, qg_refs, side_refs = refs[:rows], refs[rows : 2 * rows], refs[2 * rows : 2 * rows + 2]
         grid_refs, sems = refs[2 * rows + 2 : 2 * rows + 6], refs[2 * rows + 6]
 
-        def copies(a):
-            span = slice(TILE * a, TILE * (a + 1))
-            return [
-                pltpu.make_async_copy(source.at[span], ref.at[span], sems.at[a, n])
-                for n, (source, ref) in enumerate(zip(sources, grid_refs))
+        copies = [
+            [
+                pltpu.make_async_copy(
+                    source.at[TILE * a : TILE * (a + 1)], ref.at[TILE * a : TILE * (a + 1)], sems.at[n, a]
+                )
+                for a in range(rows)
             ]
-
-        for a in range(rows):
-            for copy in copies(a):
-                copy.start()
-        for a in range(rows):
-            for copy in copies(a):
-                copy.wait()
-            marks = [mark_ref[a, b].astype(F32) for b in range(cols)]
-            for n, ref in enumerate(grid_refs):
+            for n, (source, ref) in enumerate(zip(sources, grid_refs))
+        ]
+        for copy in sum(copies, []):
+            copy.start()
+        for n, ref in enumerate(grid_refs):
+            for a in range(rows):
+                copies[n][a].wait()
                 out = (kv_refs if n < 2 else qg_refs)[a]
                 for b in range(cols):
                     tile = tile_of(ref, a, b)
                     if n >= 2:
-                        tile = tile * (SCALE if n == 2 else marks[b])
+                        tile = tile * (SCALE if n == 2 else mark_ref[a, b].astype(F32))
                     tile = tile.astype(BF16)
                     out[rows_of(n % 2 * cols + b), :] = tile
                     for end, side in zip((0, cols - 1), side_refs):
                         if b == end:
                             side[rows_of(n * rows + a), :] = tile
-            write_marks(kv_refs[a], 2 * cols * TOKENS, marks, width)
+        for a in range(rows):
+            write_marks(kv_refs[a], 2 * cols * TOKENS, [mark_ref[a, b].astype(F32) for b in range(cols)], width)
         for b, side in zip((0, cols - 1), side_refs):
             write_marks(side, 4 * rows * TOKENS, [mark_ref[a, b].astype(F32) for a in range(rows)], width)
 
@@ -123,10 +123,10 @@
         in_specs=[SMEM] + [pl.BlockSpec(memory_space=pltpu.HBM)] * 4,
         out_specs=[VMEM] * len(shapes),
         out_shape=shapes,
-        scratch_shapes=[pltpu.VMEM(grid.shape, grid.dtype) for grid in grids] + [pltpu.SemaphoreType.DMA((rows, 4))],
+        scratch_shapes=[pltpu.VMEM(grid.shape, grid.dtype) for grid in grids] + [pltpu.SemaphoreType.DMA((4, rows))],
         compiler_params=pltpu.CompilerParams(vmem_limit_bytes=LIMIT),
         cost_estimate=pl.CostEstimate(flops=0, transcendentals=0, bytes_accessed=1 << 20),
-    )(tissue, *(pltpu.with_memory_space_constraint(grid, pltpu.HBM) for grid in grids))
+    )(*(pltpu.with_memory_space_constraint(array, pltpu.HBM) for array in (tissue, *grids)))
     return outs[:rows], outs[rows : 2 * rows], outs[2 * rows :]
 
 
@@ -226,9 +226,13 @@
         return mark_row(ref, 4 * self.rows * TOKENS, i, self.lanes)
 
 
+WIDTH = 3
+
+
 def drive(programs):
-    active = list(programs)
-    while active:
+    active, waiting = [], list(programs)
+    while active or waiting:
+        active, waiting = active + waiting[:WIDTH], waiting[WIDTH:]
         active = [program for program in active if next(program, True) is None]
 
 
@@ -236,12 +240,8 @@
     return [(a + i, b + j) for j in (-1, 0, 1) for i in (-1, 0, 1)]
 
 
-def each_group(width, step):
-    def one(g, carry):
-        step(pl.ds(pl.multiple_of(g * LANES, LANES), LANES))
-        return carry
-
-    lax.fori_loop(0, width // LANES, one, 0)
+def each_group(width, programs):
+    drive(sum((list(programs(pl.ds(g * LANES, LANES))) for g in range(width // LANES)), []))
 
 
 def columns(first, second):
@@ -307,39 +307,90 @@
 
         def step(lanes):
             block = Block(rows, cols, own_kv, (None,) * 6, lanes)
-            drive(tile(block, lanes, a, b) for a in range(rows) for b in range(cols))
+            return (tile(block, lanes, a, b) for a in range(rows) for b in range(cols))
 
         each_group(width, step)
 
     return body
 
 
-def forward(rows, cols, width):
+def corner_places(a, b, rows, cols):
+    return [(i, j) for i, j in around(a, b) if not 0 <= i < rows and not 0 <= j < cols]
+
+
+def forward_near(rows, cols, width):
     def body(mark_ref, *refs):
-        own_kv, near, own_qg = refs[:rows], refs[rows : rows + 6], refs[rows + 6 : 2 * rows + 6]
-        part_ref, level_ref, att_ref, *stat_refs = refs[2 * rows + 6 :]
+        own_kv, near, own_qg = refs[:rows], refs[rows : rows + 4] + (None, None), refs[rows + 4 : 2 * rows + 4]
+        part_ref, level_ref, part_out, level_out = refs[2 * rows + 4 :]
         mask = head_mask()
 
         def tile(block, lanes, a, b):
             _, places = split_places(a, b, rows, cols)
+            places = [place for place in places if place not in corner_places(a, b, rows, cols)]
+            index = a * cols + b
+            first = level_ref[2 * index : 2 * index + 1, lanes]
+            before = level_ref[2 * index + 1 : 2 * index + 2, lanes]
+            if not places:
+                part_out[rows_of(index), lanes] = part_ref[rows_of(index), lanes]
+                level_out[2 * index : 2 * index + 2, lanes] = level_ref[2 * index : 2 * index + 2, lanes]
+                return
+            allowed = [mark_ref[a, b].astype(F32) * block.mark(mark_ref, *place) > 0 for place in places]
+            q = spread(own_qg[a][rows_of(b), lanes], mask)
+            scores = nt(jnp.concatenate([block.tile(0, i, j, 0) for i, j in places], axis=0), q)
+            yield
+            top = softmax_part(scores, allowed, jnp.broadcast_to(first, (8, LANES)))
+            yield
+            low, total = exponentials(scores, allowed, top)
+            less = jnp.exp2(first - top)
+            yield
+            full = tn(low, jnp.concatenate([block.tile(1, i, j, 0) for i, j in places], axis=0))
+            own_by, _ = columns(less, less)
+            yield
+            part_out[rows_of(index), lanes] = gather_heads(full) + part_ref[rows_of(index), lanes] * own_by
+            level_out[2 * index : 2 * index + 1, lanes] = top
+            level_out[2 * index + 1 : 2 * index + 2, lanes] = total + less * before
+
+        def step(lanes):
+            block = Block(rows, cols, own_kv, near, lanes)
+            return (tile(block, lanes, a, b) for a in range(rows) for b in range(cols))
+
+        each_group(width, step)
+
+    return body
+
+
+def forward_last(rows, cols, width):
+    def body(mark_ref, *refs):
+        near, own_qg = (None,) * 4 + tuple(refs[:2]), refs[2 : rows + 2]
+        part_ref, level_ref, att_ref, *stat_refs = refs[rows + 2 :]
+        mask = head_mask()
+
+        def tile(block, lanes, a, b):
+            places = corner_places(a, b, rows, cols)
             index = a * cols + b
             own_mark = mark_ref[a, b].astype(F32)
-            allowed = [own_mark * block.mark(mark_ref, *place) > 0 for place in places]
-            q = spread(own_qg[a][rows_of(b), lanes], mask)
-            scores = nt(jnp.concatenate([block.tile(0, i, j, 0) for i, j in places], axis=0), q)
-            yield
-            first = level_ref[2 * index : 2 * index + 1, lanes]
-            top = softmax_part(scores, allowed, jnp.broadcast_to(first, (8, LANES)))
-            yield
-            low, total = exponentials(scores, allowed, top)
-            less = jnp.exp2(first - top)
-            total = total + less * level_ref[2 * index + 1 : 2 * index + 2, lanes]
-            yield
-            full = tn(low, jnp.concatenate([block.tile(1, i, j, 0) for i, j in places], axis=0))
-            inverse = own_mark / total
-            near_by, own_by = columns(inverse, inverse * less)
-            yield
-            att = (gather_heads(full) * near_by + part_ref[rows_of(index), lanes] * own_by).astype(BF16).astype(F32)
+            top = level_ref[2 * index : 2 * index + 1, lanes]
+            total = level_ref[2 * index + 1 : 2 * index + 2, lanes]
+            if places:
+                allowed = [own_mark * block.mark(mark_ref, *place) > 0 for place in places]
+                q = spread(own_qg[a][rows_of(b), lanes], mask)
+                scores = nt(jnp.concatenate([block.tile(0, i, j, 0) for i, j in places], axis=0), q)
+                yield
+                first, before = top, total
+                top = softmax_part(scores, allowed, jnp.broadcast_to(first, (8, LANES)))
+                yield
+                low, total = exponentials(scores, allowed, top)
+                less = jnp.exp2(first - top)
+                total = total + less * before
+                full = tn(low, jnp.concatenate([block.tile(1, i, j, 0) for i, j in places], axis=0))
+                inverse = own_mark / total
+                near_by, own_by = columns(inverse, inverse * less)
+                yield
+                att = gather_heads(full) * near_by + part_ref[rows_of(index), lanes] * own_by
+            else:
+                inverse = own_mark / total
+                att = part_ref[rows_of(index), lanes] * columns(inverse, inverse)[0]
+            att = att.astype(BF16).astype(F32)
             put_tile(att_ref, a, b, lanes, att)
             prod = (own_qg[a][rows_of(cols + b), lanes].astype(F32) * att).T
             dot = [jnp.sum(prod[rows_of(h)], axis=0, keepdims=True) for h in range(PER)]
@@ -347,8 +398,8 @@
             stat_refs[a][2 * b + 1 : 2 * b + 2, lanes] = jnp.concatenate(dot, axis=1)
 
         def step(lanes):
-            block = Block(rows, cols, own_kv, near, lanes)
-            drive(tile(block, lanes, a, b) for a in range(rows) for b in range(cols))
+            block = Block(rows, cols, None, near, lanes)
+            return (tile(block, lanes, a, b) for a in range(rows) for b in range(cols))
 
         each_group(width, step)
 
@@ -357,13 +408,16 @@
 
 def backward(rows, cols, width, a):
     def body(mark_ref, *refs):
-        all_refs = refs
         own_kv, near, own_qg = refs[:rows], refs[rows : rows + 6], refs[rows + 6 : 2 * rows + 6]
-        stat_ref, refs = refs[2 * rows + 6], refs[2 * rows + 7 + (2 if a else 0) :]
-        before_ref = None if a == 0 else all_refs[2 * rows + 8]
-        gq_ref, sum_ref, out_ref, sem = refs
+        stat_ref, gone_ref, refs = refs[2 * rows + 6], refs[2 * rows + 7], refs[2 * rows + 8 :]
+        gq_ref, sum_ref = refs[1 if a == 0 else 0], refs[2 if a == 0 else 1]
         mask = head_mask()
-        sum_ref[...] = jnp.zeros(sum_ref.shape, F32) if a == 0 else before_ref[...]
+        if a == 0:
+            copy = pltpu.make_async_copy(gone_ref, refs[0], refs[3])
+            copy.start()
+            sum_ref[...] = jnp.zeros(sum_ref.shape, F32)
+        else:
+            sum_ref[...] = gone_ref[...]
 
         def tile(block, lanes, b):
             places = around(a, b)
@@ -386,7 +440,7 @@
                 slopes.append((p * (grads[rows_of(t)] - dot)).astype(BF16))
             yield
             gq = gather_heads(tn(jnp.concatenate(slopes, axis=0), keys)) * SCALE
-            put_tile(out_ref, 0, b, lanes, gq)
+            put_tile(gq_ref, 0, b, lanes, gq)
             inside = [t for t, (i, j) in enumerate(places) if 0 <= i < rows and 0 <= j < cols]
             for n, (parts, right) in enumerate(((slopes, q), (probs, g))):
                 part = nn(jnp.concatenate([parts[t] for t in inside], axis=0), right)
@@ -396,20 +450,31 @@
 
         def step(lanes):
             block = Block(rows, cols, own_kv, near, lanes)
-            drive(tile(block, lanes, b) for b in range(cols))
+            return (tile(block, lanes, b) for b in range(cols))
 
         each_group(width, step)
-        copy = pltpu.make_async_copy(out_ref, gq_ref.at[TILE * a : TILE * (a + 1)], sem)
-        copy.start()
-        copy.wait()
+        if a == 0:
+            copy.wait()
 
     return body
 
 
-def key_side(rows, cols, width):
+def key_side(rows, cols, width, last):
     def body(mark_ref, *refs):
-        own_kv, near_kv, near_qg = refs[:rows], refs[rows : rows + 6], refs[rows + 6 : rows + 12]
-        above_s, below_s, sum_ref, gk_ref, gv_ref, acc_ref = refs[rows + 12 :]
+        own_kv, refs = refs[:rows], refs[rows:]
+        if last:
+            near_kv, near_qg, refs = (None, None, *refs[:4]), (None, None, *refs[4:8]), refs[8:]
+            sum_ref, gq_parts, (gq_ref, *out_refs) = refs[0], refs[1 : rows + 1], refs[rows + 1 : rows + 4]
+            acc_ref, *staged, sems = refs[rows + 4 :]
+            moves = [
+                pltpu.make_async_copy(part, gq_ref.at[TILE * a : TILE * (a + 1)], sems.at[a])
+                for a, part in enumerate(gq_parts)
+            ]
+            for copy in moves:
+                copy.start()
+        else:
+            near_kv, near_qg = (*refs[:2], *[None] * 4), (*refs[2:4], *[None] * 4)
+            above_s, below_s, sum_ref, acc_ref = refs[4:]
         mask = head_mask()
         acc_ref[...] = sum_ref[...]
 
@@ -451,15 +516,26 @@
             queries = Block(rows, cols, None, near_qg, lanes)
             outside = [
                 (i, j) for i in range(-1, rows + 1) for j in range(-1, cols + 1)
-                if not (0 <= i < rows and 0 <= j < cols)
+                if (not 0 <= j < cols if last else 0 <= j < cols and not 0 <= i < rows)
             ]
-            drive(tile(marks, queries, lanes, i, j) for i, j in outside)
-            for x in range(rows):
-                for y in range(cols):
-                    put_tile(gk_ref, x, y, lanes, acc_ref[0, rows_of(x * cols + y), lanes])
-                    put_tile(gv_ref, x, y, lanes, acc_ref[1, rows_of(x * cols + y), lanes])
+            return (tile(marks, queries, lanes, i, j) for i, j in outside)
 
         each_group(width, step)
+        if not last:
+            return
+        for g in range(width // LANES):
+            lanes = pl.ds(g * LANES, LANES)
+            for n in range(2):
+                for x in range(rows):
+                    for y in range(cols):
+                        put_tile(staged[n], x, y, lanes, acc_ref[n, rows_of(x * cols + y), lanes])
+                copy = pltpu.make_async_copy(
+                    staged[n].at[:, :, lanes], out_refs[n].at[:, :, lanes], sems.at[rows + 2 * g + n]
+                )
+                copy.start()
+                moves.append(copy)
+        for copy in moves:
+            copy.wait()
 
     return body
 
@@ -478,51 +554,64 @@
     pairs = 9 * rows * cols * TOKENS * TOKENS * width
     part, level = call(
         forward_own(rows, cols, width), [part_out, level_out], (tissue, *own_kv, *own_qg),
-        flops=8 * pairs, exps=pairs // (2 * HEAD),
+        flops=64 * pairs, exps=pairs // HEAD * 8,
     )
-    first_side, last_side, *sent_qg, level = lax.optimization_barrier((first_side, last_side, own_qg[0], own_qg[-1], level))
+    *sent_qg, level = lax.optimization_barrier((own_qg[0], own_qg[-1], level))
     left = shift(last_side, "cols", 1)
     right = shift(first_side, "cols", -1)
     above_qg = shift(sent_qg[1], "rows", 1)
     below_qg = shift(sent_qg[0], "rows", -1)
+    above_kv, below_kv, level = lax.optimization_barrier((above_kv, below_kv, level))
     first_kv, last_kv = pack_corners(above_kv, below_kv, cols)
-    near_kv = (above_kv, below_kv, left, right, shift(last_kv, "cols", 1), shift(first_kv, "cols", -1))
+    part, level = call(
+        forward_near(rows, cols, width), [part_out, level_out],
+        (tissue, *own_kv, above_kv, below_kv, left, right, *own_qg, part, level), flops=64 * pairs, exps=pairs // HEAD * 8,
+    )
+    corners_kv = (shift(last_kv, "cols", 1), shift(first_kv, "cols", -1))
+    near_kv = (above_kv, below_kv, left, right, *corners_kv)
     attended, *stats = call(
-        forward(rows, cols, width), [grid_out] + [stat_out] * rows,
-        (tissue, *own_kv, *near_kv, *own_qg, part, level), flops=8 * pairs, exps=pairs // (2 * HEAD),
+        forward_last(rows, cols, width), [grid_out] + [stat_out] * rows,
+        (tissue, *corners_kv, *own_qg, part, level), flops=4 * pairs, exps=pairs // (4 * HEAD),
     )
     above_s = shift(stats[-1], "rows", 1)
     below_s = shift(stats[0], "rows", -1)
-    query_parts = None
+    hbm = pl.BlockSpec(memory_space=pltpu.HBM)
+    parts = []
     for a in range(rows):
-        args = (tissue, *own_kv, *near_kv, *own_qg, stats[a]) + (query_parts or ())
-        query_parts = tuple(pl.pallas_call(
+        args = (tissue, *own_kv, *near_kv, *own_qg, stats[a], attended if a == 0 else sums)
+        half_out = jax.ShapeDtypeStruct((TILE,) + grid_out.shape[1:], BF16)
+        *done, part, sums = pl.pallas_call(
             backward(rows, cols, width, a),
-            in_specs=[SMEM] + [VMEM] * (2 * rows + 7) + ([pl.BlockSpec(memory_space=pl.ANY), VMEM] if a else []),
-            out_specs=[pl.BlockSpec(memory_space=pl.ANY), VMEM],
-            out_shape=[grid_out, sum_out],
-            scratch_shapes=[pltpu.VMEM((TILE,) + grid_out.shape[1:], BF16), pltpu.SemaphoreType.DMA],
-            input_output_aliases={2 * rows + 8: 0} if a else {},
+            in_specs=[SMEM] + [VMEM] * (len(args) - 1),
+            out_specs=[hbm] * (a == 0) + [VMEM, VMEM],
+            out_shape=[grid_out] * (a == 0) + [half_out, sum_out],
+            scratch_shapes=[pltpu.SemaphoreType.DMA] * (a == 0),
             compiler_params=pltpu.CompilerParams(vmem_limit_bytes=LIMIT),
             cost_estimate=pl.CostEstimate(flops=16 * pairs, transcendentals=pairs // (2 * HEAD), bytes_accessed=1 << 20),
-        )(*args))
+        )(*args)
+        parts.append(part)
         if a == 0:
-            above_s, below_s, sums = lax.optimization_barrier((above_s, below_s, query_parts[1]))
-            query_parts = (query_parts[0], sums)
+            attended_out = done[0]
+            above_s, below_s, sums = lax.optimization_barrier((above_s, below_s, sums))
             first_q, last_q = pack_queries(stats, above_s, below_s, above_qg, below_qg, cols)
-            near_qg = (above_qg, below_qg, left, right, shift(last_q, "cols", 1), shift(first_q, "cols", -1))
-    grad_query, sums = query_parts
-    args = (tissue, *own_kv, *near_kv, *near_qg, above_s, below_s, sums)
-    grad_key, grad_value = pl.pallas_call(
-        key_side(rows, cols, width),
+            side_qg = (left, right, shift(last_q, "cols", 1), shift(first_q, "cols", -1))
+    (sums,) = call(
+        key_side(rows, cols, width, False), [sum_out],
+        (tissue, *own_kv, above_kv, below_kv, above_qg, below_qg, above_s, below_s, sums),
+        flops=8 * pairs, exps=pairs // (4 * HEAD),
+    )
+    args = (tissue, *own_kv, *near_kv[2:], *side_qg, sums, *parts)
+    grad_query, grad_key, grad_value = pl.pallas_call(
+        key_side(rows, cols, width, True),
         in_specs=[SMEM] + [VMEM] * (len(args) - 1),
-        out_specs=[VMEM] * 2,
-        out_shape=[grid_out] * 2,
-        scratch_shapes=[pltpu.VMEM(sum_out.shape, F32)],
+        out_specs=[hbm] * 3,
+        out_shape=[grid_out] * 3,
+        scratch_shapes=[pltpu.VMEM(sum_out.shape, F32)] + [pltpu.VMEM(grid_out.shape, BF16)] * 2
+        + [pltpu.SemaphoreType.DMA((rows + 2 * (width // LANES),))],
         compiler_params=pltpu.CompilerParams(vmem_limit_bytes=LIMIT),
         cost_estimate=pl.CostEstimate(flops=8 * pairs, transcendentals=pairs // (2 * HEAD), bytes_accessed=1 << 20),
     )(*args)
-    return attended, grad_query, grad_key, grad_value
+    return attended_out, grad_query, grad_key, grad_value
 
 
 def solution(mesh):

time: 74 us -> 66.4 us (0.90)
  waiting for transfers between devices: 10.8 us -> 5.65 us
  Pallas kernels: 29.7 us -> 26.7 us
  starting transfers between devices: 31.3 us -> 32.6 us
    ppermute x12, waiting for transfers between devices: 10.8 us -> 5.65 us  [shift(): return lax.ppermute(array, axis, pairs)]
    pallas_call x2, Pallas kernels: 10.9 us -> 7.82 us  [local(): pl.pallas_call(backward(rows, cols, width, a), in_specs=[SMEM] + [VMEM] *...]
    pallas_call x1, Pallas kernels: 7.51 us -> 4.61 us  [local(): pl.pallas_call(key_side(rows, cols, width, True), in_specs=[SMEM] + [VMEM...]
    pallas_call x4 -> x6, Pallas kernels: 8.98 us -> 11.8 us  [call(): pl.pallas_call(body, in_specs=[SMEM if marks_first and n == 0 else VMEM f...]
    ppermute x12, starting transfers between devices: 31.3 us -> 32.6 us  [shift(): return lax.ppermute(array, axis, pairs)]
  transfers between devices with their start and end apart: 12 -> 12, of which waited for: 4 -> 3; matrix products, arithmetic and copies ran while one was open for 0% -> 0% of each run, Pallas kernels for 27% -> 30%
where the time goes in v4:
time: 66.4 us; the launch traced here: 66 us
  starting transfers between devices  32.6 us (49%)
  Pallas kernels  26.7 us (40%)
  waiting for transfers between devices  5.65 us (9%)
  between operations  1.03 us (2%)
    ppermute x12, starting transfers between devices, shift(): return lax.ppermute(array, axis, pairs)  32.6 us
    pallas_call x6, Pallas kernels, call(): pl.pallas_call(body, in_specs=[SMEM if marks_first and n == 0 else VMEM f...  11.8 us
    pallas_call x2, Pallas kernels, local(): pl.pallas_call(backward(rows, cols, width, a), in_specs=[SMEM] + [VMEM] *...  7.82 us
    ppermute x12, waiting for transfers between devices, shift(): return lax.ppermute(array, axis, pairs)  5.65 us
    pallas_call x1, Pallas kernels, local(): pl.pallas_call(key_side(rows, cols, width, True), in_specs=[SMEM] + [VMEM...  4.61 us
    pallas_call x1, Pallas kernels, pack(): pl.pallas_call(body, in_specs=[SMEM] + [pl.BlockSpec(memory_space=pltpu.H...  2.53 us
  transfers between devices with their start and end apart: 12, of which 3 were waited for; matrix products, arithmetic and copies ran while one was open for 0% of the time, Pallas kernels for 30%

profile of v4, /device:TPU:1, one launch (start us, length us, event | category | flops | bytes accessed | tf_op | source)
XLA Modules:
  0.0 66.0 jit_solution(12103628044813127971)
XLA Ops:
  0.6 0.0 copy-start
  0.6 2.5 %shard_map.84 = (bf16[400,768]{1,0:T(8,128)(2,1)S(1)}, bf16[400,768]{1,0:T(8,128)(2,1)S(1)}, bf16[384,768]{1,0:T(8,128)(2,1)S(1)}, bf16[384,768]{1,0:T(8,128)(2,...) custom-call(s32[2,3]{1,0:T(2,128)} %mark_ref.15, bf16[16,24,768]{2,1,0:T(8,128)(2,1)} %refs_0_.1, ...), custom_call_target="tpu_custom_call" | custom-call | bytes 1048576 | tf_op jit(solution)/shard_map/pallas_call | solution.py:121
  3.2 4.1 %collective-permute-start = (bf16[400,768]{1,0:T(8,128)(2,1)S(1)}, bf16[400,768]{1,0:T(8,128)(2,1)S(1)}, u32[]{:S(2)}, u32[]{:S(2)}) collective-permute-start(bf16[400,768]{1,0:T(8,128)(2,1)S(1)} %get-tuple-element.39.refs_1_), channel_id=1, source_target_pairs={{0,4},{4,8},{8,12},{1,5},{5,9},{9,13},{2,6},{6,10},{10,14},{3,7},{... | collective-permute-start | bytes 1843208 | tf_op jit(solution)/shard_map/ppermute | solution.py:28
  7.3 1.3 %collective-permute-start.1 = (bf16[400,768]{1,0:T(8,128)(2,1)S(1)}, bf16[400,768]{1,0:T(8,128)(2,1)S(1)}, u32[]{:S(2)}, u32[]{:S(2)}) collective-permute-start(bf16[400,768]{1,0:T(8,128)(2,1)S(1)} %get-tuple-element.38.refs_0_), channel_id=1, source_target_pairs={{4,0},{8,4},{12,8},{5,1},{9,5},{13,9},{6,2},{10,6},{14,10},{7,3},{... | collective-permute-start | bytes 1843208 | tf_op jit(solution)/shard_map/ppermute | solution.py:28
  8.6 4.0 %collective-permute-start.2 = (bf16[528,768]{1,0:T(8,128)(2,1)S(1)}, bf16[528,768]{1,0:T(8,128)(2,1)S(1)}, u32[]{:S(2)}, u32[]{:S(2)}) collective-permute-start(bf16[528,768]{1,0:T(8,128)(2,1)S(1)} %get-tuple-element.46), channel_id=1, source_target_pairs={{0,1},{1,2},{2,3},{4,5},{5,6},{6,7},{8,9},{9,10},{10,11},{12,13},{... | collective-permute-start | bytes 2433032 | tf_op jit(solution)/shard_map/ppermute | solution.py:28
  12.5 1.9 %collective-permute-start.3 = (bf16[528,768]{1,0:T(8,128)(2,1)S(1)}, bf16[528,768]{1,0:T(8,128)(2,1)S(1)}, u32[]{:S(2)}, u32[]{:S(2)}) collective-permute-start(bf16[528,768]{1,0:T(8,128)(2,1)S(1)} %get-tuple-element.47), channel_id=1, source_target_pairs={{1,0},{2,1},{3,2},{5,4},{6,5},{7,6},{9,8},{10,9},{11,10},{13,12},{... | collective-permute-start | bytes 2433032 | tf_op jit(solution)/shard_map/ppermute | solution.py:28
  14.5 0.0 copy-done
  14.5 2.8 %shard_map.85 = (f32[384,768]{1,0:T(8,128)S(1)}, f32[12,768]{1,0:T(8,128)S(1)}) custom-call(s32[2,3]{1,0:T(2,128)S(1)} %copy-done, bf16[400,768]{1,0:T(8,128)(2,1)S(1)} %get-tuple-element.38.refs_0_, bf16[400,768]{1,0:T(8,128)(2,1)S(1)} %get-tuple-element.39.refs_1_, bf16[384,768]{1,0:T(8,128)(2,1)S(1)} %get-tuple-element.62.refs_2_.refs_6_.refs_8_, ...), custom_call_target="tpu_custom_call" | custom-call | flops 10871635968 | bytes 2408472 | tf_op jit(solution)/shard_map/pallas_call | solution.py:45
  17.2 4.3 %collective-permute-start.8 = (bf16[384,768]{1,0:T(8,128)(2,1)S(1)}, bf16[384,768]{1,0:T(8,128)(2,1)S(1)}, u32[]{:S(2)}, u32[]{:S(2)}) collective-permute-start(bf16[384,768]{1,0:T(8,128)(2,1)S(1)} %get-tuple-element.61.refs_3_.refs_7_.refs_9_), channel_id=1, source_target_pairs={{0,4},{4,8},{8,12},{1,5},{5,9},{9,13},{2,6},{6,10},{10,14},{3,7},{... | collective-permute-start | bytes 1769480 | tf_op jit(solution)/shard_map/ppermute | solution.py:28
  21.5 0.0 collective-permute-done.above_ref.refs_2_
  21.5 1.3 %collective-permute-start.9 = (bf16[384,768]{1,0:T(8,128)(2,1)S(1)}, bf16[384,768]{1,0:T(8,128)(2,1)S(1)}, u32[]{:S(2)}, u32[]{:S(2)}) collective-permute-start(bf16[384,768]{1,0:T(8,128)(2,1)S(1)} %get-tuple-element.62.refs_2_.refs_6_.refs_8_), channel_id=1, source_target_pairs={{4,0},{8,4},{12,8},{5,1},{9,5},{13,9},{6,2},{10,6},{14,10},{7,3},{... | collective-permute-start | bytes 1769480 | tf_op jit(solution)/shard_map/ppermute | solution.py:28
  22.8 0.7 %collective-permute-done.1.below_ref.refs_3_ = bf16[400,768]{1,0:T(8,128)(2,1)S(1)} collective-permute-done((bf16[400,768]{1,0:T(8,128)(2,1)S(1)}, bf16[400,768]{1,0:T(8,128)(2,1)S(1)}, u32[]{:S(2)}, u32[]{:S(2)}) %collective-permute-start.1) | collective-permute-done | bytes 614432 | tf_op jit(solution)/shard_map/ppermute | solution.py:28
  23.6 0.1 shard_map.86
  23.6 4.9 %collective-permute-start.4 = (bf16[272,768]{1,0:T(8,128)(2,1)S(1)}, bf16[272,768]{1,0:T(8,128)(2,1)S(1)}, u32[]{:S(2)}, u32[]{:S(2)}) collective-permute-start(bf16[272,768]{1,0:T(8,128)(2,1)S(1)} %get-tuple-element.48), channel_id=1, source_target_pairs={{0,1},{1,2},{2,3},{4,5},{5,6},{6,7},{8,9},{9,10},{10,11},{12,13},{... | collective-permute-start | bytes 1253384 | tf_op jit(solution)/shard_map/ppermute | solution.py:28
  28.5 0.0 collective-permute-done.2.refs_4_.refs_2_.refs_6_
  28.5 1.9 %collective-permute-start.5 = (bf16[272,768]{1,0:T(8,128)(2,1)S(1)}, bf16[272,768]{1,0:T(8,128)(2,1)S(1)}, u32[]{:S(2)}, u32[]{:S(2)}) collective-permute-start(bf16[272,768]{1,0:T(8,128)(2,1)S(1)} %get-tuple-element.49), channel_id=1, source_target_pairs={{1,0},{2,1},{3,2},{5,4},{6,5},{7,6},{9,8},{10,9},{11,10},{13,12},{... | collective-permute-start | bytes 1253384 | tf_op jit(solution)/shard_map/ppermute | solution.py:28
  30.4 0.0 collective-permute-done.3.refs_5_.refs_3_.refs_7_
  30.4 3.1 %shard_map.87 = (f32[384,768]{1,0:T(8,128)S(1)}, f32[12,768]{1,0:T(8,128)S(1)}) custom-call(s32[2,3]{1,0:T(2,128)S(1)} %copy-done, bf16[400,768]{1,0:T(8,128)(2,1)S(1)} %get-tuple-element.38.refs_0_, bf16[400,768]{1,0:T(8,128)(2,1)S(1)} %get-tuple-element.39.refs_1_, bf16[400,768]{1,0:T(8,128)(2,1)S(1)} %collective-permute-done.above_ref.refs_2_, ...), custom_call_target="tpu_custom_call" | custom-call | flops 10871635968 | bytes 6475800 | tf_op jit(solution)/shard_map/pallas_call | solution.py:45
  33.6 0.0 collective-permute-done.4.refs_0_.refs_6_.refs_4_
  33.6 4.6 %collective-permute-done.5.refs_1_.refs_7_.refs_5_ = bf16[272,768]{1,0:T(8,128)(2,1)S(1)} collective-permute-done((bf16[272,768]{1,0:T(8,128)(2,1)S(1)}, bf16[272,768]{1,0:T(8,128)(2,1)S(1)}, u32[]{:S(2)}, u32[]{:S(2)}) %collective-permute-start.5) | collective-permute-done | bytes 417824 | tf_op jit(solution)/shard_map/ppermute | solution.py:28
  38.2 2.7 %shard_map.88 = (bf16[16,24,768]{2,1,0:T(8,128)(2,1)S(1)}, f32[6,768]{1,0:T(8,128)S(1)}, f32[6,768]{1,0:T(8,128)S(1)}) custom-call(s32[2,3]{1,0:T(2,128)S(1)} %copy-done, bf16[272,768]{1,0:T(8,128)(2,1)S(1)} %collective-permute-done.4.refs_0_.refs_6_.refs_4_, bf16[272,768]{1,0:T(8,128)(2,1)S(1)} %collective-permute-done.5.refs_1_.refs_7_.refs_5_, ...), custom_call_target="tpu_custom_call" | custom-call | flops 679477248 | bytes 3231768 | tf_op jit(solution)/shard_map/pallas_call | solution.py:45
  40.9 3.2 %collective-permute-start.6 = (f32[6,768]{1,0:T(8,128)S(1)}, f32[6,768]{1,0:T(8,128)S(1)}, u32[]{:S(2)}, u32[]{:S(2)}) collective-permute-start(f32[6,768]{1,0:T(8,128)S(1)} %get-tuple-element.57.refs_1_.refs_10_), channel_id=1, source_target_pairs={{0,4},{4,8},{8,12},{1,5},{5,9},{9,13},{2,6},{6,10},{10,14},{3,7},{... | collective-permute-start | bytes 55304 | tf_op jit(solution)/shard_map/ppermute | solution.py:28
  44.0 1.3 %collective-permute-start.7 = (f32[6,768]{1,0:T(8,128)S(1)}, f32[6,768]{1,0:T(8,128)S(1)}, u32[]{:S(2)}, u32[]{:S(2)}) collective-permute-start(f32[6,768]{1,0:T(8,128)S(1)} %get-tuple-element.54.refs_10_.refs_0_), channel_id=1, source_target_pairs={{4,0},{8,4},{12,8},{5,1},{9,5},{13,9},{6,2},{10,6},{14,10},{7,3},{... | collective-permute-start | bytes 55304 | tf_op jit(solution)/shard_map/ppermute | solution.py:28
  45.3 3.9 %shard_map.89 = (bf16[16,24,768]{2,1,0:T(8,128)(2,1)}, bf16[8,24,768]{2,1,0:T(8,128)(2,1)S(1)}, f32[2,384,768]{2,1,0:T(8,128)S(1)}) custom-call(s32[2,3]{1,0:T(2,128)S(1)} %copy-done, bf16[400,768]{1,0:T(8,128)(2,1)S(1)} %get-tuple-element.38.refs_0_, bf16[400,768]{1,0:T(8,128)(2,1)S(1)} %get-tuple-element.39.refs_1_, ...), custom_call_target="tpu_custom_call" | custom-call | flops 2717908992 | bytes 1048576 | tf_op jit(solution)/shard_map/pallas_call | solution.py:583
  49.2 0.0 collective-permute-done.6.refs_2_.refs_6_
  49.2 0.0 collective-permute-done.7.refs_3_.refs_7_
  49.2 0.0 collective-permute-done.8.refs_4_
  49.3 0.0 collective-permute-done.9.refs_5_
  49.3 0.1 shard_map.90
  49.4 2.2 %collective-permute-start.10 = (bf16[288,768]{1,0:T(8,128)(2,1)S(1)}, bf16[288,768]{1,0:T(8,128)(2,1)S(1)}, u32[]{:S(2)}, u32[]{:S(2)}) collective-permute-start(bf16[288,768]{1,0:T(8,128)(2,1)S(1)} %get-tuple-element.63), channel_id=1, source_target_pairs={{0,1},{1,2},{2,3},{4,5},{5,6},{6,7},{8,9},{9,10},{10,11},{12,13},{... | collective-permute-start | bytes 1327112 | tf_op jit(solution)/shard_map/ppermute | solution.py:28
  51.6 2.3 %collective-permute-start.11 = (bf16[288,768]{1,0:T(8,128)(2,1)S(1)}, bf16[288,768]{1,0:T(8,128)(2,1)S(1)}, u32[]{:S(2)}, u32[]{:S(2)}) collective-permute-start(bf16[288,768]{1,0:T(8,128)(2,1)S(1)} %get-tuple-element.64), channel_id=1, source_target_pairs={{1,0},{2,1},{3,2},{5,4},{6,5},{7,6},{9,8},{10,9},{11,10},{13,12},{... | collective-permute-start | bytes 1327112 | tf_op jit(solution)/shard_map/ppermute | solution.py:28
  53.9 3.9 %shard_map.91 = (bf16[8,24,768]{2,1,0:T(8,128)(2,1)S(1)}, f32[2,384,768]{2,1,0:T(8,128)S(1)}) custom-call(s32[2,3]{1,0:T(2,128)S(1)} %copy-done, bf16[400,768]{1,0:T(8,128)(2,1)S(1)} %get-tuple-element.38.refs_0_, bf16[400,768]{1,0:T(8,128)(2,1)S(1)} %get-tuple-element.39.refs_1_, bf16[400,768]{1,0:T(8,128)(2,1)S(1)} %collective-permute-done.above_ref.refs_2_, ...), custom_call_target="tpu_custom_call" | custom-call | flops 2717908992 | bytes 1048576 | tf_op jit(solution)/shard_map/pallas_call | solution.py:583
  57.8 3.0 %shard_map.92.refs_10_ = f32[2,384,768]{2,1,0:T(8,128)S(1)} custom-call(s32[2,3]{1,0:T(2,128)S(1)} %copy-done, bf16[400,768]{1,0:T(8,128)(2,1)S(1)} %get-tuple-element.38.refs_0_, bf16[400,768]{1,0:T(8,128)(2,1)S(1)} %get-tuple-element.39.refs_1_, bf16[400,768]{1,0:T(8,128)(2,1)S(1)} %collective-permute-done.above_ref.refs_2_, ...), custom_call_target="tpu_custom_call" | custom-call | flops 1358954496 | bytes 6033432 | tf_op jit(solution)/shard_map/pallas_call | solution.py:45
  60.9 0.0 collective-permute-done.10.refs_8_
  60.9 0.3 collective-permute-done.11.refs_9_
  61.2 4.6 %shard_map.93 = (bf16[16,24,768]{2,1,0:T(8,128)(2,1)}, bf16[16,24,768]{2,1,0:T(8,128)(2,1)}, bf16[16,24,768]{2,1,0:T(8,128)(2,1)}) custom-call(s32[2,3]{1,0:T(2,128)S(1)} %copy-done, bf16[400,768]{1,0:T(8,128)(2,1)S(1)} %get-tuple-element.38.refs_0_, bf16[400,768]{1,0:T(8,128)(2,1)S(1)} %get-tuple-element.39.refs_1_, ...), custom_call_target="tpu_custom_call" | custom-call | flops 1358954496 | bytes 1048576 | tf_op jit(solution)/shard_map/pallas_call | solution.py:604
Async XLA Ops:
  0.6 13.8 %copy-start = (s32[2,3]{1,0:T(2,128)S(1)}, s32[2,3]{1,0:T(2,128)}, u32[]{:S(2)}) copy-start(s32[2,3]{1,0:T(2,128)} %mark_ref.15) | copy-start | bytes 76
  3.2 18.4 %collective-permute-start = (bf16[400,768]{1,0:T(8,128)(2,1)S(1)}, bf16[400,768]{1,0:T(8,128)(2,1)S(1)}, u32[]{:S(2)}, u32[]{:S(2)}) collective-permute-start(bf16[400,768]{1,0:T(8,128)(2,1)S(1)} %get-tuple-element.39.refs_1_), channel_id=1, source_target_pairs={{0,4},{4,8},{8,12},{1,5},{5,9},{9,13},{2,6},{6,10},{10,14},{3,7},{... | collective-permute-start | bytes 1843208 | tf_op jit(solution)/shard_map/ppermute | solution.py:28
  7.3 16.3 %collective-permute-start.1 = (bf16[400,768]{1,0:T(8,128)(2,1)S(1)}, bf16[400,768]{1,0:T(8,128)(2,1)S(1)}, u32[]{:S(2)}, u32[]{:S(2)}) collective-permute-start(bf16[400,768]{1,0:T(8,128)(2,1)S(1)} %get-tuple-element.38.refs_0_), channel_id=1, source_target_pairs={{4,0},{8,4},{12,8},{5,1},{9,5},{13,9},{6,2},{10,6},{14,10},{7,3},{... | collective-permute-start | bytes 1843208 | tf_op jit(solution)/shard_map/ppermute | solution.py:28
  8.6 19.9 %collective-permute-start.2 = (bf16[528,768]{1,0:T(8,128)(2,1)S(1)}, bf16[528,768]{1,0:T(8,128)(2,1)S(1)}, u32[]{:S(2)}, u32[]{:S(2)}) collective-permute-start(bf16[528,768]{1,0:T(8,128)(2,1)S(1)} %get-tuple-element.46), channel_id=1, source_target_pairs={{0,1},{1,2},{2,3},{4,5},{5,6},{6,7},{8,9},{9,10},{10,11},{12,13},{... | collective-permute-start | bytes 2433032 | tf_op jit(solution)/shard_map/ppermute | solution.py:28
  12.5 17.9 %collective-permute-start.3 = (bf16[528,768]{1,0:T(8,128)(2,1)S(1)}, bf16[528,768]{1,0:T(8,128)(2,1)S(1)}, u32[]{:S(2)}, u32[]{:S(2)}) collective-permute-start(bf16[528,768]{1,0:T(8,128)(2,1)S(1)} %get-tuple-element.47), channel_id=1, source_target_pairs={{1,0},{2,1},{3,2},{5,4},{6,5},{7,6},{9,8},{10,9},{11,10},{13,12},{... | collective-permute-start | bytes 2433032 | tf_op jit(solution)/shard_map/ppermute | solution.py:28
  17.2 32.0 %collective-permute-start.8 = (bf16[384,768]{1,0:T(8,128)(2,1)S(1)}, bf16[384,768]{1,0:T(8,128)(2,1)S(1)}, u32[]{:S(2)}, u32[]{:S(2)}) collective-permute-start(bf16[384,768]{1,0:T(8,128)(2,1)S(1)} %get-tuple-element.61.refs_3_.refs_7_.refs_9_), channel_id=1, source_target_pairs={{0,4},{4,8},{8,12},{1,5},{5,9},{9,13},{2,6},{6,10},{10,14},{3,7},{... | collective-permute-start | bytes 1769480 | tf_op jit(solution)/shard_map/ppermute | solution.py:28
  21.5 27.7 %collective-permute-start.9 = (bf16[384,768]{1,0:T(8,128)(2,1)S(1)}, bf16[384,768]{1,0:T(8,128)(2,1)S(1)}, u32[]{:S(2)}, u32[]{:S(2)}) collective-permute-start(bf16[384,768]{1,0:T(8,128)(2,1)S(1)} %get-tuple-element.62.refs_2_.refs_6_.refs_8_), channel_id=1, source_target_pairs={{4,0},{8,4},{12,8},{5,1},{9,5},{13,9},{6,2},{10,6},{14,10},{7,3},{... | collective-permute-start | bytes 1769480 | tf_op jit(solution)/shard_map/ppermute | solution.py:28
  23.6 10.0 %collective-permute-start.4 = (bf16[272,768]{1,0:T(8,128)(2,1)S(1)}, bf16[272,768]{1,0:T(8,128)(2,1)S(1)}, u32[]{:S(2)}, u32[]{:S(2)}) collective-permute-start(bf16[272,768]{1,0:T(8,128)(2,1)S(1)} %get-tuple-element.48), channel_id=1, source_target_pairs={{0,1},{1,2},{2,3},{4,5},{5,6},{6,7},{8,9},{9,10},{10,11},{12,13},{... | collective-permute-start | bytes 1253384 | tf_op jit(solution)/shard_map/ppermute | solution.py:28
  28.5 9.7 %collective-permute-start.5 = (bf16[272,768]{1,0:T(8,128)(2,1)S(1)}, bf16[272,768]{1,0:T(8,128)(2,1)S(1)}, u32[]{:S(2)}, u32[]{:S(2)}) collective-permute-start(bf16[272,768]{1,0:T(8,128)(2,1)S(1)} %get-tuple-element.49), channel_id=1, source_target_pairs={{1,0},{2,1},{3,2},{5,4},{6,5},{7,6},{9,8},{10,9},{11,10},{13,12},{... | collective-permute-start | bytes 1253384 | tf_op jit(solution)/shard_map/ppermute | solution.py:28
  40.9 8.4 %collective-permute-start.6 = (f32[6,768]{1,0:T(8,128)S(1)}, f32[6,768]{1,0:T(8,128)S(1)}, u32[]{:S(2)}, u32[]{:S(2)}) collective-permute-start(f32[6,768]{1,0:T(8,128)S(1)} %get-tuple-element.57.refs_1_.refs_10_), channel_id=1, source_target_pairs={{0,4},{4,8},{8,12},{1,5},{5,9},{9,13},{2,6},{6,10},{10,14},{3,7},{... | collective-permute-start | bytes 55304 | tf_op jit(solution)/shard_map/ppermute | solution.py:28
  44.0 5.2 %collective-permute-start.7 = (f32[6,768]{1,0:T(8,128)S(1)}, f32[6,768]{1,0:T(8,128)S(1)}, u32[]{:S(2)}, u32[]{:S(2)}) collective-permute-start(f32[6,768]{1,0:T(8,128)S(1)} %get-tuple-element.54.refs_10_.refs_0_), channel_id=1, source_target_pairs={{4,0},{8,4},{12,8},{5,1},{9,5},{13,9},{6,2},{10,6},{14,10},{7,3},{... | collective-permute-start | bytes 55304 | tf_op jit(solution)/shard_map/ppermute | solution.py:28
  49.4 11.5 %collective-permute-start.10 = (bf16[288,768]{1,0:T(8,128)(2,1)S(1)}, bf16[288,768]{1,0:T(8,128)(2,1)S(1)}, u32[]{:S(2)}, u32[]{:S(2)}) collective-permute-start(bf16[288,768]{1,0:T(8,128)(2,1)S(1)} %get-tuple-element.63), channel_id=1, source_target_pairs={{0,1},{1,2},{2,3},{4,5},{5,6},{6,7},{8,9},{9,10},{10,11},{12,13},{... | collective-permute-start | bytes 1327112 | tf_op jit(solution)/shard_map/ppermute | solution.py:28
  51.6 9.6 %collective-permute-start.11 = (bf16[288,768]{1,0:T(8,128)(2,1)S(1)}, bf16[288,768]{1,0:T(8,128)(2,1)S(1)}, u32[]{:S(2)}, u32[]{:S(2)}) collective-permute-start(bf16[288,768]{1,0:T(8,128)(2,1)S(1)} %get-tuple-element.64), channel_id=1, source_target_pairs={{1,0},{2,1},{3,2},{5,4},{6,5},{7,6},{9,8},{10,9},{11,10},{13,12},{... | collective-permute-start | bytes 1327112 | tf_op jit(solution)/shard_map/ppermute | solution.py:28

commit v5 on v4

--- a/solution.py
+++ b/solution.py
@@ -40,11 +40,11 @@
     return lax.dot_general(a, b, (((0,), (0,)), ((), ())), preferred_element_type=F32)
 
 
-def call(body, out_shape, args, marks_first=True, flops=0, exps=0):
+def call(body, out_shape, args, flops=0, exps=0):
     size = sum(array.size * array.dtype.itemsize for array in args)
     return pl.pallas_call(
         body,
-        in_specs=[SMEM if marks_first and n == 0 else VMEM for n in range(len(args))],
+        in_specs=[VMEM] * len(args),
         out_specs=[VMEM] * len(out_shape),
         out_shape=out_shape,
         compiler_params=pltpu.CompilerParams(vmem_limit_bytes=LIMIT),
@@ -142,7 +142,7 @@
             write_marks(out, 4 * TOKENS, ends, width)
 
     shape = jax.ShapeDtypeStruct((4 * TOKENS + MARKS, width), BF16)
-    return call(body, [shape] * 2, (above, below), marks_first=False)
+    return call(body, [shape] * 2, (above, below))
 
 
 def pieces(x):
@@ -172,7 +172,7 @@
             out[4 * TOKENS :, :] = jnp.concatenate(parts, axis=0).astype(BF16)
 
     shape = jax.ShapeDtypeStruct((4 * TOKENS + height, width), BF16)
-    return call(body, [shape] * 2, (*stats, above_s, below_s, above_qg, below_qg), marks_first=False)
+    return call(body, [shape] * 2, (*stats, above_s, below_s, above_qg, below_qg))
 
 
 def head_mask():
@@ -213,11 +213,11 @@
         ref = self.left if j < 0 else self.right
         return ref[rows_of((side + n) * self.rows + i), self.lanes]
 
-    def mark(self, marks, i, j):
+    def mark(self, i, j):
         ends = {-1: (self.above, 0), self.rows: (self.below, 1)}
         if 0 <= j < self.cols:
             if i not in ends:
-                return marks[i, j].astype(F32)
+                return mark_row(self.own[i], 2 * self.cols * TOKENS, j, self.lanes)
             return mark_row(ends[i][0], 2 * self.cols * TOKENS, j, self.lanes)
         if i in ends:
             ref = self.corner_left if j < 0 else self.corner_right
@@ -283,14 +283,14 @@
 
 
 def forward_own(rows, cols, width):
-    def body(mark_ref, *refs):
+    def body(*refs):
         own_kv, own_qg = refs[:rows], refs[rows : 2 * rows]
         part_ref, level_ref = refs[2 * rows :]
         mask = head_mask()
 
         def tile(block, lanes, a, b):
             places, _ = split_places(a, b, rows, cols)
-            allowed = [None if place == (a, b) else mark_ref[a, b] * mark_ref[place] > 0 for place in places]
+            allowed = [None if place == (a, b) else block.mark(a, b) * block.mark(*place) > 0 for place in places]
             q = spread(own_qg[a][rows_of(b), lanes], mask)
             scores = nt(jnp.concatenate([block.tile(0, i, j, 0) for i, j in places], axis=0), q)
             yield
@@ -318,10 +318,21 @@
     return [(i, j) for i, j in around(a, b) if not 0 <= i < rows and not 0 <= j < cols]
 
 
+def place(a, b):
+    return slice(TILE * a, TILE * (a + 1)), slice(TILE * b, TILE * (b + 1))
+
+
+def finish(att_ref, a, b, lanes, att, grads):
+    att = att.astype(BF16).astype(F32)
+    put_tile(att_ref, a, b, lanes, att)
+    prod = (grads.astype(F32) * att).T
+    return jnp.concatenate([jnp.sum(prod[rows_of(h)], axis=0, keepdims=True) for h in range(PER)], axis=1)
+
+
 def forward_near(rows, cols, width):
-    def body(mark_ref, *refs):
+    def body(*refs):
         own_kv, near, own_qg = refs[:rows], refs[rows : rows + 4] + (None, None), refs[rows + 4 : 2 * rows + 4]
-        part_ref, level_ref, part_out, level_out = refs[2 * rows + 4 :]
+        part_ref, level_ref, part_out, level_out, att_ref = refs[2 * rows + 4 :]
         mask = head_mask()
 
         def tile(block, lanes, a, b):
@@ -330,11 +341,7 @@
             index = a * cols + b
             first = level_ref[2 * index : 2 * index + 1, lanes]
             before = level_ref[2 * index + 1 : 2 * index + 2, lanes]
-            if not places:
-                part_out[rows_of(index), lanes] = part_ref[rows_of(index), lanes]
-                level_out[2 * index : 2 * index + 2, lanes] = level_ref[2 * index : 2 * index + 2, lanes]
-                return
-            allowed = [mark_ref[a, b].astype(F32) * block.mark(mark_ref, *place) > 0 for place in places]
+            allowed = [block.mark(a, b) * block.mark(*place) > 0 for place in places]
             q = spread(own_qg[a][rows_of(b), lanes], mask)
             scores = nt(jnp.concatenate([block.tile(0, i, j, 0) for i, j in places], axis=0), q)
             yield
@@ -344,11 +351,21 @@
             less = jnp.exp2(first - top)
             yield
             full = tn(low, jnp.concatenate([block.tile(1, i, j, 0) for i, j in places], axis=0))
-            own_by, _ = columns(less, less)
-            yield
-            part_out[rows_of(index), lanes] = gather_heads(full) + part_ref[rows_of(index), lanes] * own_by
-            level_out[2 * index : 2 * index + 1, lanes] = top
-            level_out[2 * index + 1 : 2 * index + 2, lanes] = total + less * before
+            total = total + less * before
+            if corner_places(a, b, rows, cols):
+                own_by, _ = columns(less, less)
+                yield
+                part_out[rows_of(index), lanes] = gather_heads(full) + part_ref[rows_of(index), lanes] * own_by
+                level_out[2 * index : 2 * index + 1, lanes] = top
+                level_out[2 * index + 1 : 2 * index + 2, lanes] = total
+                return
+            inverse = block.mark(a, b) / total
+            near_by, own_by = columns(inverse, inverse * less)
+            yield
+            att = gather_heads(full) * near_by + part_ref[rows_of(index), lanes] * own_by
+            dot = finish(att_ref, a, b, lanes, att, own_qg[a][rows_of(cols + b), lanes])
+            level_out[2 * index : 2 * index + 1, lanes] = top + jnp.log2(total)
+            level_out[2 * index + 1 : 2 * index + 2, lanes] = dot
 
         def step(lanes):
             block = Block(rows, cols, own_kv, near, lanes)
@@ -360,7 +377,8 @@
 
 
 def forward_last(rows, cols, width):
-    def body(mark_ref, *refs):
+    def body(*refs):
+        own_kv, refs = refs[:rows], refs[rows:]
         near, own_qg = (None,) * 4 + tuple(refs[:2]), refs[2 : rows + 2]
         part_ref, level_ref, att_ref, *stat_refs = refs[rows + 2 :]
         mask = head_mask()
@@ -368,37 +386,32 @@
         def tile(block, lanes, a, b):
             places = corner_places(a, b, rows, cols)
             index = a * cols + b
-            own_mark = mark_ref[a, b].astype(F32)
-            top = level_ref[2 * index : 2 * index + 1, lanes]
-            total = level_ref[2 * index + 1 : 2 * index + 2, lanes]
-            if places:
-                allowed = [own_mark * block.mark(mark_ref, *place) > 0 for place in places]
-                q = spread(own_qg[a][rows_of(b), lanes], mask)
-                scores = nt(jnp.concatenate([block.tile(0, i, j, 0) for i, j in places], axis=0), q)
-                yield
-                first, before = top, total
-                top = softmax_part(scores, allowed, jnp.broadcast_to(first, (8, LANES)))
-                yield
-                low, total = exponentials(scores, allowed, top)
-                less = jnp.exp2(first - top)
-                total = total + less * before
-                full = tn(low, jnp.concatenate([block.tile(1, i, j, 0) for i, j in places], axis=0))
-                inverse = own_mark / total
-                near_by, own_by = columns(inverse, inverse * less)
-                yield
-                att = gather_heads(full) * near_by + part_ref[rows_of(index), lanes] * own_by
-            else:
-                inverse = own_mark / total
-                att = part_ref[rows_of(index), lanes] * columns(inverse, inverse)[0]
-            att = att.astype(BF16).astype(F32)
-            put_tile(att_ref, a, b, lanes, att)
-            prod = (own_qg[a][rows_of(cols + b), lanes].astype(F32) * att).T
-            dot = [jnp.sum(prod[rows_of(h)], axis=0, keepdims=True) for h in range(PER)]
+            own_mark = block.mark(a, b)
+            if not places:
+                stat_refs[a][2 * b : 2 * b + 2, lanes] = level_ref[2 * index : 2 * index + 2, lanes]
+                return
+            first = level_ref[2 * index : 2 * index + 1, lanes]
+            before = level_ref[2 * index + 1 : 2 * index + 2, lanes]
+            allowed = [own_mark * block.mark(*place) > 0 for place in places]
+            q = spread(own_qg[a][rows_of(b), lanes], mask)
+            scores = nt(jnp.concatenate([block.tile(0, i, j, 0) for i, j in places], axis=0), q)
+            yield
+            top = softmax_part(scores, allowed, jnp.broadcast_to(first, (8, LANES)))
+            yield
+            low, total = exponentials(scores, allowed, top)
+            less = jnp.exp2(first - top)
+            total = total + less * before
+            full = tn(low, jnp.concatenate([block.tile(1, i, j, 0) for i, j in places], axis=0))
+            inverse = own_mark / total
+            near_by, own_by = columns(inverse, inverse * less)
+            yield
+            att = gather_heads(full) * near_by + part_ref[rows_of(index), lanes] * own_by
+            dot = finish(att_ref, a, b, lanes, att, own_qg[a][rows_of(cols + b), lanes])
             stat_refs[a][2 * b : 2 * b + 1, lanes] = top + jnp.log2(total)
-            stat_refs[a][2 * b + 1 : 2 * b + 2, lanes] = jnp.concatenate(dot, axis=1)
+            stat_refs[a][2 * b + 1 : 2 * b + 2, lanes] = dot
 
         def step(lanes):
-            block = Block(rows, cols, None, near, lanes)
+            block = Block(rows, cols, own_kv, near, lanes)
             return (tile(block, lanes, a, b) for a in range(rows) for b in range(cols))
 
         each_group(width, step)
@@ -406,41 +419,50 @@
     return body
 
 
-def backward(rows, cols, width, a):
-    def body(mark_ref, *refs):
-        own_kv, near, own_qg = refs[:rows], refs[rows : rows + 6], refs[rows + 6 : 2 * rows + 6]
-        stat_ref, gone_ref, refs = refs[2 * rows + 6], refs[2 * rows + 7], refs[2 * rows + 8 :]
-        gq_ref, sum_ref = refs[1 if a == 0 else 0], refs[2 if a == 0 else 1]
+def backward(rows, cols, width, tiles, kind):
+    def body(*refs):
+        count = 4 if kind == 0 else 6
+        own_kv, near, refs = refs[:rows], (*refs[rows : rows + count], None, None)[:6], refs[rows + count :]
+        own_qg, stat_refs, refs = refs[:rows], refs[rows : 2 * rows], refs[2 * rows :]
+        moves = []
+        if kind == 0:
+            gq_ref, sum_ref = refs
+            sum_ref[...] = jnp.zeros(sum_ref.shape, F32)
+        elif kind == 1:
+            _, middle_ref, edge_ref, att_ref, gq_ref, sum_ref, sems = refs
+            for a in range(rows):
+                for b in range(cols):
+                    source = edge_ref if corner_places(a, b, rows, cols) else middle_ref
+                    where = place(a, b)
+                    moves.append(pltpu.make_async_copy(source.at[where], att_ref.at[where], sems.at[a * cols + b]))
+                    moves[-1].start()
+        else:
+            _, gq_ref, sum_ref = refs
         mask = head_mask()
-        if a == 0:
-            copy = pltpu.make_async_copy(gone_ref, refs[0], refs[3])
-            copy.start()
-            sum_ref[...] = jnp.zeros(sum_ref.shape, F32)
-        else:
-            sum_ref[...] = gone_ref[...]
-
-        def tile(block, lanes, b):
+
+        def tile(block, lanes, a, b):
             places = around(a, b)
-            own_mark = mark_ref[a, b].astype(F32)
+            own_mark = block.mark(a, b)
             q = spread(own_qg[a][rows_of(b), lanes], mask)
             g = spread(own_qg[a][rows_of(cols + b), lanes], mask)
             keys = jnp.concatenate([block.tile(0, i, j, 0) for i, j in places], axis=0)
             values = jnp.concatenate([block.tile(1, i, j, 0) for i, j in places], axis=0)
-            level = stat_ref[2 * b : 2 * b + 1, lanes]
-            dot = stat_ref[2 * b + 1 : 2 * b + 2, lanes]
+            index = a * cols + b if kind == 0 else b
+            level = stat_refs[a][2 * index : 2 * index + 1, lanes]
+            dot = stat_refs[a][2 * index + 1 : 2 * index + 2, lanes]
             scores, grads = nt(keys, q), nt(values, g)
             yield
             probs, slopes = [], []
-            for t, place in enumerate(places):
+            for t, spot in enumerate(places):
                 less = level
-                if place != (a, b):
-                    less = jnp.where(own_mark * block.mark(mark_ref, *place) > 0, level, BIG)
+                if spot != (a, b):
+                    less = jnp.where(own_mark * block.mark(*spot) > 0, level, BIG)
                 p = jnp.exp2(scores[rows_of(t)] * LOG2E - less)
                 probs.append(p.astype(BF16))
                 slopes.append((p * (grads[rows_of(t)] - dot)).astype(BF16))
             yield
             gq = gather_heads(tn(jnp.concatenate(slopes, axis=0), keys)) * SCALE
-            put_tile(gq_ref, 0, b, lanes, gq)
+            put_tile(gq_ref, a, b, lanes, gq)
             inside = [t for t, (i, j) in enumerate(places) if 0 <= i < rows and 0 <= j < cols]
             for n, (parts, right) in enumerate(((slopes, q), (probs, g))):
                 part = nn(jnp.concatenate([parts[t] for t in inside], axis=0), right)
@@ -450,33 +472,41 @@
 
         def step(lanes):
             block = Block(rows, cols, own_kv, near, lanes)
-            return (tile(block, lanes, b) for b in range(cols))
+            return (tile(block, lanes, a, b) for a, b in tiles)
 
         each_group(width, step)
-        if a == 0:
+        for copy in moves:
             copy.wait()
 
     return body
 
 
 def key_side(rows, cols, width, last):
-    def body(mark_ref, *refs):
+    def body(*refs):
         own_kv, refs = refs[:rows], refs[rows:]
         if last:
             near_kv, near_qg, refs = (None, None, *refs[:4]), (None, None, *refs[4:8]), refs[8:]
-            sum_ref, gq_parts, (gq_ref, *out_refs) = refs[0], refs[1 : rows + 1], refs[rows + 1 : rows + 4]
-            acc_ref, *staged, sems = refs[rows + 4 :]
-            moves = [
-                pltpu.make_async_copy(part, gq_ref.at[TILE * a : TILE * (a + 1)], sems.at[a])
-                for a, part in enumerate(gq_parts)
-            ]
-            for copy in moves:
-                copy.start()
+            middle, gq_parts = refs[1:3], refs[3 : rows + 4]
+            gq_ref, *out_refs, acc_ref, staged_k, staged_v, sems = refs[rows + 4 :]
+            staged = (staged_k, staged_v)
+            moves = []
+
+            def move(source, target):
+                moves.append(pltpu.make_async_copy(source, target, sems.at[len(moves)]))
+                moves[-1].start()
+
+            for a in range(rows):
+                for b in range(cols):
+                    where = place(a, b)
+                    move(gq_parts[a + 1 if corner_places(a, b, rows, cols) else 0].at[where], gq_ref.at[where])
+            if cols > 2:
+                where = slice(None), slice(TILE, TILE * (cols - 1))
+                for n in range(2):
+                    move(middle[n].at[where], out_refs[n].at[where])
         else:
             near_kv, near_qg = (*refs[:2], *[None] * 4), (*refs[2:4], *[None] * 4)
-            above_s, below_s, sum_ref, acc_ref = refs[4:]
+            above_s, below_s, _, acc_ref, *staged = refs[4:]
         mask = head_mask()
-        acc_ref[...] = sum_ref[...]
 
         def stat_at(i, j, lanes):
             if 0 <= j < cols:
@@ -494,14 +524,14 @@
             q = spread(queries.tile(0, i, j, 2), mask)
             g = spread(queries.tile(1, i, j, 2), mask)
             level, dot = stat_at(i, j, lanes)
-            mark = marks.mark(mark_ref, i, j)
+            mark = marks.mark(i, j)
             keys = jnp.concatenate([marks.tile(0, x, y, 0) for x, y in places], axis=0)
             values = jnp.concatenate([marks.tile(1, x, y, 0) for x, y in places], axis=0)
             scores, grads = nt(keys, q), nt(values, g)
             yield
             probs, slopes = [], []
             for t, (x, y) in enumerate(places):
-                less = jnp.where(mark * mark_ref[x, y].astype(F32) > 0, level, BIG)
+                less = jnp.where(mark * marks.mark(x, y) > 0, level, BIG)
                 p = jnp.exp2(scores[rows_of(t)] * LOG2E - less)
                 probs.append(p.astype(BF16))
                 slopes.append((p * (grads[rows_of(t)] - dot)).astype(BF16))
@@ -521,19 +551,19 @@
             return (tile(marks, queries, lanes, i, j) for i, j in outside)
 
         each_group(width, step)
-        if not last:
-            return
+        done = (0, cols - 1) if last else range(1, cols - 1)
+        done = sorted(set(done))
         for g in range(width // LANES):
             lanes = pl.ds(g * LANES, LANES)
             for n in range(2):
-                for x in range(rows):
-                    for y in range(cols):
+                for y in done:
+                    for x in range(rows):
                         put_tile(staged[n], x, y, lanes, acc_ref[n, rows_of(x * cols + y), lanes])
-                copy = pltpu.make_async_copy(
-                    staged[n].at[:, :, lanes], out_refs[n].at[:, :, lanes], sems.at[rows + 2 * g + n]
-                )
-                copy.start()
-                moves.append(copy)
+                    if last:
+                        where = slice(None), slice(TILE * y, TILE * (y + 1)), lanes
+                        move(staged[n].at[where], out_refs[n].at[where])
+        if not last:
+            return
         for copy in moves:
             copy.wait()
 
@@ -553,7 +583,7 @@
     level_out = jax.ShapeDtypeStruct((2 * rows * cols, width), F32)
     pairs = 9 * rows * cols * TOKENS * TOKENS * width
     part, level = call(
-        forward_own(rows, cols, width), [part_out, level_out], (tissue, *own_kv, *own_qg),
+        forward_own(rows, cols, width), [part_out, level_out], (*own_kv, *own_qg),
         flops=64 * pairs, exps=pairs // HEAD * 8,
     )
     *sent_qg, level = lax.optimization_barrier((own_qg[0], own_qg[-1], level))
@@ -563,55 +593,61 @@
     below_qg = shift(sent_qg[0], "rows", -1)
     above_kv, below_kv, level = lax.optimization_barrier((above_kv, below_kv, level))
     first_kv, last_kv = pack_corners(above_kv, below_kv, cols)
-    part, level = call(
-        forward_near(rows, cols, width), [part_out, level_out],
-        (tissue, *own_kv, above_kv, below_kv, left, right, *own_qg, part, level), flops=64 * pairs, exps=pairs // HEAD * 8,
+    part, level, middle = call(
+        forward_near(rows, cols, width), [part_out, level_out, grid_out],
+        (*own_kv, above_kv, below_kv, left, right, *own_qg, part, level), flops=64 * pairs, exps=pairs // HEAD * 8,
     )
+    every = [(a, b) for a in range(rows) for b in range(cols)]
+    hbm = pl.BlockSpec(memory_space=pltpu.HBM)
+
+    def run(body, args, hbm_outs, vmem_outs, scratch, sums_at, sums_out, cost):
+        return pl.pallas_call(
+            body,
+            in_specs=[VMEM] * len(args),
+            out_specs=[hbm] * len(hbm_outs) + [VMEM] * len(vmem_outs),
+            out_shape=hbm_outs + vmem_outs,
+            scratch_shapes=scratch,
+            input_output_aliases={} if sums_at is None else {sums_at: sums_out},
+            compiler_params=pltpu.CompilerParams(vmem_limit_bytes=LIMIT),
+            cost_estimate=pl.CostEstimate(flops=cost * pairs, transcendentals=cost * pairs // 32 // HEAD, bytes_accessed=1 << 20),
+        )(*args)
+
+    parts = []
+    tiles = [spot for spot in every if not corner_places(*spot, rows, cols)]
+    args = (*own_kv, above_kv, below_kv, left, right, *own_qg, *[level] * rows)
+    part_gq, sums = run(backward(rows, cols, width, tiles, 0), args, [], [grid_out, sum_out], [], None, 1, 8)
+    parts.append(part_gq)
+    level, sums = lax.optimization_barrier((level, sums))
     corners_kv = (shift(last_kv, "cols", 1), shift(first_kv, "cols", -1))
     near_kv = (above_kv, below_kv, left, right, *corners_kv)
-    attended, *stats = call(
+    edge, *stats = call(
         forward_last(rows, cols, width), [grid_out] + [stat_out] * rows,
-        (tissue, *corners_kv, *own_qg, part, level), flops=4 * pairs, exps=pairs // (4 * HEAD),
+        (*own_kv, *corners_kv, *own_qg, part, level), flops=4 * pairs, exps=pairs // (4 * HEAD),
     )
     above_s = shift(stats[-1], "rows", 1)
     below_s = shift(stats[0], "rows", -1)
-    hbm = pl.BlockSpec(memory_space=pltpu.HBM)
-    parts = []
     for a in range(rows):
-        args = (tissue, *own_kv, *near_kv, *own_qg, stats[a], attended if a == 0 else sums)
-        half_out = jax.ShapeDtypeStruct((TILE,) + grid_out.shape[1:], BF16)
-        *done, part, sums = pl.pallas_call(
-            backward(rows, cols, width, a),
-            in_specs=[SMEM] + [VMEM] * (len(args) - 1),
-            out_specs=[hbm] * (a == 0) + [VMEM, VMEM],
-            out_shape=[grid_out] * (a == 0) + [half_out, sum_out],
-            scratch_shapes=[pltpu.SemaphoreType.DMA] * (a == 0),
-            compiler_params=pltpu.CompilerParams(vmem_limit_bytes=LIMIT),
-            cost_estimate=pl.CostEstimate(flops=16 * pairs, transcendentals=pairs // (2 * HEAD), bytes_accessed=1 << 20),
-        )(*args)
-        parts.append(part)
+        tiles = [spot for spot in every if spot[0] == a and corner_places(*spot, rows, cols)]
+        args = (*own_kv, *near_kv, *own_qg, *stats, sums) + ((middle, edge) if a == 0 else ())
+        *done, part_gq, sums = run(
+            backward(rows, cols, width, tiles, 1 if a == 0 else 2), args, [grid_out] * (a == 0), [grid_out, sum_out],
+            [pltpu.SemaphoreType.DMA((rows * cols,))] * (a == 0), 3 * rows + 6, 2 if a == 0 else 1, 16,
+        )
+        parts.append(part_gq)
         if a == 0:
-            attended_out = done[0]
+            attended = done[0]
             above_s, below_s, sums = lax.optimization_barrier((above_s, below_s, sums))
             first_q, last_q = pack_queries(stats, above_s, below_s, above_qg, below_qg, cols)
             side_qg = (left, right, shift(last_q, "cols", 1), shift(first_q, "cols", -1))
-    (sums,) = call(
-        key_side(rows, cols, width, False), [sum_out],
-        (tissue, *own_kv, above_kv, below_kv, above_qg, below_qg, above_s, below_s, sums),
-        flops=8 * pairs, exps=pairs // (4 * HEAD),
+    args = (*own_kv, above_kv, below_kv, above_qg, below_qg, above_s, below_s, sums)
+    sums, *inner = run(key_side(rows, cols, width, False), args, [], [sum_out, grid_out, grid_out], [], rows + 6, 0, 8)
+    args = (*own_kv, *near_kv[2:], *side_qg, sums, *inner, *parts)
+    grad_query, grad_key, grad_value, _ = run(
+        key_side(rows, cols, width, True), args, [grid_out] * 3, [sum_out],
+        [pltpu.VMEM(grid_out.shape, BF16)] * 2 + [pltpu.SemaphoreType.DMA((rows * cols + 2 + 4 * (width // LANES),))],
+        rows + 8, 3, 8,
     )
-    args = (tissue, *own_kv, *near_kv[2:], *side_qg, sums, *parts)
-    grad_query, grad_key, grad_value = pl.pallas_call(
-        key_side(rows, cols, width, True),
-        in_specs=[SMEM] + [VMEM] * (len(args) - 1),
-        out_specs=[hbm] * 3,
-        out_shape=[grid_out] * 3,
-        scratch_shapes=[pltpu.VMEM(sum_out.shape, F32)] + [pltpu.VMEM(grid_out.shape, BF16)] * 2
-        + [pltpu.SemaphoreType.DMA((rows + 2 * (width // LANES),))],
-        compiler_params=pltpu.CompilerParams(vmem_limit_bytes=LIMIT),
-        cost_estimate=pl.CostEstimate(flops=8 * pairs, transcendentals=pairs // (2 * HEAD), bytes_accessed=1 << 20),
-    )(*args)
-    return attended_out, grad_query, grad_key, grad_value
+    return attended, grad_query, grad_key, grad_value
 
 
 def solution(mesh):

time: 66.4 us -> 64.9 us (0.977)
  Pallas kernels: 26.7 us -> 23.5 us
  waiting for transfers between devices: 5.65 us -> 6.84 us
    pallas_call x9 -> x10, Pallas kernels: 24.2 us -> 21.1 us  [the longest x5 14 us: run(): pl.pallas_call(body, in_specs=[VMEM] * len(args), out_specs=[hbm] * len(h...]
    ppermute x12, waiting for transfers between devices: 5.65 us -> 6.84 us  [shift(): return lax.ppermute(array, axis, pairs)]
  transfers between devices with their start and end apart: 12 -> 12, of which waited for: 3 -> 4; matrix products, arithmetic and copies ran while one was open for 0% -> 0% of each run, Pallas kernels for 30% -> 26%
where the time goes in v5:
time: 64.9 us; the launch traced here: 64.4 us
  starting transfers between devices  33.1 us (51%)
  Pallas kernels  23.5 us (36%)
  waiting for transfers between devices  6.84 us (11%)
  between operations  0.99 us (2%)
    ppermute x12, starting transfers between devices, shift(): return lax.ppermute(array, axis, pairs)  33.1 us
    pallas_call x5, Pallas kernels, run(): pl.pallas_call(body, in_specs=[VMEM] * len(args), out_specs=[hbm] * len(h...  14 us
    pallas_call x5, Pallas kernels, call(): pl.pallas_call(body, in_specs=[VMEM] * len(args), out_specs=[VMEM] * len(...  7.07 us
    ppermute x12, waiting for transfers between devices, shift(): return lax.ppermute(array, axis, pairs)  6.84 us
    pallas_call x1, Pallas kernels, pack(): pl.pallas_call(body, in_specs=[SMEM] + [pl.BlockSpec(memory_space=pltpu.H...  2.4 us
  transfers between devices with their start and end apart: 12, of which 4 were waited for; matrix products, arithmetic and copies ran while one was open for 0% of the time, Pallas kernels for 26%

profile of v5, /device:TPU:1, one launch (start us, length us, event | category | flops | bytes accessed | tf_op | source)
XLA Modules:
  0.0 64.4 jit_solution(3419513336411168978)
XLA Ops:
  0.6 2.4 %shard_map.84 = (bf16[400,768]{1,0:T(8,128)(2,1)S(1)}, bf16[400,768]{1,0:T(8,128)(2,1)S(1)}, bf16[384,768]{1,0:T(8,128)(2,1)S(1)}, bf16[384,768]{1,0:T(8,128)(2,...) custom-call(s32[2,3]{1,0:T(2,128)} %mark_ref.1, bf16[16,24,768]{2,1,0:T(8,128)(2,1)} %refs_0_.1, ...), custom_call_target="tpu_custom_call" | custom-call | bytes 1048576 | tf_op jit(solution)/shard_map/pallas_call | solution.py:121
  3.0 4.1 %collective-permute-start = (bf16[400,768]{1,0:T(8,128)(2,1)S(1)}, bf16[400,768]{1,0:T(8,128)(2,1)S(1)}, u32[]{:S(2)}, u32[]{:S(2)}) collective-permute-start(bf16[400,768]{1,0:T(8,128)(2,1)S(1)} %get-tuple-element.47.refs_1_), channel_id=1, source_target_pairs={{0,4},{4,8},{8,12},{1,5},{5,9},{9,13},{2,6},{6,10},{10,14},{3,7},{... | collective-permute-start | bytes 1843208 | tf_op jit(solution)/shard_map/ppermute | solution.py:28
  7.1 1.3 %collective-permute-start.1 = (bf16[400,768]{1,0:T(8,128)(2,1)S(1)}, bf16[400,768]{1,0:T(8,128)(2,1)S(1)}, u32[]{:S(2)}, u32[]{:S(2)}) collective-permute-start(bf16[400,768]{1,0:T(8,128)(2,1)S(1)} %get-tuple-element.46.refs_0_), channel_id=1, source_target_pairs={{4,0},{8,4},{12,8},{5,1},{9,5},{13,9},{6,2},{10,6},{14,10},{7,3},{... | collective-permute-start | bytes 1843208 | tf_op jit(solution)/shard_map/ppermute | solution.py:28
  8.4 4.0 %collective-permute-start.2 = (bf16[528,768]{1,0:T(8,128)(2,1)S(1)}, bf16[528,768]{1,0:T(8,128)(2,1)S(1)}, u32[]{:S(2)}, u32[]{:S(2)}) collective-permute-start(bf16[528,768]{1,0:T(8,128)(2,1)S(1)} %get-tuple-element.54), channel_id=1, source_target_pairs={{0,1},{1,2},{2,3},{4,5},{5,6},{6,7},{8,9},{9,10},{10,11},{12,13},{... | collective-permute-start | bytes 2433032 | tf_op jit(solution)/shard_map/ppermute | solution.py:28
  12.4 1.9 %collective-permute-start.3 = (bf16[528,768]{1,0:T(8,128)(2,1)S(1)}, bf16[528,768]{1,0:T(8,128)(2,1)S(1)}, u32[]{:S(2)}, u32[]{:S(2)}) collective-permute-start(bf16[528,768]{1,0:T(8,128)(2,1)S(1)} %get-tuple-element.55), channel_id=1, source_target_pairs={{1,0},{2,1},{3,2},{5,4},{6,5},{7,6},{9,8},{10,9},{11,10},{13,12},{... | collective-permute-start | bytes 2433032 | tf_op jit(solution)/shard_map/ppermute | solution.py:28
  14.3 2.3 %shard_map.85 = (f32[384,768]{1,0:T(8,128)S(1)}, f32[12,768]{1,0:T(8,128)S(1)}) custom-call(bf16[400,768]{1,0:T(8,128)(2,1)S(1)} %get-tuple-element.46.refs_0_, bf16[400,768]{1,0:T(8,128)(2,1)S(1)} %get-tuple-element.47.refs_1_, bf16[384,768]{1,0:T(8,128)(2,1)S(1)} %get-tuple-element.74.refs_2_.refs_6_.refs_4_.refs_8_, ...), custom_call_target="tpu_custom_call" | custom-call | flops 10871635968 | bytes 2408448 | tf_op jit(solution)/shard_map/pallas_call | solution.py:45
  16.6 4.3 %collective-permute-start.8 = (bf16[384,768]{1,0:T(8,128)(2,1)S(1)}, bf16[384,768]{1,0:T(8,128)(2,1)S(1)}, u32[]{:S(2)}, u32[]{:S(2)}) collective-permute-start(bf16[384,768]{1,0:T(8,128)(2,1)S(1)} %get-tuple-element.73.refs_3_.refs_7_.refs_5_.refs_9_), channel_id=1, source_target_pairs={{0,4},{4,8},{8,12},{1,5},{5,9},{9,13},{2,6},{6,10},{10,14},{3,7},{... | collective-permute-start | bytes 1769480 | tf_op jit(solution)/shard_map/ppermute | solution.py:28
  20.9 0.0 collective-permute-done.above_ref.refs_2_
  20.9 1.3 %collective-permute-start.9 = (bf16[384,768]{1,0:T(8,128)(2,1)S(1)}, bf16[384,768]{1,0:T(8,128)(2,1)S(1)}, u32[]{:S(2)}, u32[]{:S(2)}) collective-permute-start(bf16[384,768]{1,0:T(8,128)(2,1)S(1)} %get-tuple-element.74.refs_2_.refs_6_.refs_4_.refs_8_), channel_id=1, source_target_pairs={{4,0},{8,4},{12,8},{5,1},{9,5},{13,9},{6,2},{10,6},{14,10},{7,3},{... | collective-permute-start | bytes 1769480 | tf_op jit(solution)/shard_map/ppermute | solution.py:28
  22.2 1.2 %collective-permute-done.1.below_ref.refs_3_ = bf16[400,768]{1,0:T(8,128)(2,1)S(1)} collective-permute-done((bf16[400,768]{1,0:T(8,128)(2,1)S(1)}, bf16[400,768]{1,0:T(8,128)(2,1)S(1)}, u32[]{:S(2)}, u32[]{:S(2)}) %collective-permute-start.1) | collective-permute-done | bytes 614432 | tf_op jit(solution)/shard_map/ppermute | solution.py:28
  23.4 0.1 shard_map.86
  23.5 4.9 %collective-permute-start.4 = (bf16[272,768]{1,0:T(8,128)(2,1)S(1)}, bf16[272,768]{1,0:T(8,128)(2,1)S(1)}, u32[]{:S(2)}, u32[]{:S(2)}) collective-permute-start(bf16[272,768]{1,0:T(8,128)(2,1)S(1)} %get-tuple-element.56), channel_id=1, source_target_pairs={{0,1},{1,2},{2,3},{4,5},{5,6},{6,7},{8,9},{9,10},{10,11},{12,13},{... | collective-permute-start | bytes 1253384 | tf_op jit(solution)/shard_map/ppermute | solution.py:28
  28.4 0.0 collective-permute-done.2.refs_4_.refs_2_.refs_6_
  28.4 1.9 %collective-permute-start.5 = (bf16[272,768]{1,0:T(8,128)(2,1)S(1)}, bf16[272,768]{1,0:T(8,128)(2,1)S(1)}, u32[]{:S(2)}, u32[]{:S(2)}) collective-permute-start(bf16[272,768]{1,0:T(8,128)(2,1)S(1)} %get-tuple-element.57), channel_id=1, source_target_pairs={{1,0},{2,1},{3,2},{5,4},{6,5},{7,6},{9,8},{10,9},{11,10},{13,12},{... | collective-permute-start | bytes 1253384 | tf_op jit(solution)/shard_map/ppermute | solution.py:28
  30.3 0.0 collective-permute-done.3.refs_5_.refs_3_.refs_7_
  30.3 2.8 %shard_map.87 = (f32[384,768]{1,0:T(8,128)S(1)}, f32[12,768]{1,0:T(8,128)S(1)}, bf16[16,24,768]{2,1,0:T(8,128)(2,1)S(1)}) custom-call(bf16[400,768]{1,0:T(8,128)(2,1)S(1)} %get-tuple-element.46.refs_0_, bf16[400,768]{1,0:T(8,128)(2,1)S(1)} %get-tuple-element.47.refs_1_, bf16[400,768]{1,0:T(8,128)(2,1)S(1)} %collective-permute-done.above_ref.refs_2_, ...), custom_call_target="tpu_custom_call" | custom-call | flops 10871635968 | bytes 6475776 | tf_op jit(solution)/shard_map/pallas_call | solution.py:45
  33.1 2.4 %shard_map.88 = (bf16[16,24,768]{2,1,0:T(8,128)(2,1)S(1)}, f32[2,384,768]{2,1,0:T(8,128)S(1)}) custom-call(bf16[400,768]{1,0:T(8,128)(2,1)S(1)} %get-tuple-element.46.refs_0_, bf16[400,768]{1,0:T(8,128)(2,1)S(1)} %get-tuple-element.47.refs_1_, bf16[400,768]{1,0:T(8,128)(2,1)S(1)} %collective-permute-done.above_ref.refs_2_, ...), custom_call_target="tpu_custom_call" | custom-call | flops 1358954496 | bytes 1048576 | tf_op jit(solution)/shard_map/pallas_call | solution.py:604
  35.5 0.0 collective-permute-done.4.refs_2_.refs_6_.refs_4_
  35.5 2.5 %collective-permute-done.5.refs_3_.refs_7_.refs_5_ = bf16[272,768]{1,0:T(8,128)(2,1)S(1)} collective-permute-done((bf16[272,768]{1,0:T(8,128)(2,1)S(1)}, bf16[272,768]{1,0:T(8,128)(2,1)S(1)}, u32[]{:S(2)}, u32[]{:S(2)}) %collective-permute-start.5) | collective-permute-done | bytes 417824 | tf_op jit(solution)/shard_map/ppermute | solution.py:28
  38.0 1.8 %shard_map.89 = (bf16[16,24,768]{2,1,0:T(8,128)(2,1)S(1)}, f32[6,768]{1,0:T(8,128)S(1)}, f32[6,768]{1,0:T(8,128)S(1)}) custom-call(bf16[400,768]{1,0:T(8,128)(2,1)S(1)} %get-tuple-element.46.refs_0_, bf16[400,768]{1,0:T(8,128)(2,1)S(1)} %get-tuple-element.47.refs_1_, bf16[272,768]{1,0:T(8,128)(2,1)S(1)} %collective-permute-done.4.refs_2_.refs_6_.refs_4_, ...), custom_call_target="tpu_custom_call" | custom-call | flops 679477248 | bytes 4460544 | tf_op jit(solution)/shard_map/pallas_call | solution.py:45
  39.9 3.2 %collective-permute-start.6 = (f32[6,768]{1,0:T(8,128)S(1)}, f32[6,768]{1,0:T(8,128)S(1)}, u32[]{:S(2)}, u32[]{:S(2)}) collective-permute-start(f32[6,768]{1,0:T(8,128)S(1)} %get-tuple-element.65.refs_11_.refs_1_), channel_id=1, source_target_pairs={{0,4},{4,8},{8,12},{1,5},{5,9},{9,13},{2,6},{6,10},{10,14},{3,7},{... | collective-permute-start | bytes 55304 | tf_op jit(solution)/shard_map/ppermute | solution.py:28
  43.0 1.5 %collective-permute-start.7 = (f32[6,768]{1,0:T(8,128)S(1)}, f32[6,768]{1,0:T(8,128)S(1)}, u32[]{:S(2)}, u32[]{:S(2)}) collective-permute-start(f32[6,768]{1,0:T(8,128)S(1)} %get-tuple-element.64.refs_10_.refs_0_), channel_id=1, source_target_pairs={{4,0},{8,4},{12,8},{5,1},{9,5},{13,9},{6,2},{10,6},{14,10},{7,3},{... | collective-permute-start | bytes 55304 | tf_op jit(solution)/shard_map/ppermute | solution.py:28
  44.5 2.9 %shard_map.90 = (bf16[16,24,768]{2,1,0:T(8,128)(2,1)}, bf16[16,24,768]{2,1,0:T(8,128)(2,1)S(1)}, f32[2,384,768]{2,1,0:T(8,128)S(1)}) custom-call(bf16[400,768]{1,0:T(8,128)(2,1)S(1)} %get-tuple-element.46.refs_0_, bf16[400,768]{1,0:T(8,128)(2,1)S(1)} %get-tuple-element.47.refs_1_, ...), custom_call_target="tpu_custom_call", output_to_operand_aliasing={{2}: (12, {})} | custom-call | flops 2717908992 | bytes 1048576 | tf_op jit(solution)/shard_map/pallas_call | solution.py:604
  47.4 0.0 collective-permute-done.6.refs_2_.refs_6_
  47.4 0.2 collective-permute-done.7.refs_3_.refs_7_
  47.6 0.0 collective-permute-done.8.refs_4_
  47.6 0.0 collective-permute-done.9.refs_5_
  47.6 0.1 shard_map.91
  47.7 2.9 %collective-permute-start.10 = (bf16[288,768]{1,0:T(8,128)(2,1)S(1)}, bf16[288,768]{1,0:T(8,128)(2,1)S(1)}, u32[]{:S(2)}, u32[]{:S(2)}) collective-permute-start(bf16[288,768]{1,0:T(8,128)(2,1)S(1)} %get-tuple-element.75), channel_id=1, source_target_pairs={{0,1},{1,2},{2,3},{4,5},{5,6},{6,7},{8,9},{9,10},{10,11},{12,13},{... | collective-permute-start | bytes 1327112 | tf_op jit(solution)/shard_map/ppermute | solution.py:28
  50.6 1.9 %collective-permute-start.11 = (bf16[288,768]{1,0:T(8,128)(2,1)S(1)}, bf16[288,768]{1,0:T(8,128)(2,1)S(1)}, u32[]{:S(2)}, u32[]{:S(2)}) collective-permute-start(bf16[288,768]{1,0:T(8,128)(2,1)S(1)} %get-tuple-element.76), channel_id=1, source_target_pairs={{1,0},{2,1},{3,2},{5,4},{6,5},{7,6},{9,8},{10,9},{11,10},{13,12},{... | collective-permute-start | bytes 1327112 | tf_op jit(solution)/shard_map/ppermute | solution.py:28
  52.5 2.3 %shard_map.92 = (bf16[16,24,768]{2,1,0:T(8,128)(2,1)S(1)}, f32[2,384,768]{2,1,0:T(8,128)S(1)}) custom-call(bf16[400,768]{1,0:T(8,128)(2,1)S(1)} %get-tuple-element.46.refs_0_, bf16[400,768]{1,0:T(8,128)(2,1)S(1)} %get-tuple-element.47.refs_1_, bf16[400,768]{1,0:T(8,128)(2,1)S(1)} %collective-permute-done.above_ref.refs_2_, ...), custom_call_target="tpu_custom_call", output_to_operand_aliasing={{1}: (12, {})} | custom-call | flops 2717908992 | bytes 1048576 | tf_op jit(solution)/shard_map/pallas_call | solution.py:604
  54.8 2.5 %shard_map.93 = (f32[2,384,768]{2,1,0:T(8,128)S(1)}, bf16[16,24,768]{2,1,0:T(8,128)(2,1)S(1)}, bf16[16,24,768]{2,1,0:T(8,128)(2,1)S(1)}) custom-call(bf16[400,768]{1,0:T(8,128)(2,1)S(1)} %get-tuple-element.46.refs_0_, bf16[400,768]{1,0:T(8,128)(2,1)S(1)} %get-tuple-element.47.refs_1_, ...), custom_call_target="tpu_custom_call", output_to_operand_aliasing={{0}: (8, {})} | custom-call | flops 1358954496 | bytes 1048576 | tf_op jit(solution)/shard_map/pallas_call | solution.py:604
  57.3 0.0 collective-permute-done.10.refs_8_
  57.3 2.9 %collective-permute-done.11.refs_9_ = bf16[288,768]{1,0:T(8,128)(2,1)S(1)} collective-permute-done((bf16[288,768]{1,0:T(8,128)(2,1)S(1)}, bf16[288,768]{1,0:T(8,128)(2,1)S(1)}, u32[]{:S(2)}, u32[]{:S(2)}) %collective-permute-start.11) | collective-permute-done | bytes 442400 | tf_op jit(solution)/shard_map/ppermute | solution.py:28
  60.2 4.0 %shard_map.94 = (bf16[16,24,768]{2,1,0:T(8,128)(2,1)}, bf16[16,24,768]{2,1,0:T(8,128)(2,1)}, bf16[16,24,768]{2,1,0:T(8,128)(2,1)}, f32[2,384,768]{2,1,0:T(8,128)S(1)}) custom-call(bf16[400,768]{1,0:T(8,128)(2,1)S(1)} %get-tuple-element.46.refs_0_, bf16[400,768]{1,0:T(8,128)(2,1)S(1)} %get-tuple-element.47.refs_1_, ...), custom_call_target="tpu_custom_call", output_to_operand_aliasing={{3}: (10, {})} | custom-call | flops 1358954496 | bytes 1048576 | tf_op jit(solution)/shard_map/pallas_call | solution.py:604
Async XLA Ops:
  3.0 17.8 %collective-permute-start = (bf16[400,768]{1,0:T(8,128)(2,1)S(1)}, bf16[400,768]{1,0:T(8,128)(2,1)S(1)}, u32[]{:S(2)}, u32[]{:S(2)}) collective-permute-start(bf16[400,768]{1,0:T(8,128)(2,1)S(1)} %get-tuple-element.47.refs_1_), channel_id=1, source_target_pairs={{0,4},{4,8},{8,12},{1,5},{5,9},{9,13},{2,6},{6,10},{10,14},{3,7},{... | collective-permute-start | bytes 1843208 | tf_op jit(solution)/shard_map/ppermute | solution.py:28
  7.1 16.3 %collective-permute-start.1 = (bf16[400,768]{1,0:T(8,128)(2,1)S(1)}, bf16[400,768]{1,0:T(8,128)(2,1)S(1)}, u32[]{:S(2)}, u32[]{:S(2)}) collective-permute-start(bf16[400,768]{1,0:T(8,128)(2,1)S(1)} %get-tuple-element.46.refs_0_), channel_id=1, source_target_pairs={{4,0},{8,4},{12,8},{5,1},{9,5},{13,9},{6,2},{10,6},{14,10},{7,3},{... | collective-permute-start | bytes 1843208 | tf_op jit(solution)/shard_map/ppermute | solution.py:28
  8.4 19.9 %collective-permute-start.2 = (bf16[528,768]{1,0:T(8,128)(2,1)S(1)}, bf16[528,768]{1,0:T(8,128)(2,1)S(1)}, u32[]{:S(2)}, u32[]{:S(2)}) collective-permute-start(bf16[528,768]{1,0:T(8,128)(2,1)S(1)} %get-tuple-element.54), channel_id=1, source_target_pairs={{0,1},{1,2},{2,3},{4,5},{5,6},{6,7},{8,9},{9,10},{10,11},{12,13},{... | collective-permute-start | bytes 2433032 | tf_op jit(solution)/shard_map/ppermute | solution.py:28
  12.4 17.9 %collective-permute-start.3 = (bf16[528,768]{1,0:T(8,128)(2,1)S(1)}, bf16[528,768]{1,0:T(8,128)(2,1)S(1)}, u32[]{:S(2)}, u32[]{:S(2)}) collective-permute-start(bf16[528,768]{1,0:T(8,128)(2,1)S(1)} %get-tuple-element.55), channel_id=1, source_target_pairs={{1,0},{2,1},{3,2},{5,4},{6,5},{7,6},{9,8},{10,9},{11,10},{13,12},{... | collective-permute-start | bytes 2433032 | tf_op jit(solution)/shard_map/ppermute | solution.py:28
  16.6 31.0 %collective-permute-start.8 = (bf16[384,768]{1,0:T(8,128)(2,1)S(1)}, bf16[384,768]{1,0:T(8,128)(2,1)S(1)}, u32[]{:S(2)}, u32[]{:S(2)}) collective-permute-start(bf16[384,768]{1,0:T(8,128)(2,1)S(1)} %get-tuple-element.73.refs_3_.refs_7_.refs_5_.refs_9_), channel_id=1, source_target_pairs={{0,4},{4,8},{8,12},{1,5},{5,9},{9,13},{2,6},{6,10},{10,14},{3,7},{... | collective-permute-start | bytes 1769480 | tf_op jit(solution)/shard_map/ppermute | solution.py:28
  20.9 26.7 %collective-permute-start.9 = (bf16[384,768]{1,0:T(8,128)(2,1)S(1)}, bf16[384,768]{1,0:T(8,128)(2,1)S(1)}, u32[]{:S(2)}, u32[]{:S(2)}) collective-permute-start(bf16[384,768]{1,0:T(8,128)(2,1)S(1)} %get-tuple-element.74.refs_2_.refs_6_.refs_4_.refs_8_), channel_id=1, source_target_pairs={{4,0},{8,4},{12,8},{5,1},{9,5},{13,9},{6,2},{10,6},{14,10},{7,3},{... | collective-permute-start | bytes 1769480 | tf_op jit(solution)/shard_map/ppermute | solution.py:28
  23.5 12.0 %collective-permute-start.4 = (bf16[272,768]{1,0:T(8,128)(2,1)S(1)}, bf16[272,768]{1,0:T(8,128)(2,1)S(1)}, u32[]{:S(2)}, u32[]{:S(2)}) collective-permute-start(bf16[272,768]{1,0:T(8,128)(2,1)S(1)} %get-tuple-element.56), channel_id=1, source_target_pairs={{0,1},{1,2},{2,3},{4,5},{5,6},{6,7},{8,9},{9,10},{10,11},{12,13},{... | collective-permute-start | bytes 1253384 | tf_op jit(solution)/shard_map/ppermute | solution.py:28
  28.4 9.7 %collective-permute-start.5 = (bf16[272,768]{1,0:T(8,128)(2,1)S(1)}, bf16[272,768]{1,0:T(8,128)(2,1)S(1)}, u32[]{:S(2)}, u32[]{:S(2)}) collective-permute-start(bf16[272,768]{1,0:T(8,128)(2,1)S(1)} %get-tuple-element.57), channel_id=1, source_target_pairs={{1,0},{2,1},{3,2},{5,4},{6,5},{7,6},{9,8},{10,9},{11,10},{13,12},{... | collective-permute-start | bytes 1253384 | tf_op jit(solution)/shard_map/ppermute | solution.py:28
  39.9 7.5 %collective-permute-start.6 = (f32[6,768]{1,0:T(8,128)S(1)}, f32[6,768]{1,0:T(8,128)S(1)}, u32[]{:S(2)}, u32[]{:S(2)}) collective-permute-start(f32[6,768]{1,0:T(8,128)S(1)} %get-tuple-element.65.refs_11_.refs_1_), channel_id=1, source_target_pairs={{0,4},{4,8},{8,12},{1,5},{5,9},{9,13},{2,6},{6,10},{10,14},{3,7},{... | collective-permute-start | bytes 55304 | tf_op jit(solution)/shard_map/ppermute | solution.py:28
  43.0 4.6 %collective-permute-start.7 = (f32[6,768]{1,0:T(8,128)S(1)}, f32[6,768]{1,0:T(8,128)S(1)}, u32[]{:S(2)}, u32[]{:S(2)}) collective-permute-start(f32[6,768]{1,0:T(8,128)S(1)} %get-tuple-element.64.refs_10_.refs_0_), channel_id=1, source_target_pairs={{4,0},{8,4},{12,8},{5,1},{9,5},{13,9},{6,2},{10,6},{14,10},{7,3},{... | collective-permute-start | bytes 55304 | tf_op jit(solution)/shard_map/ppermute | solution.py:28
  47.7 9.6 %collective-permute-start.10 = (bf16[288,768]{1,0:T(8,128)(2,1)S(1)}, bf16[288,768]{1,0:T(8,128)(2,1)S(1)}, u32[]{:S(2)}, u32[]{:S(2)}) collective-permute-start(bf16[288,768]{1,0:T(8,128)(2,1)S(1)} %get-tuple-element.75), channel_id=1, source_target_pairs={{0,1},{1,2},{2,3},{4,5},{5,6},{6,7},{8,9},{9,10},{10,11},{12,13},{... | collective-permute-start | bytes 1327112 | tf_op jit(solution)/shard_map/ppermute | solution.py:28
  50.6 9.6 %collective-permute-start.11 = (bf16[288,768]{1,0:T(8,128)(2,1)S(1)}, bf16[288,768]{1,0:T(8,128)(2,1)S(1)}, u32[]{:S(2)}, u32[]{:S(2)}) collective-permute-start(bf16[288,768]{1,0:T(8,128)(2,1)S(1)} %get-tuple-element.76), channel_id=1, source_target_pairs={{1,0},{2,1},{3,2},{5,4},{6,5},{7,6},{9,8},{10,9},{11,10},{13,12},{... | collective-permute-start | bytes 1327112 | tf_op jit(solution)/shard_map/ppermute | solution.py:28

commit v6 on v5

--- a/solution.py
+++ b/solution.py
@@ -82,10 +82,10 @@
     rows, cols = tissue.shape
     width = grids[0].shape[-1]
 
-    def body(mark_ref, *refs):
+    def body(mark_hbm, *refs):
         sources, refs = refs[:4], refs[4:]
         kv_refs, qg_refs, side_refs = refs[:rows], refs[rows : 2 * rows], refs[2 * rows : 2 * rows + 2]
-        grid_refs, sems = refs[2 * rows + 2 : 2 * rows + 6], refs[2 * rows + 6]
+        grid_refs, (sems, mark_ref, mark_sem) = refs[2 * rows + 2 : 2 * rows + 6], refs[2 * rows + 6 :]
 
         copies = [
             [
@@ -98,6 +98,9 @@
         ]
         for copy in sum(copies, []):
             copy.start()
+        marks = pltpu.make_async_copy(mark_hbm, mark_ref, mark_sem)
+        marks.start()
+        marks.wait()
         for n, ref in enumerate(grid_refs):
             for a in range(rows):
                 copies[n][a].wait()
@@ -120,10 +123,11 @@
     shapes = [jax.ShapeDtypeStruct((height, width), BF16) for height in shapes]
     outs = pl.pallas_call(
         body,
-        in_specs=[SMEM] + [pl.BlockSpec(memory_space=pltpu.HBM)] * 4,
+        in_specs=[pl.BlockSpec(memory_space=pltpu.HBM)] * 5,
         out_specs=[VMEM] * len(shapes),
         out_shape=shapes,
-        scratch_shapes=[pltpu.VMEM(grid.shape, grid.dtype) for grid in grids] + [pltpu.SemaphoreType.DMA((4, rows))],
+        scratch_shapes=[pltpu.VMEM(grid.shape, grid.dtype) for grid in grids] + [pltpu.SemaphoreType.DMA((4, rows))]
+        + [pltpu.SMEM(tissue.shape, jnp.int32), pltpu.SemaphoreType.DMA],
         compiler_params=pltpu.CompilerParams(vmem_limit_bytes=LIMIT),
         cost_estimate=pl.CostEstimate(flops=0, transcendentals=0, bytes_accessed=1 << 20),
     )(*(pltpu.with_memory_space_constraint(array, pltpu.HBM) for array in (tissue, *grids)))

time: 64.9 us -> 64.2 us (0.989)
  Pallas kernels: 23.5 us -> 22.8 us
    pallas_call x1, Pallas kernels: 2.4 us -> 1.72 us  [pack(): pl.pallas_call(body, in_specs=[pl.BlockSpec(memory_space=pltpu.HBM)] * 5,...]
  transfers between devices with their start and end apart: 12 -> 12, of which waited for: 4 -> 4; matrix products, arithmetic and copies ran while one was open for 0% -> 0% of each run, Pallas kernels for 26% -> 27%
where the time goes in v6:
time: 64.2 us; the launch traced here: 63.7 us
  starting transfers between devices  33.1 us (52%)
  Pallas kernels  22.8 us (36%)
  waiting for transfers between devices  6.85 us (11%)
  between operations  0.99 us (2%)
    ppermute x12, starting transfers between devices, shift(): return lax.ppermute(array, axis, pairs)  33.1 us
    pallas_call x5, Pallas kernels, run(): pl.pallas_call(body, in_specs=[VMEM] * len(args), out_specs=[hbm] * len(h...  14 us
    pallas_call x5, Pallas kernels, call(): pl.pallas_call(body, in_specs=[VMEM] * len(args), out_specs=[VMEM] * len(...  7.06 us
    ppermute x12, waiting for transfers between devices, shift(): return lax.ppermute(array, axis, pairs)  6.85 us
    pallas_call x1, Pallas kernels, pack(): pl.pallas_call(body, in_specs=[pl.BlockSpec(memory_space=pltpu.HBM)] * 5,...  1.72 us
  transfers between devices with their start and end apart: 12, of which 4 were waited for; matrix products, arithmetic and copies ran while one was open for 0% of the time, Pallas kernels for 27%

profile of v6, /device:TPU:1, one launch (start us, length us, event | category | flops | bytes accessed | tf_op | source)
XLA Modules:
  0.0 63.7 jit_solution(2223931040272848793)
XLA Ops:
  0.6 1.7 %shard_map.84 = (bf16[400,768]{1,0:T(8,128)(2,1)S(1)}, bf16[400,768]{1,0:T(8,128)(2,1)S(1)}, bf16[384,768]{1,0:T(8,128)(2,1)S(1)}, bf16[384,768]{1,0:T(8,128)(2,...) custom-call(s32[2,3]{1,0:T(2,128)} %mark_hbm.1, bf16[16,24,768]{2,1,0:T(8,128)(2,1)} %refs_0_.1, ...), custom_call_target="tpu_custom_call" | custom-call | bytes 1048576 | tf_op jit(solution)/shard_map/pallas_call | solution.py:124
  2.4 4.1 %collective-permute-start = (bf16[400,768]{1,0:T(8,128)(2,1)S(1)}, bf16[400,768]{1,0:T(8,128)(2,1)S(1)}, u32[]{:S(2)}, u32[]{:S(2)}) collective-permute-start(bf16[400,768]{1,0:T(8,128)(2,1)S(1)} %get-tuple-element.47.refs_1_), channel_id=1, source_target_pairs={{0,4},{4,8},{8,12},{1,5},{5,9},{9,13},{2,6},{6,10},{10,14},{3,7},{... | collective-permute-start | bytes 1843208 | tf_op jit(solution)/shard_map/ppermute | solution.py:28
  6.4 1.3 %collective-permute-start.1 = (bf16[400,768]{1,0:T(8,128)(2,1)S(1)}, bf16[400,768]{1,0:T(8,128)(2,1)S(1)}, u32[]{:S(2)}, u32[]{:S(2)}) collective-permute-start(bf16[400,768]{1,0:T(8,128)(2,1)S(1)} %get-tuple-element.46.refs_0_), channel_id=1, source_target_pairs={{4,0},{8,4},{12,8},{5,1},{9,5},{13,9},{6,2},{10,6},{14,10},{7,3},{... | collective-permute-start | bytes 1843208 | tf_op jit(solution)/shard_map/ppermute | solution.py:28
  7.7 4.0 %collective-permute-start.2 = (bf16[528,768]{1,0:T(8,128)(2,1)S(1)}, bf16[528,768]{1,0:T(8,128)(2,1)S(1)}, u32[]{:S(2)}, u32[]{:S(2)}) collective-permute-start(bf16[528,768]{1,0:T(8,128)(2,1)S(1)} %get-tuple-element.54), channel_id=1, source_target_pairs={{0,1},{1,2},{2,3},{4,5},{5,6},{6,7},{8,9},{9,10},{10,11},{12,13},{... | collective-permute-start | bytes 2433032 | tf_op jit(solution)/shard_map/ppermute | solution.py:28
  11.7 1.9 %collective-permute-start.3 = (bf16[528,768]{1,0:T(8,128)(2,1)S(1)}, bf16[528,768]{1,0:T(8,128)(2,1)S(1)}, u32[]{:S(2)}, u32[]{:S(2)}) collective-permute-start(bf16[528,768]{1,0:T(8,128)(2,1)S(1)} %get-tuple-element.55), channel_id=1, source_target_pairs={{1,0},{2,1},{3,2},{5,4},{6,5},{7,6},{9,8},{10,9},{11,10},{13,12},{... | collective-permute-start | bytes 2433032 | tf_op jit(solution)/shard_map/ppermute | solution.py:28
  13.6 2.3 %shard_map.85 = (f32[384,768]{1,0:T(8,128)S(1)}, f32[12,768]{1,0:T(8,128)S(1)}) custom-call(bf16[400,768]{1,0:T(8,128)(2,1)S(1)} %get-tuple-element.46.refs_0_, bf16[400,768]{1,0:T(8,128)(2,1)S(1)} %get-tuple-element.47.refs_1_, bf16[384,768]{1,0:T(8,128)(2,1)S(1)} %get-tuple-element.74.refs_2_.refs_6_.refs_4_.refs_8_, ...), custom_call_target="tpu_custom_call" | custom-call | flops 10871635968 | bytes 2408448 | tf_op jit(solution)/shard_map/pallas_call | solution.py:45
  15.9 4.3 %collective-permute-start.8 = (bf16[384,768]{1,0:T(8,128)(2,1)S(1)}, bf16[384,768]{1,0:T(8,128)(2,1)S(1)}, u32[]{:S(2)}, u32[]{:S(2)}) collective-permute-start(bf16[384,768]{1,0:T(8,128)(2,1)S(1)} %get-tuple-element.73.refs_3_.refs_7_.refs_5_.refs_9_), channel_id=1, source_target_pairs={{0,4},{4,8},{8,12},{1,5},{5,9},{9,13},{2,6},{6,10},{10,14},{3,7},{... | collective-permute-start | bytes 1769480 | tf_op jit(solution)/shard_map/ppermute | solution.py:28
  20.2 0.0 collective-permute-done.above_ref.refs_2_
  20.2 1.3 %collective-permute-start.9 = (bf16[384,768]{1,0:T(8,128)(2,1)S(1)}, bf16[384,768]{1,0:T(8,128)(2,1)S(1)}, u32[]{:S(2)}, u32[]{:S(2)}) collective-permute-start(bf16[384,768]{1,0:T(8,128)(2,1)S(1)} %get-tuple-element.74.refs_2_.refs_6_.refs_4_.refs_8_), channel_id=1, source_target_pairs={{4,0},{8,4},{12,8},{5,1},{9,5},{13,9},{6,2},{10,6},{14,10},{7,3},{... | collective-permute-start | bytes 1769480 | tf_op jit(solution)/shard_map/ppermute | solution.py:28
  21.5 1.2 %collective-permute-done.1.below_ref.refs_3_ = bf16[400,768]{1,0:T(8,128)(2,1)S(1)} collective-permute-done((bf16[400,768]{1,0:T(8,128)(2,1)S(1)}, bf16[400,768]{1,0:T(8,128)(2,1)S(1)}, u32[]{:S(2)}, u32[]{:S(2)}) %collective-permute-start.1) | collective-permute-done | bytes 614432 | tf_op jit(solution)/shard_map/ppermute | solution.py:28
  22.7 0.1 shard_map.86
  22.8 4.9 %collective-permute-start.4 = (bf16[272,768]{1,0:T(8,128)(2,1)S(1)}, bf16[272,768]{1,0:T(8,128)(2,1)S(1)}, u32[]{:S(2)}, u32[]{:S(2)}) collective-permute-start(bf16[272,768]{1,0:T(8,128)(2,1)S(1)} %get-tuple-element.56), channel_id=1, source_target_pairs={{0,1},{1,2},{2,3},{4,5},{5,6},{6,7},{8,9},{9,10},{10,11},{12,13},{... | collective-permute-start | bytes 1253384 | tf_op jit(solution)/shard_map/ppermute | solution.py:28
  27.7 0.0 collective-permute-done.2.refs_4_.refs_2_.refs_6_
  27.7 1.9 %collective-permute-start.5 = (bf16[272,768]{1,0:T(8,128)(2,1)S(1)}, bf16[272,768]{1,0:T(8,128)(2,1)S(1)}, u32[]{:S(2)}, u32[]{:S(2)}) collective-permute-start(bf16[272,768]{1,0:T(8,128)(2,1)S(1)} %get-tuple-element.57), channel_id=1, source_target_pairs={{1,0},{2,1},{3,2},{5,4},{6,5},{7,6},{9,8},{10,9},{11,10},{13,12},{... | collective-permute-start | bytes 1253384 | tf_op jit(solution)/shard_map/ppermute | solution.py:28
  29.6 0.0 collective-permute-done.3.refs_5_.refs_3_.refs_7_
  29.6 2.8 %shard_map.87 = (f32[384,768]{1,0:T(8,128)S(1)}, f32[12,768]{1,0:T(8,128)S(1)}, bf16[16,24,768]{2,1,0:T(8,128)(2,1)S(1)}) custom-call(bf16[400,768]{1,0:T(8,128)(2,1)S(1)} %get-tuple-element.46.refs_0_, bf16[400,768]{1,0:T(8,128)(2,1)S(1)} %get-tuple-element.47.refs_1_, bf16[400,768]{1,0:T(8,128)(2,1)S(1)} %collective-permute-done.above_ref.refs_2_, ...), custom_call_target="tpu_custom_call" | custom-call | flops 10871635968 | bytes 6475776 | tf_op jit(solution)/shard_map/pallas_call | solution.py:45
  32.5 2.4 %shard_map.88 = (bf16[16,24,768]{2,1,0:T(8,128)(2,1)S(1)}, f32[2,384,768]{2,1,0:T(8,128)S(1)}) custom-call(bf16[400,768]{1,0:T(8,128)(2,1)S(1)} %get-tuple-element.46.refs_0_, bf16[400,768]{1,0:T(8,128)(2,1)S(1)} %get-tuple-element.47.refs_1_, bf16[400,768]{1,0:T(8,128)(2,1)S(1)} %collective-permute-done.above_ref.refs_2_, ...), custom_call_target="tpu_custom_call" | custom-call | flops 1358954496 | bytes 1048576 | tf_op jit(solution)/shard_map/pallas_call | solution.py:608
  34.8 0.0 collective-permute-done.4.refs_2_.refs_6_.refs_4_
  34.8 2.5 %collective-permute-done.5.refs_3_.refs_7_.refs_5_ = bf16[272,768]{1,0:T(8,128)(2,1)S(1)} collective-permute-done((bf16[272,768]{1,0:T(8,128)(2,1)S(1)}, bf16[272,768]{1,0:T(8,128)(2,1)S(1)}, u32[]{:S(2)}, u32[]{:S(2)}) %collective-permute-start.5) | collective-permute-done | bytes 417824 | tf_op jit(solution)/shard_map/ppermute | solution.py:28
  37.3 1.9 %shard_map.89 = (bf16[16,24,768]{2,1,0:T(8,128)(2,1)S(1)}, f32[6,768]{1,0:T(8,128)S(1)}, f32[6,768]{1,0:T(8,128)S(1)}) custom-call(bf16[400,768]{1,0:T(8,128)(2,1)S(1)} %get-tuple-element.46.refs_0_, bf16[400,768]{1,0:T(8,128)(2,1)S(1)} %get-tuple-element.47.refs_1_, bf16[272,768]{1,0:T(8,128)(2,1)S(1)} %collective-permute-done.4.refs_2_.refs_6_.refs_4_, ...), custom_call_target="tpu_custom_call" | custom-call | flops 679477248 | bytes 4460544 | tf_op jit(solution)/shard_map/pallas_call | solution.py:45
  39.2 3.2 %collective-permute-start.6 = (f32[6,768]{1,0:T(8,128)S(1)}, f32[6,768]{1,0:T(8,128)S(1)}, u32[]{:S(2)}, u32[]{:S(2)}) collective-permute-start(f32[6,768]{1,0:T(8,128)S(1)} %get-tuple-element.65.refs_11_.refs_1_), channel_id=1, source_target_pairs={{0,4},{4,8},{8,12},{1,5},{5,9},{9,13},{2,6},{6,10},{10,14},{3,7},{... | collective-permute-start | bytes 55304 | tf_op jit(solution)/shard_map/ppermute | solution.py:28
  42.4 1.5 %collective-permute-start.7 = (f32[6,768]{1,0:T(8,128)S(1)}, f32[6,768]{1,0:T(8,128)S(1)}, u32[]{:S(2)}, u32[]{:S(2)}) collective-permute-start(f32[6,768]{1,0:T(8,128)S(1)} %get-tuple-element.64.refs_10_.refs_0_), channel_id=1, source_target_pairs={{4,0},{8,4},{12,8},{5,1},{9,5},{13,9},{6,2},{10,6},{14,10},{7,3},{... | collective-permute-start | bytes 55304 | tf_op jit(solution)/shard_map/ppermute | solution.py:28
  43.8 2.9 %shard_map.90 = (bf16[16,24,768]{2,1,0:T(8,128)(2,1)}, bf16[16,24,768]{2,1,0:T(8,128)(2,1)S(1)}, f32[2,384,768]{2,1,0:T(8,128)S(1)}) custom-call(bf16[400,768]{1,0:T(8,128)(2,1)S(1)} %get-tuple-element.46.refs_0_, bf16[400,768]{1,0:T(8,128)(2,1)S(1)} %get-tuple-element.47.refs_1_, ...), custom_call_target="tpu_custom_call", output_to_operand_aliasing={{2}: (12, {})} | custom-call | flops 2717908992 | bytes 1048576 | tf_op jit(solution)/shard_map/pallas_call | solution.py:608
  46.7 0.0 collective-permute-done.6.refs_2_.refs_6_
  46.7 0.2 collective-permute-done.7.refs_3_.refs_7_
  46.9 0.0 collective-permute-done.8.refs_4_
  46.9 0.0 collective-permute-done.9.refs_5_
  46.9 0.1 shard_map.91
  47.0 2.9 %collective-permute-start.10 = (bf16[288,768]{1,0:T(8,128)(2,1)S(1)}, bf16[288,768]{1,0:T(8,128)(2,1)S(1)}, u32[]{:S(2)}, u32[]{:S(2)}) collective-permute-start(bf16[288,768]{1,0:T(8,128)(2,1)S(1)} %get-tuple-element.75), channel_id=1, source_target_pairs={{0,1},{1,2},{2,3},{4,5},{5,6},{6,7},{8,9},{9,10},{10,11},{12,13},{... | collective-permute-start | bytes 1327112 | tf_op jit(solution)/shard_map/ppermute | solution.py:28
  49.9 1.9 %collective-permute-start.11 = (bf16[288,768]{1,0:T(8,128)(2,1)S(1)}, bf16[288,768]{1,0:T(8,128)(2,1)S(1)}, u32[]{:S(2)}, u32[]{:S(2)}) collective-permute-start(bf16[288,768]{1,0:T(8,128)(2,1)S(1)} %get-tuple-element.76), channel_id=1, source_target_pairs={{1,0},{2,1},{3,2},{5,4},{6,5},{7,6},{9,8},{10,9},{11,10},{13,12},{... | collective-permute-start | bytes 1327112 | tf_op jit(solution)/shard_map/ppermute | solution.py:28
  51.8 2.3 %shard_map.92 = (bf16[16,24,768]{2,1,0:T(8,128)(2,1)S(1)}, f32[2,384,768]{2,1,0:T(8,128)S(1)}) custom-call(bf16[400,768]{1,0:T(8,128)(2,1)S(1)} %get-tuple-element.46.refs_0_, bf16[400,768]{1,0:T(8,128)(2,1)S(1)} %get-tuple-element.47.refs_1_, bf16[400,768]{1,0:T(8,128)(2,1)S(1)} %collective-permute-done.above_ref.refs_2_, ...), custom_call_target="tpu_custom_call", output_to_operand_aliasing={{1}: (12, {})} | custom-call | flops 2717908992 | bytes 1048576 | tf_op jit(solution)/shard_map/pallas_call | solution.py:608
  54.1 2.5 %shard_map.93 = (f32[2,384,768]{2,1,0:T(8,128)S(1)}, bf16[16,24,768]{2,1,0:T(8,128)(2,1)S(1)}, bf16[16,24,768]{2,1,0:T(8,128)(2,1)S(1)}) custom-call(bf16[400,768]{1,0:T(8,128)(2,1)S(1)} %get-tuple-element.46.refs_0_, bf16[400,768]{1,0:T(8,128)(2,1)S(1)} %get-tuple-element.47.refs_1_, ...), custom_call_target="tpu_custom_call", output_to_operand_aliasing={{0}: (8, {})} | custom-call | flops 1358954496 | bytes 1048576 | tf_op jit(solution)/shard_map/pallas_call | solution.py:608
  56.6 0.0 collective-permute-done.10.refs_8_
  56.6 2.9 %collective-permute-done.11.refs_9_ = bf16[288,768]{1,0:T(8,128)(2,1)S(1)} collective-permute-done((bf16[288,768]{1,0:T(8,128)(2,1)S(1)}, bf16[288,768]{1,0:T(8,128)(2,1)S(1)}, u32[]{:S(2)}, u32[]{:S(2)}) %collective-permute-start.11) | collective-permute-done | bytes 442400 | tf_op jit(solution)/shard_map/ppermute | solution.py:28
  59.5 4.0 %shard_map.94 = (bf16[16,24,768]{2,1,0:T(8,128)(2,1)}, bf16[16,24,768]{2,1,0:T(8,128)(2,1)}, bf16[16,24,768]{2,1,0:T(8,128)(2,1)}, f32[2,384,768]{2,1,0:T(8,128)S(1)}) custom-call(bf16[400,768]{1,0:T(8,128)(2,1)S(1)} %get-tuple-element.46.refs_0_, bf16[400,768]{1,0:T(8,128)(2,1)S(1)} %get-tuple-element.47.refs_1_, ...), custom_call_target="tpu_custom_call", output_to_operand_aliasing={{3}: (10, {})} | custom-call | flops 1358954496 | bytes 1048576 | tf_op jit(solution)/shard_map/pallas_call | solution.py:608
Async XLA Ops:
  2.4 17.8 %collective-permute-start = (bf16[400,768]{1,0:T(8,128)(2,1)S(1)}, bf16[400,768]{1,0:T(8,128)(2,1)S(1)}, u32[]{:S(2)}, u32[]{:S(2)}) collective-permute-start(bf16[400,768]{1,0:T(8,128)(2,1)S(1)} %get-tuple-element.47.refs_1_), channel_id=1, source_target_pairs={{0,4},{4,8},{8,12},{1,5},{5,9},{9,13},{2,6},{6,10},{10,14},{3,7},{... | collective-permute-start | bytes 1843208 | tf_op jit(solution)/shard_map/ppermute | solution.py:28
  6.4 16.3 %collective-permute-start.1 = (bf16[400,768]{1,0:T(8,128)(2,1)S(1)}, bf16[400,768]{1,0:T(8,128)(2,1)S(1)}, u32[]{:S(2)}, u32[]{:S(2)}) collective-permute-start(bf16[400,768]{1,0:T(8,128)(2,1)S(1)} %get-tuple-element.46.refs_0_), channel_id=1, source_target_pairs={{4,0},{8,4},{12,8},{5,1},{9,5},{13,9},{6,2},{10,6},{14,10},{7,3},{... | collective-permute-start | bytes 1843208 | tf_op jit(solution)/shard_map/ppermute | solution.py:28
  7.7 19.9 %collective-permute-start.2 = (bf16[528,768]{1,0:T(8,128)(2,1)S(1)}, bf16[528,768]{1,0:T(8,128)(2,1)S(1)}, u32[]{:S(2)}, u32[]{:S(2)}) collective-permute-start(bf16[528,768]{1,0:T(8,128)(2,1)S(1)} %get-tuple-element.54), channel_id=1, source_target_pairs={{0,1},{1,2},{2,3},{4,5},{5,6},{6,7},{8,9},{9,10},{10,11},{12,13},{... | collective-permute-start | bytes 2433032 | tf_op jit(solution)/shard_map/ppermute | solution.py:28
  11.7 17.9 %collective-permute-start.3 = (bf16[528,768]{1,0:T(8,128)(2,1)S(1)}, bf16[528,768]{1,0:T(8,128)(2,1)S(1)}, u32[]{:S(2)}, u32[]{:S(2)}) collective-permute-start(bf16[528,768]{1,0:T(8,128)(2,1)S(1)} %get-tuple-element.55), channel_id=1, source_target_pairs={{1,0},{2,1},{3,2},{5,4},{6,5},{7,6},{9,8},{10,9},{11,10},{13,12},{... | collective-permute-start | bytes 2433032 | tf_op jit(solution)/shard_map/ppermute | solution.py:28
  15.9 31.0 %collective-permute-start.8 = (bf16[384,768]{1,0:T(8,128)(2,1)S(1)}, bf16[384,768]{1,0:T(8,128)(2,1)S(1)}, u32[]{:S(2)}, u32[]{:S(2)}) collective-permute-start(bf16[384,768]{1,0:T(8,128)(2,1)S(1)} %get-tuple-element.73.refs_3_.refs_7_.refs_5_.refs_9_), channel_id=1, source_target_pairs={{0,4},{4,8},{8,12},{1,5},{5,9},{9,13},{2,6},{6,10},{10,14},{3,7},{... | collective-permute-start | bytes 1769480 | tf_op jit(solution)/shard_map/ppermute | solution.py:28
  20.2 26.7 %collective-permute-start.9 = (bf16[384,768]{1,0:T(8,128)(2,1)S(1)}, bf16[384,768]{1,0:T(8,128)(2,1)S(1)}, u32[]{:S(2)}, u32[]{:S(2)}) collective-permute-start(bf16[384,768]{1,0:T(8,128)(2,1)S(1)} %get-tuple-element.74.refs_2_.refs_6_.refs_4_.refs_8_), channel_id=1, source_target_pairs={{4,0},{8,4},{12,8},{5,1},{9,5},{13,9},{6,2},{10,6},{14,10},{7,3},{... | collective-permute-start | bytes 1769480 | tf_op jit(solution)/shard_map/ppermute | solution.py:28
  22.8 12.0 %collective-permute-start.4 = (bf16[272,768]{1,0:T(8,128)(2,1)S(1)}, bf16[272,768]{1,0:T(8,128)(2,1)S(1)}, u32[]{:S(2)}, u32[]{:S(2)}) collective-permute-start(bf16[272,768]{1,0:T(8,128)(2,1)S(1)} %get-tuple-element.56), channel_id=1, source_target_pairs={{0,1},{1,2},{2,3},{4,5},{5,6},{6,7},{8,9},{9,10},{10,11},{12,13},{... | collective-permute-start | bytes 1253384 | tf_op jit(solution)/shard_map/ppermute | solution.py:28
  27.7 9.7 %collective-permute-start.5 = (bf16[272,768]{1,0:T(8,128)(2,1)S(1)}, bf16[272,768]{1,0:T(8,128)(2,1)S(1)}, u32[]{:S(2)}, u32[]{:S(2)}) collective-permute-start(bf16[272,768]{1,0:T(8,128)(2,1)S(1)} %get-tuple-element.57), channel_id=1, source_target_pairs={{1,0},{2,1},{3,2},{5,4},{6,5},{7,6},{9,8},{10,9},{11,10},{13,12},{... | collective-permute-start | bytes 1253384 | tf_op jit(solution)/shard_map/ppermute | solution.py:28
  39.2 7.5 %collective-permute-start.6 = (f32[6,768]{1,0:T(8,128)S(1)}, f32[6,768]{1,0:T(8,128)S(1)}, u32[]{:S(2)}, u32[]{:S(2)}) collective-permute-start(f32[6,768]{1,0:T(8,128)S(1)} %get-tuple-element.65.refs_11_.refs_1_), channel_id=1, source_target_pairs={{0,4},{4,8},{8,12},{1,5},{5,9},{9,13},{2,6},{6,10},{10,14},{3,7},{... | collective-permute-start | bytes 55304 | tf_op jit(solution)/shard_map/ppermute | solution.py:28
  42.4 4.6 %collective-permute-start.7 = (f32[6,768]{1,0:T(8,128)S(1)}, f32[6,768]{1,0:T(8,128)S(1)}, u32[]{:S(2)}, u32[]{:S(2)}) collective-permute-start(f32[6,768]{1,0:T(8,128)S(1)} %get-tuple-element.64.refs_10_.refs_0_), channel_id=1, source_target_pairs={{4,0},{8,4},{12,8},{5,1},{9,5},{13,9},{6,2},{10,6},{14,10},{7,3},{... | collective-permute-start | bytes 55304 | tf_op jit(solution)/shard_map/ppermute | solution.py:28
  47.0 9.6 %collective-permute-start.10 = (bf16[288,768]{1,0:T(8,128)(2,1)S(1)}, bf16[288,768]{1,0:T(8,128)(2,1)S(1)}, u32[]{:S(2)}, u32[]{:S(2)}) collective-permute-start(bf16[288,768]{1,0:T(8,128)(2,1)S(1)} %get-tuple-element.75), channel_id=1, source_target_pairs={{0,1},{1,2},{2,3},{4,5},{5,6},{6,7},{8,9},{9,10},{10,11},{12,13},{... | collective-permute-start | bytes 1327112 | tf_op jit(solution)/shard_map/ppermute | solution.py:28
  49.9 9.6 %collective-permute-start.11 = (bf16[288,768]{1,0:T(8,128)(2,1)S(1)}, bf16[288,768]{1,0:T(8,128)(2,1)S(1)}, u32[]{:S(2)}, u32[]{:S(2)}) collective-permute-start(bf16[288,768]{1,0:T(8,128)(2,1)S(1)} %get-tuple-element.76), channel_id=1, source_target_pairs={{1,0},{2,1},{3,2},{5,4},{6,5},{7,6},{9,8},{10,9},{11,10},{13,12},{... | collective-permute-start | bytes 1327112 | tf_op jit(solution)/shard_map/ppermute | solution.py:28

commit v7 on v6

--- a/solution.py
+++ b/solution.py
@@ -78,15 +78,16 @@
     out[start : start + MARKS, :] = rows.astype(BF16)
 
 
-def pack(grids, tissue):
+def pack(grids, tissue, own_kv=None):
     rows, cols = tissue.shape
     width = grids[0].shape[-1]
+    keys = own_kv is None
 
     def body(mark_hbm, *refs):
-        sources, refs = refs[:4], refs[4:]
-        kv_refs, qg_refs, side_refs = refs[:rows], refs[rows : 2 * rows], refs[2 * rows : 2 * rows + 2]
-        grid_refs, (sems, mark_ref, mark_sem) = refs[2 * rows + 2 : 2 * rows + 6], refs[2 * rows + 6 :]
-
+        sources, refs = refs[:2], refs[2:]
+        kv_refs, refs = ((), refs) if keys else (refs[:rows], refs[rows:])
+        row_refs, side_refs = refs[:rows], refs[rows : rows + (0 if keys else 2)]
+        *grid_refs, sems, mark_ref, mark_sem = refs[-5:]
         copies = [
             [
                 pltpu.make_async_copy(
@@ -101,37 +102,39 @@
         marks = pltpu.make_async_copy(mark_hbm, mark_ref, mark_sem)
         marks.start()
         marks.wait()
+        for end, side in zip((0, cols - 1), side_refs):
+            for n in range(2):
+                for a in range(rows):
+                    side[rows_of(n * rows + a), :] = kv_refs[a][rows_of(n * cols + end), :]
+            write_marks(side, 4 * rows * TOKENS, [mark_ref[a, end].astype(F32) for a in range(rows)], width)
         for n, ref in enumerate(grid_refs):
             for a in range(rows):
                 copies[n][a].wait()
-                out = (kv_refs if n < 2 else qg_refs)[a]
                 for b in range(cols):
                     tile = tile_of(ref, a, b)
-                    if n >= 2:
-                        tile = tile * (SCALE if n == 2 else mark_ref[a, b].astype(F32))
+                    if not keys:
+                        tile = tile * (SCALE if n == 0 else mark_ref[a, b].astype(F32))
                     tile = tile.astype(BF16)
-                    out[rows_of(n % 2 * cols + b), :] = tile
+                    row_refs[a][rows_of(n * cols + b), :] = tile
                     for end, side in zip((0, cols - 1), side_refs):
                         if b == end:
-                            side[rows_of(n * rows + a), :] = tile
-        for a in range(rows):
-            write_marks(kv_refs[a], 2 * cols * TOKENS, [mark_ref[a, b].astype(F32) for b in range(cols)], width)
-        for b, side in zip((0, cols - 1), side_refs):
-            write_marks(side, 4 * rows * TOKENS, [mark_ref[a, b].astype(F32) for a in range(rows)], width)
-
-    shapes = [2 * cols * TOKENS + MARKS] * rows + [2 * cols * TOKENS] * rows + [4 * rows * TOKENS + MARKS] * 2
-    shapes = [jax.ShapeDtypeStruct((height, width), BF16) for height in shapes]
-    outs = pl.pallas_call(
+                            side[rows_of((n + 2) * rows + a), :] = tile
+        if keys:
+            for a in range(rows):
+                write_marks(row_refs[a], 2 * cols * TOKENS, [mark_ref[a, b].astype(F32) for b in range(cols)], width)
+
+    heights = [2 * cols * TOKENS + (MARKS if keys else 0)] * rows + [4 * rows * TOKENS + MARKS] * (0 if keys else 2)
+    shapes = [jax.ShapeDtypeStruct((height, width), BF16) for height in heights]
+    return pl.pallas_call(
         body,
-        in_specs=[pl.BlockSpec(memory_space=pltpu.HBM)] * 5,
+        in_specs=[pl.BlockSpec(memory_space=pltpu.HBM)] * 3 + [VMEM] * (0 if keys else rows),
         out_specs=[VMEM] * len(shapes),
         out_shape=shapes,
-        scratch_shapes=[pltpu.VMEM(grid.shape, grid.dtype) for grid in grids] + [pltpu.SemaphoreType.DMA((4, rows))]
+        scratch_shapes=[pltpu.VMEM(grid.shape, grid.dtype) for grid in grids] + [pltpu.SemaphoreType.DMA((2, rows))]
         + [pltpu.SMEM(tissue.shape, jnp.int32), pltpu.SemaphoreType.DMA],
         compiler_params=pltpu.CompilerParams(vmem_limit_bytes=LIMIT),
         cost_estimate=pl.CostEstimate(flops=0, transcendentals=0, bytes_accessed=1 << 20),
-    )(*(pltpu.with_memory_space_constraint(array, pltpu.HBM) for array in (tissue, *grids)))
-    return outs[:rows], outs[rows : 2 * rows], outs[2 * rows :]
+    )(*(pltpu.with_memory_space_constraint(array, pltpu.HBM) for array in (tissue, *grids)), *(own_kv or ()))
 
 
 def pack_corners(above, below, cols):
@@ -230,7 +233,7 @@
         return mark_row(ref, 4 * self.rows * TOKENS, i, self.lanes)
 
 
-WIDTH = 3
+WIDTH = 8
 
 
 def drive(programs):
@@ -577,7 +580,8 @@
 def local(query_grid, key_grid, value_grid, out_grad, tissue):
     rows, cols = tissue.shape
     width = query_grid.shape[-1]
-    own_kv, own_qg, (first_side, last_side) = pack((key_grid, value_grid, query_grid, out_grad), tissue)
+    own_kv = pack((key_grid, value_grid), tissue)
+    *own_qg, first_side, last_side = pack((query_grid, out_grad), tissue, own_kv)
     above_kv = shift(own_kv[-1], "rows", 1)
     below_kv = shift(own_kv[0], "rows", -1)
     grid_out = jax.ShapeDtypeStruct(query_grid.shape, BF16)

time: 64.2 us -> 64.1 us (level)
  waiting for transfers between devices: 6.85 us -> 5.51 us
  Pallas kernels: 22.8 us -> 23.9 us
    ppermute x12, waiting for transfers between devices: 6.85 us -> 5.51 us  [shift(): return lax.ppermute(array, axis, pairs)]
    pallas_call x1 -> x2, Pallas kernels: 1.72 us -> 2.62 us  [pack(): pl.pallas_call(body, in_specs=[pl.BlockSpec(memory_space=pltpu.HBM)] * 3...]
  transfers between devices with their start and end apart: 12 -> 12, of which waited for: 4 -> 3; matrix products, arithmetic and copies ran while one was open for 0% -> 0% of each run, Pallas kernels for 27% -> 29%
where the time goes in v7:
time: 64.1 us; the launch traced here: 63.6 us
  starting transfers between devices  33.2 us (52%)
  Pallas kernels  23.9 us (37%)
  waiting for transfers between devices  5.51 us (9%)
  between operations  1.01 us (2%)
    ppermute x12, starting transfers between devices, shift(): return lax.ppermute(array, axis, pairs)  33.2 us
    pallas_call x5, Pallas kernels, run(): pl.pallas_call(body, in_specs=[VMEM] * len(args), out_specs=[hbm] * len(h...  14 us
    pallas_call x5, Pallas kernels, call(): pl.pallas_call(body, in_specs=[VMEM] * len(args), out_specs=[VMEM] * len(...  7.28 us
    ppermute x12, waiting for transfers between devices, shift(): return lax.ppermute(array, axis, pairs)  5.51 us
    pallas_call x2, Pallas kernels, pack(): pl.pallas_call(body, in_specs=[pl.BlockSpec(memory_space=pltpu.HBM)] * 3...  2.62 us
  transfers between devices with their start and end apart: 12, of which 3 were waited for; matrix products, arithmetic and copies ran while one was open for 0% of the time, Pallas kernels for 29%

profile of v7, /device:TPU:1, one launch (start us, length us, event | category | flops | bytes accessed | tf_op | source)
XLA Modules:
  0.0 63.6 jit_solution(16986483431794761881)
XLA Ops:
  0.6 1.3 %shard_map.84 = (bf16[400,768]{1,0:T(8,128)(2,1)S(1)}, bf16[400,768]{1,0:T(8,128)(2,1)S(1)}) custom-call(s32[2,3]{1,0:T(2,128)} %mark_hbm.3, bf16[16,24,768]{2,1,0:T(8,128)(2,1)} %refs_0_.2, bf16[16,24,768]{2,1,0:T(8,128)(2,1)} %refs_1_.2), custom_call_target="tpu_custom_call" | custom-call | bytes 1048576 | tf_op jit(solution)/shard_map/pallas_call | solution.py:128
  1.9 4.1 %collective-permute-start = (bf16[400,768]{1,0:T(8,128)(2,1)S(1)}, bf16[400,768]{1,0:T(8,128)(2,1)S(1)}, u32[]{:S(2)}, u32[]{:S(2)}) collective-permute-start(bf16[400,768]{1,0:T(8,128)(2,1)S(1)} %get-tuple-element.47.refs_3_.refs_1_), channel_id=1, source_target_pairs={{0,4},{4,8},{8,12},{1,5},{5,9},{9,13},{2,6},{6,10},{10,14},{3,7},{... | collective-permute-start | bytes 1843208 | tf_op jit(solution)/shard_map/ppermute | solution.py:28
  6.0 1.3 %collective-permute-start.1 = (bf16[400,768]{1,0:T(8,128)(2,1)S(1)}, bf16[400,768]{1,0:T(8,128)(2,1)S(1)}, u32[]{:S(2)}, u32[]{:S(2)}) collective-permute-start(bf16[400,768]{1,0:T(8,128)(2,1)S(1)} %get-tuple-element.46.refs_2_.refs_0_), channel_id=1, source_target_pairs={{4,0},{8,4},{12,8},{5,1},{9,5},{13,9},{6,2},{10,6},{14,10},{7,3},{... | collective-permute-start | bytes 1843208 | tf_op jit(solution)/shard_map/ppermute | solution.py:28
  7.3 1.3 %shard_map.85 = (bf16[384,768]{1,0:T(8,128)(2,1)S(1)}, bf16[384,768]{1,0:T(8,128)(2,1)S(1)}, bf16[528,768]{1,0:T(8,128)(2,1)S(1)}, bf16[528,768]{1,0:T(8,128)(2,1)S(1)}) custom-call(s32[2,3]{1,0:T(2,128)} %mark_hbm.3, bf16[16,24,768]{2,1,0:T(8,128)(2,1)} %refs_0_.3, bf16[16,24,768]{2,1,0:T(8,128)(2,1)} %refs_1_.3, ...), custom_call_target="tpu_custom_call" | custom-call | bytes 1048576 | tf_op jit(solution)/shard_map/pallas_call | solution.py:128
  8.6 4.0 %collective-permute-start.2 = (bf16[528,768]{1,0:T(8,128)(2,1)S(1)}, bf16[528,768]{1,0:T(8,128)(2,1)S(1)}, u32[]{:S(2)}, u32[]{:S(2)}) collective-permute-start(bf16[528,768]{1,0:T(8,128)(2,1)S(1)} %get-tuple-element.54), channel_id=1, source_target_pairs={{0,1},{1,2},{2,3},{4,5},{5,6},{6,7},{8,9},{9,10},{10,11},{12,13},{... | collective-permute-start | bytes 2433032 | tf_op jit(solution)/shard_map/ppermute | solution.py:28
  12.6 1.9 %collective-permute-start.3 = (bf16[528,768]{1,0:T(8,128)(2,1)S(1)}, bf16[528,768]{1,0:T(8,128)(2,1)S(1)}, u32[]{:S(2)}, u32[]{:S(2)}) collective-permute-start(bf16[528,768]{1,0:T(8,128)(2,1)S(1)} %get-tuple-element.55), channel_id=1, source_target_pairs={{1,0},{2,1},{3,2},{5,4},{6,5},{7,6},{9,8},{10,9},{11,10},{13,12},{... | collective-permute-start | bytes 2433032 | tf_op jit(solution)/shard_map/ppermute | solution.py:28
  14.5 2.5 %shard_map.86 = (f32[384,768]{1,0:T(8,128)S(1)}, f32[12,768]{1,0:T(8,128)S(1)}) custom-call(bf16[400,768]{1,0:T(8,128)(2,1)S(1)} %get-tuple-element.46.refs_2_.refs_0_, bf16[400,768]{1,0:T(8,128)(2,1)S(1)} %get-tuple-element.47.refs_3_.refs_1_, bf16[384,768]{1,0:T(8,128)(2,1)S(1)} %get-tuple-element.74.refs_2_.refs_6_.refs_4_.refs_8_, ...), custom_call_target="tpu_custom_call" | custom-call | flops 10871635968 | bytes 2408448 | tf_op jit(solution)/shard_map/pallas_call | solution.py:45
  17.0 4.3 %collective-permute-start.8 = (bf16[384,768]{1,0:T(8,128)(2,1)S(1)}, bf16[384,768]{1,0:T(8,128)(2,1)S(1)}, u32[]{:S(2)}, u32[]{:S(2)}) collective-permute-start(bf16[384,768]{1,0:T(8,128)(2,1)S(1)} %get-tuple-element.73.refs_3_.refs_7_.refs_5_.refs_9_), channel_id=1, source_target_pairs={{0,4},{4,8},{8,12},{1,5},{5,9},{9,13},{2,6},{6,10},{10,14},{3,7},{... | collective-permute-start | bytes 1769480 | tf_op jit(solution)/shard_map/ppermute | solution.py:28
  21.3 0.0 collective-permute-done.above_ref.refs_2_
  21.3 1.3 %collective-permute-start.9 = (bf16[384,768]{1,0:T(8,128)(2,1)S(1)}, bf16[384,768]{1,0:T(8,128)(2,1)S(1)}, u32[]{:S(2)}, u32[]{:S(2)}) collective-permute-start(bf16[384,768]{1,0:T(8,128)(2,1)S(1)} %get-tuple-element.74.refs_2_.refs_6_.refs_4_.refs_8_), channel_id=1, source_target_pairs={{4,0},{8,4},{12,8},{5,1},{9,5},{13,9},{6,2},{10,6},{14,10},{7,3},{... | collective-permute-start | bytes 1769480 | tf_op jit(solution)/shard_map/ppermute | solution.py:28
  22.6 0.0 collective-permute-done.1.below_ref.refs_3_
  22.6 0.1 shard_map.87
  22.7 4.5 %collective-permute-start.4 = (bf16[272,768]{1,0:T(8,128)(2,1)S(1)}, bf16[272,768]{1,0:T(8,128)(2,1)S(1)}, u32[]{:S(2)}, u32[]{:S(2)}) collective-permute-start(bf16[272,768]{1,0:T(8,128)(2,1)S(1)} %get-tuple-element.56), channel_id=1, source_target_pairs={{0,1},{1,2},{2,3},{4,5},{5,6},{6,7},{8,9},{9,10},{10,11},{12,13},{... | collective-permute-start | bytes 1253384 | tf_op jit(solution)/shard_map/ppermute | solution.py:28
  27.2 0.0 collective-permute-done.2.refs_4_.refs_2_.refs_6_
  27.3 1.9 %collective-permute-start.5 = (bf16[272,768]{1,0:T(8,128)(2,1)S(1)}, bf16[272,768]{1,0:T(8,128)(2,1)S(1)}, u32[]{:S(2)}, u32[]{:S(2)}) collective-permute-start(bf16[272,768]{1,0:T(8,128)(2,1)S(1)} %get-tuple-element.57), channel_id=1, source_target_pairs={{1,0},{2,1},{3,2},{5,4},{6,5},{7,6},{9,8},{10,9},{11,10},{13,12},{... | collective-permute-start | bytes 1253384 | tf_op jit(solution)/shard_map/ppermute | solution.py:28
  29.2 0.0 collective-permute-done.3.refs_5_.refs_3_.refs_7_
  29.2 2.9 %shard_map.88 = (f32[384,768]{1,0:T(8,128)S(1)}, f32[12,768]{1,0:T(8,128)S(1)}, bf16[16,24,768]{2,1,0:T(8,128)(2,1)S(1)}) custom-call(bf16[400,768]{1,0:T(8,128)(2,1)S(1)} %get-tuple-element.46.refs_2_.refs_0_, bf16[400,768]{1,0:T(8,128)(2,1)S(1)} %get-tuple-element.47.refs_3_.refs_1_, bf16[400,768]{1,0:T(8,128)(2,1)S(1)} %collective-permute-done.above_ref.refs_2_, ...), custom_call_target="tpu_custom_call" | custom-call | flops 10871635968 | bytes 6475776 | tf_op jit(solution)/shard_map/pallas_call | solution.py:45
  32.1 2.4 %shard_map.89 = (bf16[16,24,768]{2,1,0:T(8,128)(2,1)S(1)}, f32[2,384,768]{2,1,0:T(8,128)S(1)}) custom-call(bf16[400,768]{1,0:T(8,128)(2,1)S(1)} %get-tuple-element.46.refs_2_.refs_0_, bf16[400,768]{1,0:T(8,128)(2,1)S(1)} %get-tuple-element.47.refs_3_.refs_1_, bf16[400,768]{1,0:T(8,128)(2,1)S(1)} %collective-permute-done.above_ref.refs_2_, ...), custom_call_target="tpu_custom_call" | custom-call | flops 1358954496 | bytes 1048576 | tf_op jit(solution)/shard_map/pallas_call | solution.py:612
  34.5 0.0 collective-permute-done.4.refs_2_.refs_6_.refs_4_
  34.5 2.4 %collective-permute-done.5.refs_3_.refs_7_.refs_5_ = bf16[272,768]{1,0:T(8,128)(2,1)S(1)} collective-permute-done((bf16[272,768]{1,0:T(8,128)(2,1)S(1)}, bf16[272,768]{1,0:T(8,128)(2,1)S(1)}, u32[]{:S(2)}, u32[]{:S(2)}) %collective-permute-start.5) | collective-permute-done | bytes 417824 | tf_op jit(solution)/shard_map/ppermute | solution.py:28
  36.9 1.7 %shard_map.90 = (bf16[16,24,768]{2,1,0:T(8,128)(2,1)S(1)}, f32[6,768]{1,0:T(8,128)S(1)}, f32[6,768]{1,0:T(8,128)S(1)}) custom-call(bf16[400,768]{1,0:T(8,128)(2,1)S(1)} %get-tuple-element.46.refs_2_.refs_0_, bf16[400,768]{1,0:T(8,128)(2,1)S(1)} %get-tuple-element.47.refs_3_.refs_1_, bf16[272,768]{1,0:T(8,128)(2,1)S(1)} %collective-permute-done.4.refs_2_.refs_6_.refs_4_, ...), custom_call_target="tpu_custom_call" | custom-call | flops 679477248 | bytes 4460544 | tf_op jit(solution)/shard_map/pallas_call | solution.py:45
  38.7 3.7 %collective-permute-start.6 = (f32[6,768]{1,0:T(8,128)S(1)}, f32[6,768]{1,0:T(8,128)S(1)}, u32[]{:S(2)}, u32[]{:S(2)}) collective-permute-start(f32[6,768]{1,0:T(8,128)S(1)} %get-tuple-element.65.refs_11_.refs_1_), channel_id=1, source_target_pairs={{0,4},{4,8},{8,12},{1,5},{5,9},{9,13},{2,6},{6,10},{10,14},{3,7},{... | collective-permute-start | bytes 55304 | tf_op jit(solution)/shard_map/ppermute | solution.py:28
  42.3 1.5 %collective-permute-start.7 = (f32[6,768]{1,0:T(8,128)S(1)}, f32[6,768]{1,0:T(8,128)S(1)}, u32[]{:S(2)}, u32[]{:S(2)}) collective-permute-start(f32[6,768]{1,0:T(8,128)S(1)} %get-tuple-element.64.refs_10_.refs_0_), channel_id=1, source_target_pairs={{4,0},{8,4},{12,8},{5,1},{9,5},{13,9},{6,2},{10,6},{14,10},{7,3},{... | collective-permute-start | bytes 55304 | tf_op jit(solution)/shard_map/ppermute | solution.py:28
  43.8 2.8 %shard_map.91 = (bf16[16,24,768]{2,1,0:T(8,128)(2,1)}, bf16[16,24,768]{2,1,0:T(8,128)(2,1)S(1)}, f32[2,384,768]{2,1,0:T(8,128)S(1)}) custom-call(bf16[400,768]{1,0:T(8,128)(2,1)S(1)} %get-tuple-element.46.refs_2_.refs_0_, bf16[400,768]{1,0:T(8,128)(2,1)S(1)} %get-tuple-element.47.refs_3_.refs_1_, ...), custom_call_target="tpu_custom_call", output_to_operand_aliasing={{2}: (12, {})} | custom-call | flops 2717908992 | bytes 1048576 | tf_op jit(solution)/shard_map/pallas_call | solution.py:612
  46.6 0.0 collective-permute-done.6.refs_2_.refs_6_
  46.7 0.2 collective-permute-done.7.refs_3_.refs_7_
  46.9 0.0 collective-permute-done.8.refs_4_
  46.9 0.0 collective-permute-done.9.refs_5_
  46.9 0.1 shard_map.92
  47.0 2.9 %collective-permute-start.10 = (bf16[288,768]{1,0:T(8,128)(2,1)S(1)}, bf16[288,768]{1,0:T(8,128)(2,1)S(1)}, u32[]{:S(2)}, u32[]{:S(2)}) collective-permute-start(bf16[288,768]{1,0:T(8,128)(2,1)S(1)} %get-tuple-element.75), channel_id=1, source_target_pairs={{0,1},{1,2},{2,3},{4,5},{5,6},{6,7},{8,9},{9,10},{10,11},{12,13},{... | collective-permute-start | bytes 1327112 | tf_op jit(solution)/shard_map/ppermute | solution.py:28
  49.9 1.9 %collective-permute-start.11 = (bf16[288,768]{1,0:T(8,128)(2,1)S(1)}, bf16[288,768]{1,0:T(8,128)(2,1)S(1)}, u32[]{:S(2)}, u32[]{:S(2)}) collective-permute-start(bf16[288,768]{1,0:T(8,128)(2,1)S(1)} %get-tuple-element.76), channel_id=1, source_target_pairs={{1,0},{2,1},{3,2},{5,4},{6,5},{7,6},{9,8},{10,9},{11,10},{13,12},{... | collective-permute-start | bytes 1327112 | tf_op jit(solution)/shard_map/ppermute | solution.py:28
  51.8 2.3 %shard_map.93 = (bf16[16,24,768]{2,1,0:T(8,128)(2,1)S(1)}, f32[2,384,768]{2,1,0:T(8,128)S(1)}) custom-call(bf16[400,768]{1,0:T(8,128)(2,1)S(1)} %get-tuple-element.46.refs_2_.refs_0_, bf16[400,768]{1,0:T(8,128)(2,1)S(1)} %get-tuple-element.47.refs_3_.refs_1_, ...), custom_call_target="tpu_custom_call", output_to_operand_aliasing={{1}: (12, {})} | custom-call | flops 2717908992 | bytes 1048576 | tf_op jit(solution)/shard_map/pallas_call | solution.py:612
  54.1 2.5 %shard_map.94 = (f32[2,384,768]{2,1,0:T(8,128)S(1)}, bf16[16,24,768]{2,1,0:T(8,128)(2,1)S(1)}, bf16[16,24,768]{2,1,0:T(8,128)(2,1)S(1)}) custom-call(bf16[400,768]{1,0:T(8,128)(2,1)S(1)} %get-tuple-element.46.refs_2_.refs_0_, bf16[400,768]{1,0:T(8,128)(2,1)S(1)} %get-tuple-element.47.refs_3_.refs_1_, ...), custom_call_target="tpu_custom_call", output_to_operand_aliasing={{0}: (8, {})} | custom-call | flops 1358954496 | bytes 1048576 | tf_op jit(solution)/shard_map/pallas_call | solution.py:612
  56.6 0.0 collective-permute-done.10.refs_8_
  56.6 2.9 %collective-permute-done.11.refs_9_ = bf16[288,768]{1,0:T(8,128)(2,1)S(1)} collective-permute-done((bf16[288,768]{1,0:T(8,128)(2,1)S(1)}, bf16[288,768]{1,0:T(8,128)(2,1)S(1)}, u32[]{:S(2)}, u32[]{:S(2)}) %collective-permute-start.11) | collective-permute-done | bytes 442400 | tf_op jit(solution)/shard_map/ppermute | solution.py:28
  59.5 4.0 %shard_map.95 = (bf16[16,24,768]{2,1,0:T(8,128)(2,1)}, bf16[16,24,768]{2,1,0:T(8,128)(2,1)}, bf16[16,24,768]{2,1,0:T(8,128)(2,1)}, f32[2,384,768]{2,1,0:T(8,128)S(1)}) custom-call(bf16[400,768]{1,0:T(8,128)(2,1)S(1)} %get-tuple-element.46.refs_2_.refs_0_, bf16[400,768]{1,0:T(8,128)(2,1)S(1)} %get-tuple-element.47.refs_3_.refs_1_, ...), custom_call_target="tpu_custom_call", output_to_operand_aliasing={{3}: (10, {})} | custom-call | flops 1358954496 | bytes 1048576 | tf_op jit(solution)/shard_map/pallas_call | solution.py:612
Async XLA Ops:
  1.9 19.4 %collective-permute-start = (bf16[400,768]{1,0:T(8,128)(2,1)S(1)}, bf16[400,768]{1,0:T(8,128)(2,1)S(1)}, u32[]{:S(2)}, u32[]{:S(2)}) collective-permute-start(bf16[400,768]{1,0:T(8,128)(2,1)S(1)} %get-tuple-element.47.refs_3_.refs_1_), channel_id=1, source_target_pairs={{0,4},{4,8},{8,12},{1,5},{5,9},{9,13},{2,6},{6,10},{10,14},{3,7},{... | collective-permute-start | bytes 1843208 | tf_op jit(solution)/shard_map/ppermute | solution.py:28
  6.0 16.6 %collective-permute-start.1 = (bf16[400,768]{1,0:T(8,128)(2,1)S(1)}, bf16[400,768]{1,0:T(8,128)(2,1)S(1)}, u32[]{:S(2)}, u32[]{:S(2)}) collective-permute-start(bf16[400,768]{1,0:T(8,128)(2,1)S(1)} %get-tuple-element.46.refs_2_.refs_0_), channel_id=1, source_target_pairs={{4,0},{8,4},{12,8},{5,1},{9,5},{13,9},{6,2},{10,6},{14,10},{7,3},{... | collective-permute-start | bytes 1843208 | tf_op jit(solution)/shard_map/ppermute | solution.py:28
  8.6 18.6 %collective-permute-start.2 = (bf16[528,768]{1,0:T(8,128)(2,1)S(1)}, bf16[528,768]{1,0:T(8,128)(2,1)S(1)}, u32[]{:S(2)}, u32[]{:S(2)}) collective-permute-start(bf16[528,768]{1,0:T(8,128)(2,1)S(1)} %get-tuple-element.54), channel_id=1, source_target_pairs={{0,1},{1,2},{2,3},{4,5},{5,6},{6,7},{8,9},{9,10},{10,11},{12,13},{... | collective-permute-start | bytes 2433032 | tf_op jit(solution)/shard_map/ppermute | solution.py:28
  12.6 16.6 %collective-permute-start.3 = (bf16[528,768]{1,0:T(8,128)(2,1)S(1)}, bf16[528,768]{1,0:T(8,128)(2,1)S(1)}, u32[]{:S(2)}, u32[]{:S(2)}) collective-permute-start(bf16[528,768]{1,0:T(8,128)(2,1)S(1)} %get-tuple-element.55), channel_id=1, source_target_pairs={{1,0},{2,1},{3,2},{5,4},{6,5},{7,6},{9,8},{10,9},{11,10},{13,12},{... | collective-permute-start | bytes 2433032 | tf_op jit(solution)/shard_map/ppermute | solution.py:28
  17.0 29.9 %collective-permute-start.8 = (bf16[384,768]{1,0:T(8,128)(2,1)S(1)}, bf16[384,768]{1,0:T(8,128)(2,1)S(1)}, u32[]{:S(2)}, u32[]{:S(2)}) collective-permute-start(bf16[384,768]{1,0:T(8,128)(2,1)S(1)} %get-tuple-element.73.refs_3_.refs_7_.refs_5_.refs_9_), channel_id=1, source_target_pairs={{0,4},{4,8},{8,12},{1,5},{5,9},{9,13},{2,6},{6,10},{10,14},{3,7},{... | collective-permute-start | bytes 1769480 | tf_op jit(solution)/shard_map/ppermute | solution.py:28
  21.3 25.6 %collective-permute-start.9 = (bf16[384,768]{1,0:T(8,128)(2,1)S(1)}, bf16[384,768]{1,0:T(8,128)(2,1)S(1)}, u32[]{:S(2)}, u32[]{:S(2)}) collective-permute-start(bf16[384,768]{1,0:T(8,128)(2,1)S(1)} %get-tuple-element.74.refs_2_.refs_6_.refs_4_.refs_8_), channel_id=1, source_target_pairs={{4,0},{8,4},{12,8},{5,1},{9,5},{13,9},{6,2},{10,6},{14,10},{7,3},{... | collective-permute-start | bytes 1769480 | tf_op jit(solution)/shard_map/ppermute | solution.py:28
  22.7 11.8 %collective-permute-start.4 = (bf16[272,768]{1,0:T(8,128)(2,1)S(1)}, bf16[272,768]{1,0:T(8,128)(2,1)S(1)}, u32[]{:S(2)}, u32[]{:S(2)}) collective-permute-start(bf16[272,768]{1,0:T(8,128)(2,1)S(1)} %get-tuple-element.56), channel_id=1, source_target_pairs={{0,1},{1,2},{2,3},{4,5},{5,6},{6,7},{8,9},{9,10},{10,11},{12,13},{... | collective-permute-start | bytes 1253384 | tf_op jit(solution)/shard_map/ppermute | solution.py:28
  27.3 9.7 %collective-permute-start.5 = (bf16[272,768]{1,0:T(8,128)(2,1)S(1)}, bf16[272,768]{1,0:T(8,128)(2,1)S(1)}, u32[]{:S(2)}, u32[]{:S(2)}) collective-permute-start(bf16[272,768]{1,0:T(8,128)(2,1)S(1)} %get-tuple-element.57), channel_id=1, source_target_pairs={{1,0},{2,1},{3,2},{5,4},{6,5},{7,6},{9,8},{10,9},{11,10},{13,12},{... | collective-permute-start | bytes 1253384 | tf_op jit(solution)/shard_map/ppermute | solution.py:28
  38.7 8.0 %collective-permute-start.6 = (f32[6,768]{1,0:T(8,128)S(1)}, f32[6,768]{1,0:T(8,128)S(1)}, u32[]{:S(2)}, u32[]{:S(2)}) collective-permute-start(f32[6,768]{1,0:T(8,128)S(1)} %get-tuple-element.65.refs_11_.refs_1_), channel_id=1, source_target_pairs={{0,4},{4,8},{8,12},{1,5},{5,9},{9,13},{2,6},{6,10},{10,14},{3,7},{... | collective-permute-start | bytes 55304 | tf_op jit(solution)/shard_map/ppermute | solution.py:28
  42.3 4.6 %collective-permute-start.7 = (f32[6,768]{1,0:T(8,128)S(1)}, f32[6,768]{1,0:T(8,128)S(1)}, u32[]{:S(2)}, u32[]{:S(2)}) collective-permute-start(f32[6,768]{1,0:T(8,128)S(1)} %get-tuple-element.64.refs_10_.refs_0_), channel_id=1, source_target_pairs={{4,0},{8,4},{12,8},{5,1},{9,5},{13,9},{6,2},{10,6},{14,10},{7,3},{... | collective-permute-start | bytes 55304 | tf_op jit(solution)/shard_map/ppermute | solution.py:28
  47.0 9.6 %collective-permute-start.10 = (bf16[288,768]{1,0:T(8,128)(2,1)S(1)}, bf16[288,768]{1,0:T(8,128)(2,1)S(1)}, u32[]{:S(2)}, u32[]{:S(2)}) collective-permute-start(bf16[288,768]{1,0:T(8,128)(2,1)S(1)} %get-tuple-element.75), channel_id=1, source_target_pairs={{0,1},{1,2},{2,3},{4,5},{5,6},{6,7},{8,9},{9,10},{10,11},{12,13},{... | collective-permute-start | bytes 1327112 | tf_op jit(solution)/shard_map/ppermute | solution.py:28
  49.9 9.6 %collective-permute-start.11 = (bf16[288,768]{1,0:T(8,128)(2,1)S(1)}, bf16[288,768]{1,0:T(8,128)(2,1)S(1)}, u32[]{:S(2)}, u32[]{:S(2)}) collective-permute-start(bf16[288,768]{1,0:T(8,128)(2,1)S(1)} %get-tuple-element.76), channel_id=1, source_target_pairs={{1,0},{2,1},{3,2},{5,4},{6,5},{7,6},{9,8},{10,9},{11,10},{13,12},{... | collective-permute-start | bytes 1327112 | tf_op jit(solution)/shard_map/ppermute | solution.py:28
